TPU v7x, 128 devices: a whole 4x4x4 slice. The times are simulated.
128 devices in a mesh: row: 16 (over x, z_hi, core), col: 8 (over z_lo, y).
Axes of the slice: x: 4, y: 4, z: 4 (z_hi: 2, z_lo: 2; z = z_hi * 2 + z_lo), core: 2. Of those that a mesh axis runs over, the one named last changes fastest.
Arguments:
- pair: bfloat16 [1024, 1024, 128], P('row', 'col'), may hold values from -6 to 6
- bias_weight: bfloat16 [128, 16], replicated
- single: bfloat16 [48, 1024, 768], P('col', 'row'), may hold values from -6 to 6
- w_qkv: bfloat16 [768, 2304], replicated, may hold values from -0.21875 to 0.21875
- w_out: bfloat16 [768, 768], replicated, may hold values from -0.21875 to 0.21875
- w_gate_up: bfloat16 [768, 3072], replicated, may hold values from -0.21875 to 0.21875
- w_down: bfloat16 [1536, 768], replicated, may hold values from -0.15625 to 0.15625
- cotangent: bfloat16 [48, 1024, 768], P('col', 'row'), may hold values from -300 to 300
Outputs:
- updated: bfloat16 [48, 1024, 768], P('col', 'row')
- pair_grad: float32 [1024, 1024, 128], P('row', 'col')
All inputs are finite; a program needn't handle non-finite values.
Results may differ from a plain program's by a relative error of at most 0.012.
The roundings to bfloat16 on the way count: a program that leaves them out, or rounds other values in their place, can miss the bound.
Values may be sent and summed in bfloat16 or wider, within the bound.
No kernel may reach another device: no remote copies, remote signals or barrier semaphores. Data moves between devices by JAX's collectives and lax.ppermute only.
A program may use at most 192 MiB of HBM per device.

v0:
```python
import math

import jax
import jax.numpy as jnp
from jax import lax
from jax.sharding import PartitionSpec as P


def normalize(values):
    mean_val = jnp.mean(values, axis=-1, keepdims=True)
    centred = values - mean_val
    variance = jnp.mean(centred * centred, axis=-1, keepdims=True)
    scaled = lax.rsqrt(variance + 1e-05)
    return (centred * scaled, scaled)


def project_pair(piece, bias_weight):
    normed_pair, scaled = normalize(piece.astype(jnp.float32))
    row_count, col_count, chans = normed_pair.shape
    flat = jnp.dot(
        normed_pair.reshape(row_count * col_count, chans),
        bias_weight.astype(jnp.float32),
        precision=lax.Precision.HIGHEST,
    )
    return jnp.transpose(flat.reshape(row_count, col_count, -1), (2, 0, 1)).astype(jnp.bfloat16)


def attend_sample(queries, key_rows, value_rows, cotan, bias, head_count):
    row_count, width = queries.shape
    head_size = width // head_count
    query_h = queries.reshape(row_count, head_count, head_size)
    key_h = key_rows.reshape(-1, head_count, head_size)
    value_h = value_rows.reshape(-1, head_count, head_size)
    cotan_h = cotan.reshape(row_count, head_count, head_size)
    scores = jnp.einsum(
        "ihe,jhe->hij", query_h, key_h, preferred_element_type=jnp.float32
    ) / math.sqrt(head_size) + bias.astype(jnp.float32)
    weights = jax.nn.softmax(scores, axis=-1)
    rounded = weights.astype(jnp.bfloat16)
    attended = jnp.einsum("hij,jhe->ihe", rounded, value_h, preferred_element_type=jnp.float32)
    dprob = jnp.einsum("ihe,jhe->hij", cotan_h, value_h, preferred_element_type=jnp.float32)
    row_delta = jnp.sum(cotan_h.astype(jnp.float32) * attended, axis=2)
    grad_term = weights * (dprob - jnp.transpose(row_delta)[:, :, None])
    return (attended.reshape(row_count, width), grad_term)


def transition(single, attended, w_out, w_gate_up, w_down):
    width = single.shape[-1]
    flat_in = single.reshape(-1, width).astype(jnp.float32)
    mid = flat_in + jnp.dot(
        attended.reshape(-1, width).astype(jnp.bfloat16), w_out, preferred_element_type=jnp.float32
    )
    normed_mid = normalize(mid)[0].astype(jnp.bfloat16)
    gate_up = jnp.dot(normed_mid, w_gate_up, preferred_element_type=jnp.float32)
    half = gate_up.shape[1] // 2
    hidden = (jax.nn.silu(gate_up[:, :half]) * gate_up[:, half:]).astype(jnp.bfloat16)
    result = mid + jnp.dot(hidden, w_down, preferred_element_type=jnp.float32)
    return result.astype(jnp.bfloat16).reshape(single.shape)


def back_norm(normed_grad, normed_pair, scaled):
    centred = normed_grad - jnp.mean(normed_grad, axis=-1, keepdims=True)
    along = jnp.mean(normed_grad * normed_pair, axis=-1, keepdims=True)
    return (centred - normed_pair * along) * scaled


def shards(pair, bias_weight, single, w_qkv, w_out, w_gate_up, w_down, cotangent):
    width = single.shape[2]
    head_count = bias_weight.shape[1]
    samp_count, row_count = (single.shape[0], single.shape[1])
    bias = lax.all_gather(project_pair(pair, bias_weight), "col", axis=2, tiled=True)
    normed = normalize(single.astype(jnp.float32))[0].astype(jnp.bfloat16)
    flat_normed = normed.reshape(samp_count * row_count, width)
    queries = jnp.dot(flat_normed, w_qkv[:, :width], preferred_element_type=jnp.float32).astype(
        jnp.bfloat16
    )
    queries = queries.reshape(samp_count, row_count, width)
    w_kv = w_qkv[:, width:]
    kv_local = jnp.dot(flat_normed, w_kv, preferred_element_type=jnp.float32).astype(jnp.bfloat16)
    kv_local = kv_local.reshape(samp_count, row_count, 2 * width)
    kv_all = lax.all_gather(kv_local, "row", axis=1, tiled=True)

    def one_sample(carry, inputs):
        query_s, kv_s, cotan_s = inputs
        attended, grad_term = attend_sample(
            query_s, kv_s[:, :width], kv_s[:, width:], cotan_s, bias, head_count
        )
        return (carry + grad_term, attended)

    start_grad = jnp.zeros((head_count, row_count, kv_all.shape[1]), jnp.float32)
    grad_local, attended = lax.scan(one_sample, start_grad, (queries, kv_all, cotangent))
    updated = transition(single, attended, w_out, w_gate_up, w_down)
    bias_grad = lax.psum_scatter(grad_local, "col", scatter_dimension=2, tiled=True)
    normed_pair, scaled = normalize(pair.astype(jnp.float32))
    col_count, chans = (pair.shape[1], pair.shape[2])
    flat_grad = jnp.transpose(bias_grad, (1, 2, 0)).reshape(row_count * col_count, head_count)
    normed_grad = jnp.dot(
        flat_grad, jnp.transpose(bias_weight.astype(jnp.float32)), precision=lax.Precision.HIGHEST
    )
    normed_grad = normed_grad.reshape(row_count, col_count, chans)
    pair_grad = back_norm(normed_grad, normed_pair, scaled)
    return (updated, pair_grad)


def solution(mesh):
    return jax.shard_map(
        shards,
        mesh=mesh,
        in_specs=(
            P("row", "col", None),
            P(),
            P("col", "row", None),
            P(),
            P(),
            P(),
            P(),
            P("col", "row", None),
        ),
        out_specs=(P("col", "row", None), P("row", "col", None)),
        check_vma=False,
    )
```

profile of v0, /device:TPU:1, one launch (start us, length us, event | category | flops | bytes accessed | tf_op | source)
XLA Modules:
  0.0 442.7 jit_solution(11677037070908961696)
XLA Ops:
  7.2 4.2 copy.27
  17.9 4.0 convolution_convert_fusion
  24.9 36.6 %all-gather.5.cloned.1.call-done = bf16[16,64,1024]{2,0,1:T(8,128)(2,1)} async-done(((bf16[16,64,128]{2,0,1:T(8,128)(2,1)}), bf16[16,64,1024]{2,0,1:T(8,128)(2,1)}) %all-gather.5.cloned.1.call-update) | async-done | bytes 2097168 | tf_op jit(solution)/shard_map/all_gather | solution.py:71
  61.5 4.0 copy.31
  65.5 124.4 %all-gather.3.cloned.1.call-done = bf16[6,1024,1536]{2,1,0:T(8,128)(2,1)} async-done(((bf16[6,64,1536]{2,1,0:T(8,128)(2,1)}), bf16[6,1024,1536]{2,1,0:T(8,128)(2,1)}) %all-gather.3.cloned.1.call-update) | async-done | bytes 18874384 | tf_op jit(solution)/shard_map/all_gather | solution.py:81
  190.0 182.2 %while.13 = (s32[]{:T(128)}, f32[16,64,1024]{2,1,0:T(8,128)}, bf16[6,64,768]{2,1,0:T(8,128)(2,1)}, bf16[6,64,768]{2,1,0:T(8,128)(2,1)}, bf16[6,1024,1536]{2,1,0:...) while((s32[]{:T(128)}, f32[16,64,1024]{2,1,0:T(8,128)}, ...), condition=%wide.region_8.9_spmd.clone, body=%wide.region_4.8_spmd.clone.sunk | while | flops 314769408 | bytes 48255596 | solution.py:91
  194.9 4.7 %copy.59 = bf16[1,1024,1536]{1,2,0:T(8,128)(2,1)} copy(bf16[1,1024,1536]{2,1,0:T(8,128)(2,1)} %constant_dynamic-slice_fusion.6) | data formatting | bytes 6291456 | tf_op jit(solution)/shard_map/while/body/jit(dynamic_index_in_dim)/dynamic_slice | solution.py:91
  199.5 3.9 fusion.68
  203.4 5.7 %fusion.69 = (f32[16,64]{1,0:T(8,128)S(1)}, f32[16,64,1024]{2,1,0:T(8,128)}) fusion(bf16[16,64,1024]{2,1,0:T(8,128)(2,1)} %get-tuple-element.206, bf16[64,16,48]{0,2,1:T(8,128)(2,1)S(1)} %bitcast.70, bf16[1024,16,48]{0,2,1:T(8,128)(2,1)} %bitcast.67), kind=kOutput, calls=%fused_computation.64.clone.1 | convolution fusion | flops 105907200 | bytes 7966720 | tf_op jit(solution)/shard_map/while/body/eval_jaxpr/sub | solution.py:38
  212.8 5.8 %select_add_fusion.2 = f32[16,64,1024]{2,1,0:T(8,128)} fusion(f32[16,64,1024]{2,1,0:T(8,128)} %get-tuple-element.193, bf16[64,16,48]{0,2,1:T(8,128)(2,1)S(1)} %bitcast.73, bf16[1024,16,48]{0,2,1:T(8,128)(2,1)} %bitcast.69, f32[16,64]{1,0:T(8,128)S(1)} %bitcast.82, pred[]{:T(512)S(6)} %compare.3, f32[16,64,1024]{2,1,0:T(8,128)} %get-tuple-element.179, ...), kind=kOutput, calls=%fused_computation.1.clone.1 | convolution fusion | flops 105906176 | bytes 14262273 | tf_op jit(solution)/shard_map/while/body/eval_jaxpr/ihe,jhe->hij/dot_general | solution.py:41
  224.2 4.7 %copy.59 = bf16[1,1024,1536]{1,2,0:T(8,128)(2,1)} copy(bf16[1,1024,1536]{2,1,0:T(8,128)(2,1)} %constant_dynamic-slice_fusion.6) | data formatting | bytes 6291456 | tf_op jit(solution)/shard_map/while/body/jit(dynamic_index_in_dim)/dynamic_slice | solution.py:91
  228.9 3.9 fusion.68
  232.8 5.7 %fusion.69 = (f32[16,64]{1,0:T(8,128)S(1)}, f32[16,64,1024]{2,1,0:T(8,128)}) fusion(bf16[16,64,1024]{2,1,0:T(8,128)(2,1)} %get-tuple-element.206, bf16[64,16,48]{0,2,1:T(8,128)(2,1)S(1)} %bitcast.70, bf16[1024,16,48]{0,2,1:T(8,128)(2,1)} %bitcast.67), kind=kOutput, calls=%fused_computation.64.clone.1 | convolution fusion | flops 105907200 | bytes 7966720 | tf_op jit(solution)/shard_map/while/body/eval_jaxpr/sub | solution.py:38
  242.1 7.0 %select_add_fusion.2 = f32[16,64,1024]{2,1,0:T(8,128)} fusion(f32[16,64,1024]{2,1,0:T(8,128)} %get-tuple-element.193, bf16[64,16,48]{0,2,1:T(8,128)(2,1)S(1)} %bitcast.73, bf16[1024,16,48]{0,2,1:T(8,128)(2,1)} %bitcast.69, f32[16,64]{1,0:T(8,128)S(1)} %bitcast.82, pred[]{:T(512)S(6)} %compare.3, f32[16,64,1024]{2,1,0:T(8,128)} %get-tuple-element.179, ...), kind=kOutput, calls=%fused_computation.1.clone.1 | convolution fusion | flops 105906176 | bytes 14262273 | tf_op jit(solution)/shard_map/while/body/eval_jaxpr/ihe,jhe->hij/dot_general | solution.py:41
  254.8 4.7 %copy.59 = bf16[1,1024,1536]{1,2,0:T(8,128)(2,1)} copy(bf16[1,1024,1536]{2,1,0:T(8,128)(2,1)} %constant_dynamic-slice_fusion.6) | data formatting | bytes 6291456 | tf_op jit(solution)/shard_map/while/body/jit(dynamic_index_in_dim)/dynamic_slice | solution.py:91
  259.4 3.9 fusion.68
  263.4 5.7 %fusion.69 = (f32[16,64]{1,0:T(8,128)S(1)}, f32[16,64,1024]{2,1,0:T(8,128)}) fusion(bf16[16,64,1024]{2,1,0:T(8,128)(2,1)} %get-tuple-element.206, bf16[64,16,48]{0,2,1:T(8,128)(2,1)S(1)} %bitcast.70, bf16[1024,16,48]{0,2,1:T(8,128)(2,1)} %bitcast.67), kind=kOutput, calls=%fused_computation.64.clone.1 | convolution fusion | flops 105907200 | bytes 7966720 | tf_op jit(solution)/shard_map/while/body/eval_jaxpr/sub | solution.py:38
  272.7 7.0 %select_add_fusion.2 = f32[16,64,1024]{2,1,0:T(8,128)} fusion(f32[16,64,1024]{2,1,0:T(8,128)} %get-tuple-element.193, bf16[64,16,48]{0,2,1:T(8,128)(2,1)S(1)} %bitcast.73, bf16[1024,16,48]{0,2,1:T(8,128)(2,1)} %bitcast.69, f32[16,64]{1,0:T(8,128)S(1)} %bitcast.82, pred[]{:T(512)S(6)} %compare.3, f32[16,64,1024]{2,1,0:T(8,128)} %get-tuple-element.179, ...), kind=kOutput, calls=%fused_computation.1.clone.1 | convolution fusion | flops 105906176 | bytes 14262273 | tf_op jit(solution)/shard_map/while/body/eval_jaxpr/ihe,jhe->hij/dot_general | solution.py:41
  285.3 4.7 %copy.59 = bf16[1,1024,1536]{1,2,0:T(8,128)(2,1)} copy(bf16[1,1024,1536]{2,1,0:T(8,128)(2,1)} %constant_dynamic-slice_fusion.6) | data formatting | bytes 6291456 | tf_op jit(solution)/shard_map/while/body/jit(dynamic_index_in_dim)/dynamic_slice | solution.py:91
  290.0 3.9 fusion.68
  293.9 5.7 %fusion.69 = (f32[16,64]{1,0:T(8,128)S(1)}, f32[16,64,1024]{2,1,0:T(8,128)}) fusion(bf16[16,64,1024]{2,1,0:T(8,128)(2,1)} %get-tuple-element.206, bf16[64,16,48]{0,2,1:T(8,128)(2,1)S(1)} %bitcast.70, bf16[1024,16,48]{0,2,1:T(8,128)(2,1)} %bitcast.67), kind=kOutput, calls=%fused_computation.64.clone.1 | convolution fusion | flops 105907200 | bytes 7966720 | tf_op jit(solution)/shard_map/while/body/eval_jaxpr/sub | solution.py:38
  303.3 7.0 %select_add_fusion.2 = f32[16,64,1024]{2,1,0:T(8,128)} fusion(f32[16,64,1024]{2,1,0:T(8,128)} %get-tuple-element.193, bf16[64,16,48]{0,2,1:T(8,128)(2,1)S(1)} %bitcast.73, bf16[1024,16,48]{0,2,1:T(8,128)(2,1)} %bitcast.69, f32[16,64]{1,0:T(8,128)S(1)} %bitcast.82, pred[]{:T(512)S(6)} %compare.3, f32[16,64,1024]{2,1,0:T(8,128)} %get-tuple-element.179, ...), kind=kOutput, calls=%fused_computation.1.clone.1 | convolution fusion | flops 105906176 | bytes 14262273 | tf_op jit(solution)/shard_map/while/body/eval_jaxpr/ihe,jhe->hij/dot_general | solution.py:41
  315.9 4.7 %copy.59 = bf16[1,1024,1536]{1,2,0:T(8,128)(2,1)} copy(bf16[1,1024,1536]{2,1,0:T(8,128)(2,1)} %constant_dynamic-slice_fusion.6) | data formatting | bytes 6291456 | tf_op jit(solution)/shard_map/while/body/jit(dynamic_index_in_dim)/dynamic_slice | solution.py:91
  324.5 5.7 %fusion.69 = (f32[16,64]{1,0:T(8,128)S(1)}, f32[16,64,1024]{2,1,0:T(8,128)}) fusion(bf16[16,64,1024]{2,1,0:T(8,128)(2,1)} %get-tuple-element.206, bf16[64,16,48]{0,2,1:T(8,128)(2,1)S(1)} %bitcast.70, bf16[1024,16,48]{0,2,1:T(8,128)(2,1)} %bitcast.67), kind=kOutput, calls=%fused_computation.64.clone.1 | convolution fusion | flops 105907200 | bytes 7966720 | tf_op jit(solution)/shard_map/while/body/eval_jaxpr/sub | solution.py:38
  333.8 7.0 %select_add_fusion.2 = f32[16,64,1024]{2,1,0:T(8,128)} fusion(f32[16,64,1024]{2,1,0:T(8,128)} %get-tuple-element.193, bf16[64,16,48]{0,2,1:T(8,128)(2,1)S(1)} %bitcast.73, bf16[1024,16,48]{0,2,1:T(8,128)(2,1)} %bitcast.69, f32[16,64]{1,0:T(8,128)S(1)} %bitcast.82, pred[]{:T(512)S(6)} %compare.3, f32[16,64,1024]{2,1,0:T(8,128)} %get-tuple-element.179, ...), kind=kOutput, calls=%fused_computation.1.clone.1 | convolution fusion | flops 105906176 | bytes 14262273 | tf_op jit(solution)/shard_map/while/body/eval_jaxpr/ihe,jhe->hij/dot_general | solution.py:41
  346.5 4.7 %copy.59 = bf16[1,1024,1536]{1,2,0:T(8,128)(2,1)} copy(bf16[1,1024,1536]{2,1,0:T(8,128)(2,1)} %constant_dynamic-slice_fusion.6) | data formatting | bytes 6291456 | tf_op jit(solution)/shard_map/while/body/jit(dynamic_index_in_dim)/dynamic_slice | solution.py:91
  355.1 5.7 %fusion.69 = (f32[16,64]{1,0:T(8,128)S(1)}, f32[16,64,1024]{2,1,0:T(8,128)}) fusion(bf16[16,64,1024]{2,1,0:T(8,128)(2,1)} %get-tuple-element.206, bf16[64,16,48]{0,2,1:T(8,128)(2,1)S(1)} %bitcast.70, bf16[1024,16,48]{0,2,1:T(8,128)(2,1)} %bitcast.67), kind=kOutput, calls=%fused_computation.64.clone.1 | convolution fusion | flops 105907200 | bytes 7966720 | tf_op jit(solution)/shard_map/while/body/eval_jaxpr/sub | solution.py:38
  364.4 7.0 %select_add_fusion.2 = f32[16,64,1024]{2,1,0:T(8,128)} fusion(f32[16,64,1024]{2,1,0:T(8,128)} %get-tuple-element.193, bf16[64,16,48]{0,2,1:T(8,128)(2,1)S(1)} %bitcast.73, bf16[1024,16,48]{0,2,1:T(8,128)(2,1)} %bitcast.69, f32[16,64]{1,0:T(8,128)S(1)} %bitcast.82, pred[]{:T(512)S(6)} %compare.3, f32[16,64,1024]{2,1,0:T(8,128)} %get-tuple-element.179, ...), kind=kOutput, calls=%fused_computation.1.clone.1 | convolution fusion | flops 105906176 | bytes 14262273 | tf_op jit(solution)/shard_map/while/body/eval_jaxpr/ihe,jhe->hij/dot_general | solution.py:41
  374.7 4.4 fusion.32
  381.3 41.4 %reduce-scatter.2.cloned.1.call-done = f32[16,64,128]{2,1,0:T(8,128)} async-done(((f32[16,64,1024]{2,1,0:T(8,128)}), f32[16,64,128]{2,1,0:T(8,128)}) %reduce-scatter.2.cloned.1.call-update) | async-done | bytes 524304 | tf_op jit(solution)/shard_map/reduce_scatter | solution.py:93
  422.7 4.6 %fusion.40 = (f32[64,128]{1,0:T(8,128)S(1)}, f32[64,128]{1,0:T(8,128)S(1)}, f32[64,128,128]{1,2,0:T(8,128)S(1)}) fusion(f32[64,128]{1,0:T(8,128)S(1)} %add_rsqrt_fusion, f32[64,128]{1,0:T(8,128)S(1)} %broadcast_multiply_fusion.2, bf16[64,128,128]{1,2,0:T(8,128)(2,1)} %copy.27, bf16[128,16]{0,1:T(8,128)(2,1)S(1)} %copy-done.5, f32[64,128,16]{1,0,2:T(8,128)} %bitcast.79), kind=kOutput, calls=%fused_computation.62 | convolution fusion | flops 207601664 | bytes 6950912 | tf_op jit(solution)/shard_map/dot_general | solution.py:97
  430.5 5.6 %copy.35 = f32[64,128,128]{2,1,0:T(8,128)} copy(f32[64,128,128]{1,2,0:T(8,128)} %fusion.17) | data formatting | bytes 8388608
  (82 shorter events, 80.8 us)
Async XLA Ops:
  7.2 371.9 %copy-start = (bf16[1536,768]{1,0:T(8,128)(2,1)S(1)}, bf16[1536,768]{1,0:T(8,128)(2,1)}, u32[]{:S(2)}) copy-start(bf16[1536,768]{1,0:T(8,128)(2,1)} %param.16) | copy-start | bytes 7077892
  7.2 54.3 %all-gather.5.cloned.1.call-start = ((), (), s32[]{:S(2)}) async-start(), calls=%async_computation.2 | async-start | bytes 2359296 | tf_op jit(solution)/shard_map/all_gather | solution.py:71
  11.4 2.3 copy-start.1
  11.4 3.1 copy-start.5
  13.7 3.5 copy-start.3
  17.2 172.8 %all-gather.3.cloned.1.call-start = ((), (), s32[]{:S(2)}) async-start(), calls=%async_computation.1 | async-start | bytes 20054016 | tf_op jit(solution)/shard_map/all_gather | solution.py:81
  17.9 4.0 copy-start.4
  21.9 400.8 %reduce-scatter.2.cloned.1.call-start = ((), (), s32[]{:S(2)}) async-start(), calls=%async_computation.3 | async-start | bytes 4718592 | tf_op jit(solution)/shard_map/reduce_scatter | solution.py:93
  422.7 4.6 %copy-start.2 = (bf16[64,128,128]{1,2,0:T(8,128)(2,1)S(1)}, bf16[64,128,128]{1,2,0:T(8,128)(2,1)}, u32[]{:S(2)}) copy-start(bf16[64,128,128]{1,2,0:T(8,128)(2,1)} %copy.27) | copy-start | bytes 6291460
Sparse Core Ops, SparseCore 0:
  17.3 44.1 all-gather.4
  64.0 125.9 all-gather.2
  372.3 50.3 reduce-scatter.1
where the time goes:
time: 444 us; the launch traced here: 443 us
  waiting for transfers between devices  202 us (45%)
  matrix products  118 us (27%)
  local copies, waits for them, and re-layouts  100 us (23%)
  between operations  13.9 us (3%)
  other arithmetic  7.22 us (2%)
    all_gather x1, waiting for transfers between devices, shards(): kv_all = lax.all_gather(kv_local, 'row', axis=1, tiled=True)  124 us
    dynamic_slice x30, local copies, waits for them, and re-layouts, shards(): lax.scan(one_sample, start_grad, (queries, kv_all, cotangent))  58.3 us
    reduce_scatter x1, waiting for transfers between devices, shards(): lax.psum_scatter(grad_local, 'col', scatter_dimension=2, tiled=True)  41.4 us
    dot_general x6, matrix products, attend_sample(): jnp.einsum('ihe,jhe->hij', cotan_h, value_h, preferred_element_type=jnp.f...  40.7 us
    all_gather x1, waiting for transfers between devices, shards(): lax.all_gather(project_pair(pair, bias_weight), 'col', axis=2, tiled=True)  36.6 us
    sub x6, matrix products, attend_sample(): weights = jax.nn.softmax(scores, axis=-1)  34.1 us
    slice x6, local copies, waits for them, and re-layouts, one_sample(): kv_s[:, :width]  23.5 us
    dot_general x6, matrix products, attend_sample(): jnp.einsum('hij,jhe->ihe', rounded, value_h, preferred_element_type=jnp.f...  20.8 us
  transfers between devices with their start and end apart: 3, of which 3 were waited for; matrix products, arithmetic and copies ran while one was open for 5% of the time, Pallas kernels for 0%

commit v1 on v0

v1 whole, which is shorter than its diff:
```python
import functools
import math

import jax
import jax.numpy as jnp
from jax import lax
from jax.experimental import pallas as pl
from jax.experimental.pallas import tpu as pltpu
from jax.sharding import PartitionSpec as P

BF = jnp.bfloat16
F32 = jnp.float32
LOG2E = 1.4426950408889634


def normalize(values):
    mean_val = jnp.mean(values, axis=-1, keepdims=True)
    centred = values - mean_val
    variance = jnp.mean(centred * centred, axis=-1, keepdims=True)
    scaled = lax.rsqrt(variance + 1e-05)
    return (centred * scaled, scaled)


def project_pair(piece, bias_weight):
    normed_pair, scaled = normalize(piece.astype(F32))
    row_count, col_count, chans = normed_pair.shape
    flat = jnp.dot(
        normed_pair.reshape(row_count * col_count, chans),
        bias_weight.astype(F32),
        precision=lax.Precision.HIGHEST,
    )
    return jnp.transpose(flat.reshape(row_count, col_count, -1), (2, 0, 1)).astype(BF)


def attend_kernel(n_col, n_chip, n_samp, size, c_ref, blk_ref, *refs):
    bias_refs = refs[:n_col]
    att_ref = refs[n_col]
    out_refs = refs[n_col + 1 : 2 * n_col + 1]
    bias2, acc, kt, vt = refs[2 * n_col + 1 :]
    samp = pl.program_id(0)
    me = c_ref[0]
    block = blk_ref.shape[2]
    wide = block * n_col

    @pl.when(samp == 0)
    def _():
        for k in range(n_col):
            bias2[:, k * block : (k + 1) * block] = bias_refs[k][...].astype(F32) * LOG2E
        acc[...] = jnp.zeros_like(acc)
        kt[2 * size :, :] = jnp.zeros((kt.shape[0] - 2 * size, wide), BF)
        row = lax.broadcasted_iota(jnp.int32, (vt.shape[0] - size, wide), 0)
        vt[size:, :] = jnp.where(row < 3, 1.0, 0.0).astype(BF)

    for k in range(n_col):
        owner = jnp.bitwise_xor(me, k)
        cols = slice(k * block, (k + 1) * block)
        keys = blk_ref[owner, size : 2 * size, :]
        kt[:size, cols] = keys
        kt[size : 2 * size, cols] = keys
        vt[:size, cols] = blk_ref[owner, 2 * size : 3 * size, :]

    scale = LOG2E / math.sqrt(size)

    def one_block(b, carry):
        rows = pl.ds(pl.multiple_of(b * block, block), block)
        query = blk_ref[b, :size, :].astype(F32) * scale
        high = query.astype(BF).astype(F32)
        rest = jnp.zeros((block - 2 * size, block), F32)
        lhs = jnp.concatenate([high, query - high, rest], axis=0).T.astype(BF)
        scores = jnp.dot(lhs, kt[...], preferred_element_type=F32) + bias2[rows, :]
        top = jnp.max(scores, axis=1, keepdims=True)
        probs = jnp.exp2(scores - top)
        total = jnp.sum(probs, axis=1, keepdims=True)
        probs = probs * (1.0 / total)
        attended = lax.dot_general(
            probs.astype(BF), vt[...], (((1,), (1,)), ((), ())), preferred_element_type=F32
        )
        attended_t = attended.T[:size]
        att_ref[b, :, :] = attended_t.astype(BF)
        cotan = blk_ref[b, 3 * size :, :].astype(F32)
        delta = -jnp.sum(cotan * attended_t, axis=0, keepdims=True)
        d0 = delta.astype(BF).astype(F32)
        d1 = (delta - d0).astype(BF).astype(F32)
        d2 = delta - d0 - d1
        row = lax.broadcasted_iota(jnp.int32, (block - size, block), 0)
        tail = jnp.where(row == 0, d0, jnp.where(row == 1, d1, jnp.where(row == 2, d2, 0.0)))
        lhs2 = jnp.concatenate([cotan, tail], axis=0).T.astype(BF)
        dprob = jnp.dot(lhs2, vt[...], preferred_element_type=F32)
        acc[rows, :] += probs * dprob
        return carry

    lax.fori_loop(0, n_chip, one_block, 0)

    @pl.when(samp == n_samp - 1)
    def _():
        for k in range(n_col):
            out_refs[k][...] = acc[:, k * block : (k + 1) * block].astype(BF)


def attend(me, qkvc, biases, n_samp, size):
    n_chip, _, _, lanes = qkvc.shape
    per = n_samp // 2
    block = lanes // per
    n_col = len(biases)
    tokens = n_chip * block
    wide = n_col * block
    whole = pl.BlockSpec((tokens, block), lambda s, c: (0, 0))
    spec = lambda feats: pl.BlockSpec((n_chip, None, feats, block), lambda s, c: (0, s // per, 0, s % per))
    return pl.pallas_call(
        functools.partial(attend_kernel, n_col, n_chip, n_samp, size),
        grid_spec=pltpu.PrefetchScalarGridSpec(
            num_scalar_prefetch=1,
            grid=(n_samp,),
            in_specs=[spec(4 * size)] + [whole] * n_col,
            out_specs=[spec(size)] + [whole] * n_col,
            scratch_shapes=[
                pltpu.VMEM((tokens, wide), F32),
                pltpu.VMEM((tokens, wide), F32),
                pltpu.VMEM((block, wide), BF),
                pltpu.VMEM((block, wide), BF),
            ],
        ),
        out_shape=[jax.ShapeDtypeStruct((n_chip, 2, size, lanes), BF)]
        + [jax.ShapeDtypeStruct((tokens, block), BF)] * n_col,
        compiler_params=pltpu.CompilerParams(
            dimension_semantics=("arbitrary",), vmem_limit_bytes=48 * 1024 * 1024
        ),
    )(me, qkvc, *biases)


def transition(flat_in, attended_t, w_out, w_gate_up, w_down):
    mid = flat_in.astype(F32) + lax.dot_general(
        attended_t, w_out, (((0,), (0,)), ((), ())), preferred_element_type=F32
    )
    normed_mid = normalize(mid)[0].astype(BF)
    gate_up = jnp.dot(normed_mid, w_gate_up, preferred_element_type=F32)
    half = gate_up.shape[1] // 2
    hidden = (jax.nn.silu(gate_up[:, :half]) * gate_up[:, half:]).astype(BF)
    result = mid + jnp.dot(hidden, w_down, preferred_element_type=F32)
    return result.astype(BF)


def swap_cores(axis, size):
    return [(i, i ^ 1) for i in range(size)]


def back_pair(pair, bias_grad, bias_weight):
    normed_pair, scaled = normalize(pair.astype(F32))
    normed_grad = lax.dot_general(
        bias_grad, bias_weight, (((0,), (1,)), ((), ())), preferred_element_type=F32
    )
    centred = normed_grad - jnp.mean(normed_grad, axis=-1, keepdims=True)
    along = jnp.mean(normed_grad * normed_pair, axis=-1, keepdims=True)
    return (centred - normed_pair * along) * scaled


def shards(n_row, n_col, pair, bias_weight, single, w_qkv, w_out, w_gate_up, w_down, cotangent):
    samp, rows, width = single.shape
    heads = bias_weight.shape[1]
    size = width // heads
    half = samp // 2
    block = 2 * rows
    n_chip = n_row // 2
    core = lax.rem(lax.axis_index("row"), 2)
    me = lax.axis_index("col").astype(jnp.int32).reshape(1)
    cores = [(i, i ^ 1) for i in range(n_row)]

    def join(values):
        keep = lax.dynamic_slice_in_dim(values, core * half, half, 0)
        send = lax.dynamic_slice_in_dim(values, (1 - core) * half, half, 0)
        got = lax.ppermute(send, "row", cores)
        first = jnp.where(core == 0, keep, got)
        second = jnp.where(core == 0, got, keep)
        return jnp.concatenate([first, second], axis=1)

    tokens = join(single).reshape(half * block, width)
    cotan = join(cotangent).reshape(half * block, width)

    bias = lax.all_to_all(project_pair(pair, bias_weight), "row", 0, 0, tiled=True)
    bias, tokens = lax.optimization_barrier((bias, tokens))
    bias = bias.reshape(n_row * rows, pair.shape[1])
    biases = [bias] + [
        lax.ppermute(bias, "col", [(i, i ^ k) for i in range(n_col)]) for k in range(1, n_col)
    ]

    normed = normalize(tokens.astype(F32))[0].astype(BF)
    projected = lax.dot_general(
        w_qkv, normed, (((0,), (1,)), ((), ())), preferred_element_type=F32
    ).astype(BF)
    projected = projected.reshape(3, heads, size, half * block)
    cotan_t = cotan.T.reshape(heads, size, half * block)
    packed = jnp.concatenate([projected[0], projected[1], projected[2], cotan_t], axis=1)
    packed = lax.all_to_all(packed, "row", 0, 0, tiled=True)
    packed = packed.reshape(n_chip, 2, 4 * size, half * block)
    attended, *grads = attend(me, packed, biases, samp, size)

    grads = [grads[0]] + [
        lax.ppermute(grads[k], "col", [(i, i ^ k) for i in range(n_col)]) for k in range(1, n_col)
    ]
    attended = attended.reshape(n_row, size, half * block)
    attended = lax.all_to_all(attended, "row", 0, 0, tiled=True)
    updated = transition(tokens, attended.reshape(width, half * block), w_out, w_gate_up, w_down)
    updated = updated.reshape(half, block, width)
    mine = lax.dynamic_slice_in_dim(updated, core * rows, rows, 1)
    theirs = lax.dynamic_slice_in_dim(updated, (1 - core) * rows, rows, 1)
    got = lax.ppermute(theirs, "row", cores)
    updated = jnp.concatenate([jnp.where(core == 0, mine, got), jnp.where(core == 0, got, mine)], axis=0)

    bias_grad = grads[0].astype(F32)
    for k in range(1, n_col):
        bias_grad = bias_grad + grads[k].astype(F32)
    bias_grad = bias_grad.astype(BF).reshape(n_row, rows, pair.shape[1])
    bias_grad = lax.all_to_all(bias_grad, "row", 0, 0, tiled=True)
    pair_grad = back_pair(pair, bias_grad, bias_weight)
    return (updated, pair_grad)


def solution(mesh):
    sizes = dict(mesh.shape)
    return jax.shard_map(
        functools.partial(shards, sizes["row"], sizes["col"]),
        mesh=mesh,
        in_specs=(
            P("row", "col", None),
            P(),
            P("col", "row", None),
            P(),
            P(),
            P(),
            P(),
            P("col", "row", None),
        ),
        out_specs=(P("col", "row", None), P("row", "col", None)),
        check_vma=False,
    )
```

time: 444 us -> 254 us (0.57)
  waiting for transfers between devices: 202 us -> 75.6 us
  matrix products: 118 us -> 17.7 us
  local copies, waits for them, and re-layouts: 100 us -> 29.5 us
  Pallas kernels: 0 us -> 55 us
  starting transfers between devices: 0.12 us -> 53 us
  other arithmetic: 7.22 us -> 21.5 us
  between operations: 13.9 us -> 0.94 us
    all_gather x2 -> x0, waiting for transfers between devices: 161 us -> none  [the longest x1 124 us: shards(): kv_all = lax.all_gather(kv_local, 'row', axis=1, tiled=True)]
    dot_general x18 -> x5, matrix products: 81.8 us -> 15.9 us  [the longest x1 4.96 us: back_pair(): lax.dot_general(bias_grad, bias_weight, (((0,), (1,)), ((), ())), preferr...]
    ppermute x0 -> x17, waiting for transfers between devices: none -> 59 us  [the longest x7 39.5 us: shards(): lax.ppermute(bias, 'col', [(i, i ^ k) for i in range(n_col)])]
    pallas_call x0 -> x1, Pallas kernels: none -> 55 us  [attend(): pl.pallas_call(functools.partial(attend_kernel, n_col, n_chip, n_samp, si...]
    dynamic_slice x30 -> x3, local copies, waits for them, and re-layouts: 58.3 us -> 4.28 us  [the longest x2 3.54 us: join(): send = lax.dynamic_slice_in_dim(values, (1 - core) * half, half, 0)]
    reduce_scatter x1 -> x0, waiting for transfers between devices: 41.4 us -> none  [shards(): lax.psum_scatter(grad_local, 'col', scatter_dimension=2, tiled=True)]
    sub x6 -> x0, matrix products: 34.1 us -> none  [attend_sample(): weights = jax.nn.softmax(scores, axis=-1)]
    all_to_all x0 -> x4, starting transfers between devices: none -> 29.2 us  [the longest x1 11.3 us: shards(): bias_grad = lax.all_to_all(bias_grad, 'row', 0, 0, tiled=True)]
  transfers between devices with their start and end apart: 3 -> 21, of which waited for: 3 -> 10; matrix products, arithmetic and copies ran while one was open for 5% -> 13% of each run, Pallas kernels for 0% -> 0%
where the time goes in v1:
time: 254 us; the launch traced here: 253 us
  waiting for transfers between devices  75.6 us (30%)
  Pallas kernels  55 us (22%)
  starting transfers between devices  53 us (21%)
  local copies, waits for them, and re-layouts  29.5 us (12%)
  other arithmetic  21.5 us (8%)
  matrix products  17.7 us (7%)
    pallas_call x1, Pallas kernels, attend(): pl.pallas_call(functools.partial(attend_kernel, n_col, n_chip, n_samp, si...  55 us
    ppermute x7, waiting for transfers between devices, shards(): lax.ppermute(bias, 'col', [(i, i ^ k) for i in range(n_col)])  39.5 us
    ppermute x7, waiting for transfers between devices, shards(): lax.ppermute(grads[k], 'col', [(i, i ^ k) for i in range(n_col)])  19.5 us
    unnamed x38, local copies, waits for them, and re-layouts  14.7 us
    ppermute x7, starting transfers between devices, shards(): lax.ppermute(grads[k], 'col', [(i, i ^ k) for i in range(n_col)])  11.9 us
    all_to_all x1, starting transfers between devices, shards(): bias_grad = lax.all_to_all(bias_grad, 'row', 0, 0, tiled=True)  11.3 us
    all_to_all x1, waiting for transfers between devices, shards(): bias_grad = lax.all_to_all(bias_grad, 'row', 0, 0, tiled=True)  9.01 us
    ppermute x7, starting transfers between devices, shards(): lax.ppermute(bias, 'col', [(i, i ^ k) for i in range(n_col)])  8.89 us
  transfers between devices with their start and end apart: 21, of which 10 were waited for; matrix products, arithmetic and copies ran while one was open for 13% of the time, Pallas kernels for 0%

profile of v1, /device:TPU:1, one launch (start us, length us, event | category | flops | bytes accessed | tf_op | source)
XLA Modules:
  0.0 253.2 jit_solution(11950342094234353898)
XLA Ops:
  5.6 4.1 %copy.28 = bf16[64,128,128]{1,2,0:T(8,128)(2,1)} copy(bf16[64,128,128]{2,1,0:T(8,128)(2,1)} %param.8) | data formatting | bytes 4194304 | tf_op args[0]
  9.7 2.2 convert_reduce_fusion
  15.5 8.2 %all-to-all-start = ((bf16[16,64,128]{2,1,0:T(8,128)(2,1)}), bf16[16,64,128]{2,1,0:T(8,128)(2,1)}, u32[]{:S(2)}, u32[]{:S(2)}) async-start(bf16[16,64,128]{2,1,0:T(8,128)(2,1)} %copy.30), calls=%async_computation | async-start | bytes 524288 | tf_op jit(solution)/shard_map/all_to_all | solution.py:179
  23.7 2.1 broadcast_select_fusion.3
  26.7 2.1 copy.34
  35.3 2.7 %fusion.10 = bf16[2304,384]{0,1:T(8,128)(2,1)S(1)} fusion(bf16[768,2304]{1,0:T(8,128)(2,1)S(1)} %copy-done, bf16[384,768]{1,0:T(8,128)(2,1)} %bitcast.34, f32[384]{0:T(512)S(1)} %add_rsqrt_fusion.2, f32[384]{0:T(512)S(1)} %broadcast_multiply_fusion.4), kind=kOutput, calls=%fused_computation.12 | convolution fusion | flops 1361018880 | bytes 5901312 | tf_op jit(solution)/shard_map/dot_general | solution.py:187
  39.3 2.1 copy.33
  41.4 2.1 copy.32
  43.5 2.1 copy.31
  45.6 3.3 %pad_maximum_fusion = bf16[16,192,384]{2,1,0:T(8,128)(2,1)} fusion(bf16[16,48,384]{2,1,0:T(8,128)(2,1)} %bitcast.36, bf16[16,48,384]{2,1,0:T(8,128)(2,1)} %bitcast.37, bf16[16,48,384]{2,1,0:T(8,128)(2,1)} %bitcast.38, bf16[16,48,384]{2,1,0:T(8,128)(2,1)} %bitcast.39), kind=kLoop, calls=%fused_computation.15 | loop fusion | flops 9437184 | bytes 4718592 | tf_op jit(solution)/shard_map/concatenate | solution.py:192
  49.0 5.3 %all-to-all-start.1 = ((bf16[16,192,384]{2,1,0:T(8,128)(2,1)}), bf16[16,192,384]{2,1,0:T(8,128)(2,1)}, u32[]{:S(2)}, u32[]{:S(2)}) async-start(bf16[16,192,384]{2,1,0:T(8,128)(2,1)} %pad_maximum_fusion), calls=%async_computation.1 | async-start | bytes 4718592 | tf_op jit(solution)/shard_map/all_to_all | solution.py:193
  55.6 2.6 %collective-permute-start.3 = (bf16[1024,128]{1,0:T(8,128)(2,1)}, bf16[1024,128]{1,0:T(8,128)(2,1)S(1)}, u32[]{:S(2)}, u32[]{:S(2)}) collective-permute-start(bf16[1024,128]{1,0:T(8,128)(2,1)} %bitcast.12.refs_0_), channel_id=1, source_target_pairs={{0,2},{1,3},{2,0},{3,1},{4,6},{5,7},{6,4},{7,5},{8,10},{9,11},{10,... | collective-permute-start | bytes 786440 | tf_op jit(solution)/shard_map/ppermute | solution.py:183
  59.4 2.9 %collective-permute-done.2.refs_1_ = bf16[1024,128]{1,0:T(8,128)(2,1)S(1)} collective-permute-done((bf16[1024,128]{1,0:T(8,128)(2,1)}, bf16[1024,128]{1,0:T(8,128)(2,1)S(1)}, u32[]{:S(2)}, u32[]{:S(2)}) %collective-permute-start.2) | collective-permute-done | bytes 262176 | tf_op jit(solution)/shard_map/ppermute | solution.py:183
  63.0 3.4 %collective-permute-start.7 = (bf16[1024,128]{1,0:T(8,128)(2,1)}, bf16[1024,128]{1,0:T(8,128)(2,1)}, u32[]{:S(2)}, u32[]{:S(2)}) collective-permute-start(bf16[1024,128]{1,0:T(8,128)(2,1)} %bitcast.12.refs_0_), channel_id=1, source_target_pairs={{0,6},{1,7},{2,4},{3,5},{4,2},{5,3},{6,0},{7,1},{8,14},{9,15},{10,... | collective-permute-start | bytes 786440 | tf_op jit(solution)/shard_map/ppermute | solution.py:183
  66.3 4.0 %collective-permute-done.3.refs_2_ = bf16[1024,128]{1,0:T(8,128)(2,1)S(1)} collective-permute-done((bf16[1024,128]{1,0:T(8,128)(2,1)}, bf16[1024,128]{1,0:T(8,128)(2,1)S(1)}, u32[]{:S(2)}, u32[]{:S(2)}) %collective-permute-start.3) | collective-permute-done | bytes 262176 | tf_op jit(solution)/shard_map/ppermute | solution.py:183
  72.4 31.7 %collective-permute-done.5.refs_4_ = bf16[1024,128]{1,0:T(8,128)(2,1)} collective-permute-done((bf16[1024,128]{1,0:T(8,128)(2,1)}, bf16[1024,128]{1,0:T(8,128)(2,1)}, u32[]{:S(2)}, u32[]{:S(2)}) %collective-permute-start.5) | collective-permute-done | bytes 262176 | tf_op jit(solution)/shard_map/ppermute | solution.py:183
  106.0 55.0 %shard_map.95 = (bf16[8,2,48,384]{3,2,1,0:T(8,128)(2,1)S(1)}, bf16[1024,128]{1,0:T(8,128)(2,1)S(1)}, bf16[1024,128]{1,0:T(8,128)(2,1)S(1)}, bf16[1024,128]{1,0:T...) custom-call(s32[1]{0:T(128)} %bitcast.3.c_ref, ...), custom_call_target="tpu_custom_call" | custom-call | tf_op jit(solution)/shard_map/pallas_call | solution.py:109
  161.8 3.2 %collective-permute-start.16 = (bf16[1024,128]{1,0:T(8,128)(2,1)S(1)}, bf16[1024,128]{1,0:T(8,128)(2,1)S(1)}, u32[]{:S(2)}, u32[]{:S(2)}) collective-permute-start(bf16[1024,128]{1,0:T(8,128)(2,1)S(1)} %get-tuple-element.23), channel_id=1, source_target_pairs={{0,7},{1,6},{2,5},{3,4},{4,3},{5,2},{6,1},{7,0},{8,15},{9,14},{10,... | collective-permute-start | bytes 786440 | tf_op jit(solution)/shard_map/ppermute | solution.py:198
  167.2 2.7 %collective-permute-start.12 = (bf16[1024,128]{1,0:T(8,128)(2,1)S(1)}, bf16[1024,128]{1,0:T(8,128)(2,1)S(1)}, u32[]{:S(2)}, u32[]{:S(2)}) collective-permute-start(bf16[1024,128]{1,0:T(8,128)(2,1)S(1)} %get-tuple-element.19), channel_id=1, source_target_pairs={{0,3},{1,2},{2,1},{3,0},{4,7},{5,6},{6,5},{7,4},{8,11},{9,10},{10,... | collective-permute-start | bytes 786440 | tf_op jit(solution)/shard_map/ppermute | solution.py:198
  169.9 9.6 %collective-permute-done.16 = bf16[1024,128]{1,0:T(8,128)(2,1)S(1)} collective-permute-done((bf16[1024,128]{1,0:T(8,128)(2,1)S(1)}, bf16[1024,128]{1,0:T(8,128)(2,1)S(1)}, u32[]{:S(2)}, u32[]{:S(2)}) %collective-permute-start.16) | collective-permute-done | bytes 262176 | tf_op jit(solution)/shard_map/ppermute | solution.py:198
  180.5 2.8 %collective-permute-start.10 = (bf16[1024,128]{1,0:T(8,128)(2,1)S(1)}, bf16[1024,128]{1,0:T(8,128)(2,1)S(1)}, u32[]{:S(2)}, u32[]{:S(2)}) collective-permute-start(bf16[1024,128]{1,0:T(8,128)(2,1)S(1)} %get-tuple-element.17), channel_id=1, source_target_pairs={{0,1},{1,0},{2,3},{3,2},{4,5},{5,4},{6,7},{7,6},{8,9},{9,8},{10,11... | collective-permute-start | bytes 786440 | tf_op jit(solution)/shard_map/ppermute | solution.py:198
  183.3 5.7 %collective-permute-done.13 = bf16[1024,128]{1,0:T(8,128)(2,1)S(1)} collective-permute-done((bf16[1024,128]{1,0:T(8,128)(2,1)S(1)}, bf16[1024,128]{1,0:T(8,128)(2,1)S(1)}, u32[]{:S(2)}, u32[]{:S(2)}) %collective-permute-start.13) | collective-permute-done | bytes 262176 | tf_op jit(solution)/shard_map/ppermute | solution.py:198
  189.0 4.2 %collective-permute-done.10 = bf16[1024,128]{1,0:T(8,128)(2,1)S(1)} collective-permute-done((bf16[1024,128]{1,0:T(8,128)(2,1)S(1)}, bf16[1024,128]{1,0:T(8,128)(2,1)S(1)}, u32[]{:S(2)}, u32[]{:S(2)}) %collective-permute-start.10) | collective-permute-done | bytes 262176 | tf_op jit(solution)/shard_map/ppermute | solution.py:198
  194.2 11.3 %all-to-all-start.3 = ((bf16[16,64,128]{2,1,0:T(8,128)(2,1)}), bf16[16,64,128]{2,1,0:T(8,128)(2,1)}, u32[]{:S(2)}, u32[]{:S(2)}) async-start(bf16[16,64,128]{2,1,0:T(8,128)(2,1)} %bitcast.41), calls=%async_computation.3 | async-start | bytes 524288 | tf_op jit(solution)/shard_map/all_to_all | solution.py:213
  205.5 9.0 %all-to-all-done.3 = bf16[16,64,128]{2,1,0:T(8,128)(2,1)} async-done(((bf16[16,64,128]{2,1,0:T(8,128)(2,1)}), bf16[16,64,128]{2,1,0:T(8,128)(2,1)}, u32[]{:S(2)}, u32[]{:S(2)}) %all-to-all-start.3) | async-done | bytes 262176 | tf_op jit(solution)/shard_map/all_to_all | solution.py:213
  214.6 4.4 %all-to-all-start.2 = ((bf16[16,48,384]{2,1,0:T(8,128)(2,1)}), bf16[16,48,384]{2,1,0:T(8,128)(2,1)}, u32[]{:S(2)}, u32[]{:S(2)}) async-start(bf16[16,48,384]{2,1,0:T(8,128)(2,1)} %bitcast.31), calls=%async_computation.2 | async-start | bytes 1179648 | tf_op jit(solution)/shard_map/all_to_all | solution.py:201
  218.9 5.0 %fusion.37 = (f32[64,128]{1,0:T(8,128)S(1)}, f32[64,128]{1,0:T(8,128)S(1)}, f32[64,128,128]{1,2,0:T(8,128)}) fusion(f32[64,128]{1,0:T(8,128)} %copy-done.12, f32[64,128]{1,0:T(8,128)} %copy-done.10, bf16[64,128,128]{1,2,0:T(8,128)(2,1)} %copy.28, bf16[128,16]{0,1:T(8,128)(2,1)S(1)} %copy-done.16, bf16[16,64,128]{2,1,0:T(8,128)(2,1)} %all-to-all-done.3), kind=kOutput, calls=%fused_computation.62 | convolution fusion | flops 39829504 | bytes 6688768 | tf_op jit(solution)/shard_map/dot_general | solution.py:149
  225.1 5.7 %all-to-all-done.2 = bf16[16,48,384]{2,1,0:T(8,128)(2,1)} async-done(((bf16[16,48,384]{2,1,0:T(8,128)(2,1)}), bf16[16,48,384]{2,1,0:T(8,128)(2,1)}, u32[]{:S(2)}, u32[]{:S(2)}) %all-to-all-start.2) | async-done | bytes 589856 | tf_op jit(solution)/shard_map/all_to_all | solution.py:201
  230.8 2.3 fusion.39
  233.4 4.5 %fusion.26 = f32[384,3072]{1,0:T(8,128)S(1)} fusion(bf16[768,3072]{1,0:T(8,128)(2,1)} %param.13, f32[384,768]{1,0:T(8,128)S(1)} %get-tuple-element.42, f32[384]{0:T(512)S(1)} %add_rsqrt_fusion.1, f32[384]{0:T(512)S(1)} %broadcast_multiply_fusion.3), kind=kOutput, calls=%fused_computation.31 | convolution fusion | flops 1812824064 | bytes 10619904 | tf_op jit(solution)/shard_map/dot_general | solution.py:136
  242.6 3.1 %fusion.8 = f32[64,128,128]{1,2,0:T(8,128)} fusion(bf16[64,128,128]{1,2,0:T(8,128)(2,1)S(1)} %copy-done.7, f32[64,128,128]{1,2,0:T(8,128)S(1)} %copy-done.8, f32[64,128]{1,0:T(8,128)S(1)} %copy-done.14, f32[64,128]{1,0:T(8,128)S(1)} %copy-done.15, f32[64,128]{1,0:T(8,128)S(1)} %copy-done.13, f32[64,128]{1,0:T(8,128)S(1)} %copy-done.11), kind=kLoop, calls=%fused_computation.10 | loop fusion | flops 7340032 | bytes 10616832 | tf_op jit(solution)/shard_map/mul | solution.py:154
  245.6 5.6 %copy.36 = f32[64,128,128]{2,1,0:T(8,128)} copy(f32[64,128,128]{1,2,0:T(8,128)} %fusion.8) | data formatting | bytes 8388608
  (85 shorter events, 37.2 us)
Async XLA Ops:
  0.6 34.7 %copy-start = (bf16[768,2304]{1,0:T(8,128)(2,1)S(1)}, bf16[768,2304]{1,0:T(8,128)(2,1)}, u32[]{:S(2)}) copy-start(bf16[768,2304]{1,0:T(8,128)(2,1)} %param.11) | copy-start | bytes 10616836
  2.5 21.2 %collective-permute-start.1 = (bf16[3,64,768]{2,1,0:T(8,128)(2,1)}, bf16[3,64,768]{2,1,0:T(8,128)(2,1)}, u32[]{:S(2)}, u32[]{:S(2)}) collective-permute-start(bf16[3,64,768]{2,1,0:T(8,128)(2,1)} %constant_dynamic-slice_fusion.1), channel_id=1, source_target_pairs={{0,8},{8,0},{16,24},{24,16},{32,40},{40,32},{48,56},{56,48},{64,72... | collective-permute-start | bytes 884744 | tf_op jit(solution)/shard_map/ppermute | solution.py:171
  5.6 18.1 %collective-permute-start = (bf16[3,64,768]{2,1,0:T(8,128)(2,1)}, bf16[3,64,768]{2,1,0:T(8,128)(2,1)}, u32[]{:S(2)}, u32[]{:S(2)}) collective-permute-start(bf16[3,64,768]{2,1,0:T(8,128)(2,1)} %constant_dynamic-slice_fusion.2), channel_id=1, source_target_pairs={{0,8},{8,0},{16,24},{24,16},{32,40},{40,32},{48,56},{56,48},{64,72... | collective-permute-start | bytes 884744 | tf_op jit(solution)/shard_map/ppermute | solution.py:171
  9.7 2.3 copy-start.6
  9.7 3.1 %copy-start.16 = (bf16[128,16]{0,1:T(8,128)(2,1)S(1)}, bf16[128,16]{0,1:T(8,128)(2,1)}, u32[]{:S(2)}) copy-start(bf16[128,16]{0,1:T(8,128)(2,1)} %param.9) | copy-start | bytes 12292
  12.0 2.7 %copy-start.10 = (f32[64,128]{1,0:T(8,128)}, f32[64,128]{1,0:T(8,128)S(1)}, u32[]{:S(2)}) copy-start(f32[64,128]{1,0:T(8,128)S(1)} %broadcast_multiply_fusion.2) | copy-start | bytes 98308
  15.5 17.2 %all-to-all-start = ((bf16[16,64,128]{2,1,0:T(8,128)(2,1)}), bf16[16,64,128]{2,1,0:T(8,128)(2,1)}, u32[]{:S(2)}, u32[]{:S(2)}) async-start(bf16[16,64,128]{2,1,0:T(8,128)(2,1)} %copy.30), calls=%async_computation | async-start | bytes 524288 | tf_op jit(solution)/shard_map/all_to_all | solution.py:179
  49.0 55.1 %all-to-all-start.1 = ((bf16[16,192,384]{2,1,0:T(8,128)(2,1)}), bf16[16,192,384]{2,1,0:T(8,128)(2,1)}, u32[]{:S(2)}, u32[]{:S(2)}) async-start(bf16[16,192,384]{2,1,0:T(8,128)(2,1)} %pad_maximum_fusion), calls=%async_computation.1 | async-start | bytes 4718592 | tf_op jit(solution)/shard_map/all_to_all | solution.py:193
  54.3 8.0 %collective-permute-start.2 = (bf16[1024,128]{1,0:T(8,128)(2,1)}, bf16[1024,128]{1,0:T(8,128)(2,1)S(1)}, u32[]{:S(2)}, u32[]{:S(2)}) collective-permute-start(bf16[1024,128]{1,0:T(8,128)(2,1)} %bitcast.12.refs_0_), channel_id=1, source_target_pairs={{0,1},{1,0},{2,3},{3,2},{4,5},{5,4},{6,7},{7,6},{8,9},{9,8},{10,11... | collective-permute-start | bytes 786440 | tf_op jit(solution)/shard_map/ppermute | solution.py:183
  55.6 14.8 %collective-permute-start.3 = (bf16[1024,128]{1,0:T(8,128)(2,1)}, bf16[1024,128]{1,0:T(8,128)(2,1)S(1)}, u32[]{:S(2)}, u32[]{:S(2)}) collective-permute-start(bf16[1024,128]{1,0:T(8,128)(2,1)} %bitcast.12.refs_0_), channel_id=1, source_target_pairs={{0,2},{1,3},{2,0},{3,1},{4,6},{5,7},{6,4},{7,5},{8,10},{9,11},{10,... | collective-permute-start | bytes 786440 | tf_op jit(solution)/shard_map/ppermute | solution.py:183
  58.2 14.2 %collective-permute-start.4 = (bf16[1024,128]{1,0:T(8,128)(2,1)}, bf16[1024,128]{1,0:T(8,128)(2,1)}, u32[]{:S(2)}, u32[]{:S(2)}) collective-permute-start(bf16[1024,128]{1,0:T(8,128)(2,1)} %bitcast.12.refs_0_), channel_id=1, source_target_pairs={{0,3},{1,2},{2,1},{3,0},{4,7},{5,6},{6,5},{7,4},{8,11},{9,10},{10,... | collective-permute-start | bytes 786440 | tf_op jit(solution)/shard_map/ppermute | solution.py:183
  58.2 45.9 %collective-permute-start.5 = (bf16[1024,128]{1,0:T(8,128)(2,1)}, bf16[1024,128]{1,0:T(8,128)(2,1)}, u32[]{:S(2)}, u32[]{:S(2)}) collective-permute-start(bf16[1024,128]{1,0:T(8,128)(2,1)} %bitcast.12.refs_0_), channel_id=1, source_target_pairs={{0,4},{1,5},{2,6},{3,7},{4,0},{5,1},{6,2},{7,3},{8,12},{9,13},{10,... | collective-permute-start | bytes 786440 | tf_op jit(solution)/shard_map/ppermute | solution.py:183
  58.9 45.1 %collective-permute-start.6 = (bf16[1024,128]{1,0:T(8,128)(2,1)}, bf16[1024,128]{1,0:T(8,128)(2,1)}, u32[]{:S(2)}, u32[]{:S(2)}) collective-permute-start(bf16[1024,128]{1,0:T(8,128)(2,1)} %bitcast.12.refs_0_), channel_id=1, source_target_pairs={{0,5},{1,4},{2,7},{3,6},{4,1},{5,0},{6,3},{7,2},{8,13},{9,12},{10,... | collective-permute-start | bytes 786440 | tf_op jit(solution)/shard_map/ppermute | solution.py:183
  63.0 41.1 %collective-permute-start.7 = (bf16[1024,128]{1,0:T(8,128)(2,1)}, bf16[1024,128]{1,0:T(8,128)(2,1)}, u32[]{:S(2)}, u32[]{:S(2)}) collective-permute-start(bf16[1024,128]{1,0:T(8,128)(2,1)} %bitcast.12.refs_0_), channel_id=1, source_target_pairs={{0,6},{1,7},{2,4},{3,5},{4,2},{5,3},{6,0},{7,1},{8,14},{9,15},{10,... | collective-permute-start | bytes 786440 | tf_op jit(solution)/shard_map/ppermute | solution.py:183
  71.1 33.0 %collective-permute-start.8 = (bf16[1024,128]{1,0:T(8,128)(2,1)}, bf16[1024,128]{1,0:T(8,128)(2,1)}, u32[]{:S(2)}, u32[]{:S(2)}) collective-permute-start(bf16[1024,128]{1,0:T(8,128)(2,1)} %bitcast.12.refs_0_), channel_id=1, source_target_pairs={{0,7},{1,6},{2,5},{3,4},{4,3},{5,2},{6,1},{7,0},{8,15},{9,14},{10,... | collective-permute-start | bytes 786440 | tf_op jit(solution)/shard_map/ppermute | solution.py:183
  161.8 17.6 %collective-permute-start.16 = (bf16[1024,128]{1,0:T(8,128)(2,1)S(1)}, bf16[1024,128]{1,0:T(8,128)(2,1)S(1)}, u32[]{:S(2)}, u32[]{:S(2)}) collective-permute-start(bf16[1024,128]{1,0:T(8,128)(2,1)S(1)} %get-tuple-element.23), channel_id=1, source_target_pairs={{0,7},{1,6},{2,5},{3,4},{4,3},{5,2},{6,1},{7,0},{8,15},{9,14},{10,... | collective-permute-start | bytes 786440 | tf_op jit(solution)/shard_map/ppermute | solution.py:198
  165.0 15.5 %collective-permute-start.15 = (bf16[1024,128]{1,0:T(8,128)(2,1)S(1)}, bf16[1024,128]{1,0:T(8,128)(2,1)S(1)}, u32[]{:S(2)}, u32[]{:S(2)}) collective-permute-start(bf16[1024,128]{1,0:T(8,128)(2,1)S(1)} %get-tuple-element.22), channel_id=1, source_target_pairs={{0,6},{1,7},{2,4},{3,5},{4,2},{5,3},{6,0},{7,1},{8,14},{9,15},{10,... | collective-permute-start | bytes 786440 | tf_op jit(solution)/shard_map/ppermute | solution.py:198
  165.8 17.5 %collective-permute-start.14 = (bf16[1024,128]{1,0:T(8,128)(2,1)S(1)}, bf16[1024,128]{1,0:T(8,128)(2,1)S(1)}, u32[]{:S(2)}, u32[]{:S(2)}) collective-permute-start(bf16[1024,128]{1,0:T(8,128)(2,1)S(1)} %get-tuple-element.21), channel_id=1, source_target_pairs={{0,5},{1,4},{2,7},{3,6},{4,1},{5,0},{6,3},{7,2},{8,13},{9,12},{10,... | collective-permute-start | bytes 786440 | tf_op jit(solution)/shard_map/ppermute | solution.py:198
  166.4 22.6 %collective-permute-start.13 = (bf16[1024,128]{1,0:T(8,128)(2,1)S(1)}, bf16[1024,128]{1,0:T(8,128)(2,1)S(1)}, u32[]{:S(2)}, u32[]{:S(2)}) collective-permute-start(bf16[1024,128]{1,0:T(8,128)(2,1)S(1)} %get-tuple-element.20), channel_id=1, source_target_pairs={{0,4},{1,5},{2,6},{3,7},{4,0},{5,1},{6,2},{7,3},{8,12},{9,13},{10,... | collective-permute-start | bytes 786440 | tf_op jit(solution)/shard_map/ppermute | solution.py:198
  167.2 21.9 %collective-permute-start.12 = (bf16[1024,128]{1,0:T(8,128)(2,1)S(1)}, bf16[1024,128]{1,0:T(8,128)(2,1)S(1)}, u32[]{:S(2)}, u32[]{:S(2)}) collective-permute-start(bf16[1024,128]{1,0:T(8,128)(2,1)S(1)} %get-tuple-element.19), channel_id=1, source_target_pairs={{0,3},{1,2},{2,1},{3,0},{4,7},{5,6},{6,5},{7,4},{8,11},{9,10},{10,... | collective-permute-start | bytes 786440 | tf_op jit(solution)/shard_map/ppermute | solution.py:198
  179.5 9.6 %collective-permute-start.11 = (bf16[1024,128]{1,0:T(8,128)(2,1)S(1)}, bf16[1024,128]{1,0:T(8,128)(2,1)S(1)}, u32[]{:S(2)}, u32[]{:S(2)}) collective-permute-start(bf16[1024,128]{1,0:T(8,128)(2,1)S(1)} %get-tuple-element.18), channel_id=1, source_target_pairs={{0,2},{1,3},{2,0},{3,1},{4,6},{5,7},{6,4},{7,5},{8,10},{9,11},{10,... | collective-permute-start | bytes 786440 | tf_op jit(solution)/shard_map/ppermute | solution.py:198
  180.5 12.7 %collective-permute-start.10 = (bf16[1024,128]{1,0:T(8,128)(2,1)S(1)}, bf16[1024,128]{1,0:T(8,128)(2,1)S(1)}, u32[]{:S(2)}, u32[]{:S(2)}) collective-permute-start(bf16[1024,128]{1,0:T(8,128)(2,1)S(1)} %get-tuple-element.17), channel_id=1, source_target_pairs={{0,1},{1,0},{2,3},{3,2},{4,5},{5,4},{6,7},{7,6},{8,9},{9,8},{10,11... | collective-permute-start | bytes 786440 | tf_op jit(solution)/shard_map/ppermute | solution.py:198
  194.2 20.4 %all-to-all-start.3 = ((bf16[16,64,128]{2,1,0:T(8,128)(2,1)}), bf16[16,64,128]{2,1,0:T(8,128)(2,1)}, u32[]{:S(2)}, u32[]{:S(2)}) async-start(bf16[16,64,128]{2,1,0:T(8,128)(2,1)} %bitcast.41), calls=%async_computation.3 | async-start | bytes 524288 | tf_op jit(solution)/shard_map/all_to_all | solution.py:213
  214.6 16.2 %all-to-all-start.2 = ((bf16[16,48,384]{2,1,0:T(8,128)(2,1)}), bf16[16,48,384]{2,1,0:T(8,128)(2,1)}, u32[]{:S(2)}, u32[]{:S(2)}) async-start(bf16[16,48,384]{2,1,0:T(8,128)(2,1)} %bitcast.31), calls=%async_computation.2 | async-start | bytes 1179648 | tf_op jit(solution)/shard_map/all_to_all | solution.py:201
  233.4 4.6 %copy-start.17 = (bf16[1536,768]{1,0:T(8,128)(2,1)S(1)}, bf16[1536,768]{1,0:T(8,128)(2,1)}, u32[]{:S(2)}) copy-start(bf16[1536,768]{1,0:T(8,128)(2,1)} %param.14) | copy-start | bytes 7077892
  238.0 4.6 %copy-start.7 = (bf16[64,128,128]{1,2,0:T(8,128)(2,1)S(1)}, bf16[64,128,128]{1,2,0:T(8,128)(2,1)}, u32[]{:S(2)}) copy-start(bf16[64,128,128]{1,2,0:T(8,128)(2,1)} %copy.28) | copy-start | bytes 6291460
  238.0 4.6 %copy-start.8 = (f32[64,128,128]{1,2,0:T(8,128)S(1)}, f32[64,128,128]{1,2,0:T(8,128)}, u32[]{:S(2)}) copy-start(f32[64,128,128]{1,2,0:T(8,128)} %get-tuple-element.43) | copy-start | bytes 12582916
  238.0 4.6 %copy-start.11 = (f32[64,128]{1,0:T(8,128)S(1)}, f32[64,128]{1,0:T(8,128)}, u32[]{:S(2)}) copy-start(f32[64,128]{1,0:T(8,128)} %copy-done.10) | copy-start | bytes 98308
  238.0 4.5 %copy-start.13 = (f32[64,128]{1,0:T(8,128)S(1)}, f32[64,128]{1,0:T(8,128)}, u32[]{:S(2)}) copy-start(f32[64,128]{1,0:T(8,128)} %copy-done.12) | copy-start | bytes 98308
  238.0 4.5 %copy-start.14 = (f32[64,128]{1,0:T(8,128)S(1)}, f32[64,128]{1,0:T(8,128)}, u32[]{:S(2)}) copy-start(f32[64,128]{1,0:T(8,128)} %broadcast_multiply_fusion) | copy-start | bytes 98308
  238.0 4.5 %copy-start.15 = (f32[64,128]{1,0:T(8,128)S(1)}, f32[64,128]{1,0:T(8,128)}, u32[]{:S(2)}) copy-start(f32[64,128]{1,0:T(8,128)} %broadcast_multiply_fusion.1) | copy-start | bytes 98308
  241.0 10.2 %collective-permute-start.9 = (bf16[3,64,768]{2,1,0:T(8,128)(2,1)}, bf16[3,64,768]{2,1,0:T(8,128)(2,1)}, u32[]{:S(2)}, u32[]{:S(2)}) collective-permute-start(bf16[3,64,768]{2,1,0:T(8,128)(2,1)} %constant_dynamic-slice_fusion), channel_id=1, source_target_pairs={{0,8},{8,0},{16,24},{24,16},{32,40},{40,32},{48,56},{56,48},{64,72... | collective-permute-start | bytes 884744 | tf_op jit(solution)/shard_map/ppermute | solution.py:206
  (7 other events, 6.8 us)

commit v2 on v1

v2 whole, which is shorter than its diff:
```python
import functools
import math

import jax
import jax.numpy as jnp
from jax import lax
from jax.experimental import pallas as pl
from jax.experimental.pallas import tpu as pltpu
from jax.sharding import PartitionSpec as P

BF = jnp.bfloat16
F32 = jnp.float32
LOG2E = 1.4426950408889634


def unit(values):
    mean_val = jnp.mean(values, axis=-1, keepdims=True)
    centred = values - mean_val
    variance = jnp.mean(centred * centred, axis=-1, keepdims=True)
    scaled = lax.rsqrt(variance + 1e-05)
    return centred * scaled, scaled

def pair_kernel(pair_ref, w_ref, out_ref):
    rows, cols, chans = pair_ref.shape
    heads = w_ref.shape[0]
    normed, _ = unit(pair_ref[...].astype(F32).reshape(rows * cols, chans))
    high = normed.astype(BF)
    low = (normed - high.astype(F32)).astype(BF)
    both = jnp.concatenate([high, low], axis=1)
    flat = lax.dot_general(w_ref[...], both, (((1,), (1,)), ((), ())), preferred_element_type=F32)
    out_ref[...] = flat.reshape(heads, rows, cols).astype(BF)

def pair_bias(pair, bias_weight, step=16):
    rows, cols, chans = pair.shape
    heads = bias_weight.shape[1]
    w = bias_weight.T
    w = jnp.concatenate([w, w], axis=1)
    return pl.pallas_call(
        pair_kernel, grid=(rows // step,),
        in_specs=[pl.BlockSpec((step, cols, chans), lambda i: (i, 0, 0)),
                  pl.BlockSpec((heads, 2 * chans), lambda i: (0, 0))],
        out_specs=pl.BlockSpec((heads, step, cols), lambda i: (0, i, 0)),
        out_shape=jax.ShapeDtypeStruct((heads, rows, cols), BF),
        compiler_params=pltpu.CompilerParams(dimension_semantics=("arbitrary",), vmem_limit_bytes=48 << 20),
    )(pair, w)

def back_kernel(pair_ref, grad_ref, w_ref, out_ref):
    rows, cols, chans = pair_ref.shape
    heads = w_ref.shape[0]
    normed, scaled = unit(pair_ref[...].astype(F32).reshape(rows * cols, chans))
    grad = grad_ref[...].reshape(heads, rows * cols)
    normed_grad = lax.dot_general(grad, w_ref[...], (((0,), (0,)), ((), ())), preferred_element_type=F32)
    centred = normed_grad - jnp.mean(normed_grad, axis=-1, keepdims=True)
    along = jnp.mean(normed_grad * normed, axis=-1, keepdims=True)
    out_ref[...] = ((centred - normed * along) * scaled).reshape(rows, cols, chans)

def pair_back(pair, grad, bias_weight, step=16):
    rows, cols, chans = pair.shape
    heads = bias_weight.shape[1]
    return pl.pallas_call(
        back_kernel, grid=(rows // step,),
        in_specs=[pl.BlockSpec((step, cols, chans), lambda i: (i, 0, 0)),
                  pl.BlockSpec((heads, step, cols), lambda i: (0, i, 0)),
                  pl.BlockSpec((heads, chans), lambda i: (0, 0))],
        out_specs=pl.BlockSpec((step, cols, chans), lambda i: (i, 0, 0)),
        out_shape=jax.ShapeDtypeStruct((rows, cols, chans), F32),
        compiler_params=pltpu.CompilerParams(dimension_semantics=("arbitrary",), vmem_limit_bytes=48 << 20),
    )(pair, grad, bias_weight.T)

def project_kernel(core_ref, single_ref, got_ref, cot_ref, gotc_ref, w_ref, packed_ref, tokens_ref, normed, cotan):
    half, block, width = tokens_ref.shape
    heads, _, lanes = packed_ref.shape
    size = width // heads
    rows = block // 2
    step = pl.program_id(0)
    core = core_ref[0]

    @pl.when(step == 0)
    def _():
        mine = pl.ds(pl.multiple_of(core * rows, rows), rows)
        other = pl.ds(pl.multiple_of((1 - core) * rows, rows), rows)
        for u in range(half):
            for src, far, dst in ((single_ref, got_ref, tokens_ref), (cot_ref, gotc_ref, cotan)):
                dst[u, mine, :] = src[core * half + u]
                dst[u, other, :] = far[core * half + u]
        normed[...] = unit(tokens_ref[...].reshape(lanes, width).astype(F32))[0].astype(BF)
        turned = cotan[...].reshape(lanes, width).astype(F32).T.astype(BF)
        for h in range(heads):
            packed_ref[h, 3 * size : 4 * size, :] = turned[h * size : (h + 1) * size]

    cols = w_ref.shape[1]
    out = jnp.dot(normed[...], w_ref[...], preferred_element_type=F32).T.astype(BF)
    for p in range(3):
        @pl.when(step // 2 == p)
        def _():
            base = (step % 2) * (cols // size)
            for h in range(cols // size):
                packed_ref[base + h, p * size : (p + 1) * size, :] = out[h * size : (h + 1) * size]

def project(core, single, got, cot, gotc, w_qkv, heads):
    samp, rows, width = single.shape
    half, block = samp // 2, 2 * rows
    lanes = half * block
    size = width // heads
    whole = pl.BlockSpec((samp, rows, width), lambda i, c: (0, 0, 0))
    return pl.pallas_call(
        project_kernel,
        grid_spec=pltpu.PrefetchScalarGridSpec(
            num_scalar_prefetch=1, grid=(6,),
            in_specs=[whole] * 4 + [pl.BlockSpec((width, width // 2), lambda i, c: (0, i))],
            out_specs=[pl.BlockSpec((heads, 4 * size, lanes), lambda i, c: (0, 0, 0)),
                       pl.BlockSpec((half, block, width), lambda i, c: (0, 0, 0))],
            scratch_shapes=[pltpu.VMEM((lanes, width), BF), pltpu.VMEM((half, block, width), BF)],
        ),
        out_shape=[jax.ShapeDtypeStruct((heads, 4 * size, lanes), BF), jax.ShapeDtypeStruct((half, block, width), BF)],
        compiler_params=pltpu.CompilerParams(dimension_semantics=("arbitrary",), vmem_limit_bytes=48 << 20),
    )(core, single, got, cot, gotc, w_qkv)


def attend_kernel(n_col, n_chip, n_samp, size, span, unroll, c_ref, blk_ref, *refs):
    bias_refs = refs[:n_col]
    att_ref = refs[n_col]
    out_refs = refs[n_col + 1 : 2 * n_col + 1]
    bias2, acc, kt, vt = refs[2 * n_col + 1 :]
    samp = pl.program_id(0)
    me = c_ref[0]
    block = blk_ref.shape[2]
    wide = block * n_col

    @pl.when(samp == 0)
    def _():
        for k in range(n_col):
            bias2[:, k * block : (k + 1) * block] = bias_refs[k][...].astype(F32) * LOG2E
        acc[...] = jnp.zeros_like(acc)
        rest = block - 2 * size
        kt[2 * size :, :] = jnp.zeros((rest, wide), BF)
        row = lax.broadcasted_iota(jnp.int32, (rest, wide), 0)
        vt[2 * size :, :] = jnp.where(row < 3, 1.0, 0.0).astype(BF)

    for k in range(n_col):
        owner = jnp.bitwise_xor(me, k)
        cols = slice(k * block, (k + 1) * block)
        keys = blk_ref[owner, size : 2 * size, :]
        kt[:size, cols] = keys
        kt[size : 2 * size, cols] = keys
        vals = blk_ref[owner, 2 * size : 3 * size, :]
        vt[:size, cols] = vals
        vt[size : 2 * size, cols] = vals

    scale = LOG2E / math.sqrt(size)
    rest = block - 2 * size
    row = lax.broadcasted_iota(jnp.int32, (rest, block), 0)

    def split(v):
        high = v.astype(BF).astype(F32)
        return high, v - high

    def one_block(b, carry):
        rows = pl.ds(pl.multiple_of(b * (block * span), block * span), block * span)
        lhs = []
        for i in range(span):
            high, low = split(blk_ref[b * span + i, :size, :].astype(F32) * scale)
            lhs.append(jnp.concatenate([high, low, jnp.zeros((rest, block), F32)], axis=0).T.astype(BF))
        lhs = jnp.concatenate(lhs, axis=0) if span > 1 else lhs[0]
        scores = jnp.dot(lhs, kt[...], preferred_element_type=F32) + bias2[rows, :]
        top = jnp.max(scores, axis=1, keepdims=True)
        probs = jnp.exp2(scores - top)
        mixed = lax.dot_general(
            probs.astype(BF), vt[...], (((1,), (1,)), ((), ())), preferred_element_type=F32
        )
        lhs2 = []
        for i in range(span):
            mixed_t = mixed[i * block : (i + 1) * block].T
            inv = 1.0 / mixed_t[2 * size : 2 * size + 1]
            att = mixed_t[:size] * inv
            att_ref[b * span + i, :, :] = att.astype(BF)
            cotan = blk_ref[b * span + i, 3 * size :, :].astype(F32)
            delta = -jnp.sum(cotan * att, axis=0, keepdims=True) * inv
            high, low = split(cotan * inv)
            d0, rem = split(delta)
            d1, d2 = split(rem)
            tail = jnp.where(row == 0, d0, jnp.where(row == 1, d1, jnp.where(row == 2, d2, 0.0)))
            lhs2.append(jnp.concatenate([high, low, tail], axis=0).T.astype(BF))
        lhs2 = jnp.concatenate(lhs2, axis=0) if span > 1 else lhs2[0]
        acc[rows, :] += probs * jnp.dot(lhs2, vt[...], preferred_element_type=F32)
        return carry

    lax.fori_loop(0, n_chip // span, one_block, 0, unroll=unroll)

    @pl.when(samp == n_samp - 1)
    def _():
        for k in range(n_col):
            out_refs[k][...] = acc[:, k * block : (k + 1) * block].astype(BF)


def attend(me, qkvc, biases, n_samp, size, span=1, unroll=1):
    n_chip, _, _, lanes = qkvc.shape
    per = n_samp // 2
    block = lanes // per
    n_col = len(biases)
    tokens = n_chip * block
    wide = n_col * block
    whole = pl.BlockSpec((tokens, block), lambda s, c: (0, 0))
    spec = lambda feats: pl.BlockSpec((n_chip, None, feats, block), lambda s, c: (0, s // per, 0, s % per))
    return pl.pallas_call(
        functools.partial(attend_kernel, n_col, n_chip, n_samp, size, span, unroll),
        grid_spec=pltpu.PrefetchScalarGridSpec(
            num_scalar_prefetch=1,
            grid=(n_samp,),
            in_specs=[spec(4 * size)] + [whole] * n_col,
            out_specs=[spec(size)] + [whole] * n_col,
            scratch_shapes=[
                pltpu.VMEM((tokens, wide), F32),
                pltpu.VMEM((tokens, wide), F32),
                pltpu.VMEM((block, wide), BF),
                pltpu.VMEM((block, wide), BF),
            ],
        ),
        out_shape=[jax.ShapeDtypeStruct((n_chip, 2, size, lanes), BF)]
        + [jax.ShapeDtypeStruct((tokens, block), BF)] * n_col,
        compiler_params=pltpu.CompilerParams(
            dimension_semantics=("arbitrary",), vmem_limit_bytes=56 * 1024 * 1024
        ),
    )(me, qkvc, *biases)


def transition(flat_in, attended_t, w_out, w_gate_up, w_down):
    mid = flat_in.astype(F32) + lax.dot_general(
        attended_t, w_out, (((0,), (0,)), ((), ())), preferred_element_type=F32
    )
    normed_mid = unit(mid)[0].astype(BF)
    gate_up = jnp.dot(normed_mid, w_gate_up, preferred_element_type=F32)
    half = gate_up.shape[1] // 2
    hidden = (jax.nn.silu(gate_up[:, :half]) * gate_up[:, half:]).astype(BF)
    result = mid + jnp.dot(hidden, w_down, preferred_element_type=F32)
    return result.astype(BF)


def shards(n_row, n_col, pair, bias_weight, single, w_qkv, w_out, w_gate_up, w_down, cotangent):
    samp, rows, width = single.shape
    heads = bias_weight.shape[1]
    size = width // heads
    half = samp // 2
    block = 2 * rows
    n_chip = n_row // 2
    core = lax.rem(lax.axis_index("row"), 2).astype(jnp.int32)
    me = lax.axis_index("col").astype(jnp.int32).reshape(1)
    cores = [(i, i ^ 1) for i in range(n_row)]
    flip = lambda k: [(i, i ^ k) for i in range(n_col)]

    got = lax.ppermute(single, "row", cores)
    got_cot = lax.ppermute(cotangent, "row", cores)
    bias = lax.all_to_all(pair_bias(pair, bias_weight, 32), "row", 0, 0, tiled=True)
    bias = bias.reshape(n_row * rows, pair.shape[1])
    packed, tokens = project(core.reshape(1), single, got, cotangent, got_cot, w_qkv, heads)

    far = lax.ppermute(bias, "col", flip(n_col // 2))
    biases = [bias] + [lax.ppermute(bias, "col", flip(k)) for k in range(1, n_col // 2)]
    biases += [far] + [lax.ppermute(far, "col", flip(k)) for k in range(1, n_col // 2)]

    packed = lax.all_to_all(packed, "row", 0, 0, tiled=True)
    packed = packed.reshape(n_chip, 2, 4 * size, half * block)
    attended, *grads = attend(me, packed, biases, samp, size, n_chip)

    grads = [grads[0]] + [lax.ppermute(grads[k], "col", flip(k)) for k in range(1, n_col)]
    attended = attended.reshape(n_row, size, half * block)
    attended = lax.all_to_all(attended, "row", 0, 0, tiled=True)

    bias_grad = grads[0].astype(F32)
    for k in range(1, n_col):
        bias_grad = bias_grad + grads[k].astype(F32)
    attended, bias_grad = lax.optimization_barrier((attended, bias_grad.astype(BF)))
    bias_grad = bias_grad.reshape(n_row, rows, pair.shape[1])
    bias_grad = lax.all_to_all(bias_grad, "row", 0, 0, tiled=True)

    updated = transition(
        tokens.reshape(half * block, width), attended.reshape(width, half * block), w_out, w_gate_up, w_down
    )
    updated, bias_grad = lax.optimization_barrier((updated, bias_grad))
    updated = updated.reshape(half, block, width)
    mine = lax.dynamic_slice_in_dim(updated, core * rows, rows, 1)
    theirs = lax.dynamic_slice_in_dim(updated, (1 - core) * rows, rows, 1)
    got = lax.ppermute(theirs, "row", cores)
    updated = jnp.concatenate([jnp.where(core == 0, mine, got), jnp.where(core == 0, got, mine)], axis=0)
    pair_grad = pair_back(pair, bias_grad, bias_weight, 16)
    return (updated, pair_grad)


def solution(mesh):
    sizes = dict(mesh.shape)
    return jax.shard_map(
        functools.partial(shards, sizes["row"], sizes["col"]),
        mesh=mesh,
        in_specs=(
            P("row", "col", None),
            P(),
            P("col", "row", None),
            P(),
            P(),
            P(),
            P(),
            P("col", "row", None),
        ),
        out_specs=(P("col", "row", None), P("row", "col", None)),
        check_vma=False,
    )
```

time: 254 us -> 177 us (0.70)
  local copies, waits for them, and re-layouts: 29.5 us -> 6.46 us
  other arithmetic: 21.5 us -> 5.46 us
  waiting for transfers between devices: 75.6 us -> 59.9 us
  Pallas kernels: 55 us -> 40.2 us
  matrix products: 17.7 us -> 8.27 us
    pallas_call x1, Pallas kernels: 55 us -> 23.5 us  [attend(): pl.pallas_call(functools.partial(attend_kernel, n_col, n_chip, n_samp, si...]
    pallas_call x0 -> x3, Pallas kernels: none -> 16.6 us  [the longest x1 6.66 us: project(): pl.pallas_call(project_kernel, grid_spec=pltpu.PrefetchScalarGridSpec(num...]
    dot_general x3 -> x0, matrix products: 9.46 us -> none  [the longest x1 4.96 us: back_pair(): lax.dot_general(bias_grad, bias_weight, (((0,), (1,)), ((), ())), preferr...]
    all_to_all x1, starting transfers between devices: 4.38 us -> 13.8 us  [shards(): attended = lax.all_to_all(attended, 'row', 0, 0, tiled=True)]
    unnamed x38 -> x30, local copies, waits for them, and re-layouts: 14.7 us -> 6.44 us
    slice x4 -> x0, local copies, waits for them, and re-layouts: 7.64 us -> none  [the longest x2 3.38 us: shards(): projected[0]]
    all_to_all x1, waiting for transfers between devices: 9.01 us -> 2.6 us  [shards(): bias_grad = lax.all_to_all(bias_grad, 'row', 0, 0, tiled=True)]
    reduce_sum x5 -> x1, other arithmetic: 5.92 us -> 0.26 us  [unit(): variance = jnp.mean(centred * centred, axis=-1, keepdims=True)]
  transfers between devices with their start and end apart: 21 -> 21, of which waited for: 10 -> 9; matrix products, arithmetic and copies ran while one was open for 13% -> 5% of each run, Pallas kernels for 0% -> 9%
where the time goes in v2:
time: 177 us
  waiting for transfers between devices  59.9 us (34%)
  starting transfers between devices  55.4 us (31%)
  Pallas kernels  40.2 us (23%)
  matrix products  8.27 us (5%)
  local copies, waits for them, and re-layouts  6.46 us (4%)
  other arithmetic  5.46 us (3%)
    ppermute x1, waiting for transfers between devices, shards(): far = lax.ppermute(bias, 'col', flip(n_col // 2))  25.1 us
    pallas_call x1, Pallas kernels, attend(): pl.pallas_call(functools.partial(attend_kernel, n_col, n_chip, n_samp, si...  23.5 us
    ppermute x7, waiting for transfers between devices, shards(): lax.ppermute(grads[k], 'col', flip(k))  18.5 us
    all_to_all x1, starting transfers between devices, shards(): attended = lax.all_to_all(attended, 'row', 0, 0, tiled=True)  13.8 us
    ppermute x3, waiting for transfers between devices, shards(): lax.ppermute(far, 'col', flip(k))  13.6 us
    all_to_all x1, starting transfers between devices, shards(): lax.all_to_all(pair_bias(pair, bias_weight, 32), 'row', 0, 0, tiled=True)  8.17 us
    ppermute x7, starting transfers between devices, shards(): lax.ppermute(grads[k], 'col', flip(k))  7.88 us
    all_to_all x1, starting transfers between devices, shards(): bias_grad = lax.all_to_all(bias_grad, 'row', 0, 0, tiled=True)  7.79 us
  transfers between devices with their start and end apart: 21, of which 9 were waited for; matrix products, arithmetic and copies ran while one was open for 5% of the time, Pallas kernels for 9%

profile of v2, /device:TPU:1, one launch (start us, length us, event | category | flops | bytes accessed | tf_op | source)
XLA Modules:
  0.0 176.5 jit_solution(3284905729317383704)
XLA Ops:
  0.6 1.5 collective-permute-start
  3.0 1.6 copy-done.1
  4.6 3.5 %shard_map.96 = bf16[16,64,128]{2,1,0:T(8,128)(2,1)} custom-call(bf16[64,128,128]{2,1,0:T(8,128)(2,1)S(1)} %copy-done.1, bf16[16,256]{1,0:T(8,128)(2,1)S(1)} %pad_maximum_fusion.1.w_ref), custom_call_target="tpu_custom_call" | custom-call | tf_op jit(solution)/shard_map/pallas_call | solution.py:38
  8.1 8.2 %all-to-all-start.1 = ((bf16[16,64,128]{2,1,0:T(8,128)(2,1)}), bf16[16,64,128]{2,1,0:T(8,128)(2,1)}, u32[]{:S(2)}, u32[]{:S(2)}) async-start(bf16[16,64,128]{2,1,0:T(8,128)(2,1)} %shard_map.96), calls=%async_computation.1 | async-start | bytes 524288 | tf_op jit(solution)/shard_map/all_to_all | solution.py:253
  16.3 6.7 %shard_map.95 = (bf16[16,192,384]{2,1,0:T(8,128)(2,1)S(1)}, bf16[3,128,768]{2,1,0:T(8,128)(2,1)S(1)}) custom-call(s32[1]{0:T(128)} %bitcast.core_ref, bf16[6,64,768]{2,1,0:T(8,128)(2,1)S(1)} %copy-done.4, bf16[6,64,768]{2,1,0:T(8,128)(2,1)} %collective-permute-done.got_ref, bf16[6,64,768]{2,1,0:T(8,128)(2,1)S(1)} %copy-done.5, ...), custom_call_target="tpu_custom_call" | custom-call | tf_op jit(solution)/shard_map/pallas_call | solution.py:106
  23.0 1.4 copy-done.3
  25.3 7.2 %all-to-all-start = ((bf16[16,192,384]{2,1,0:T(8,128)(2,1)}), bf16[16,192,384]{2,1,0:T(8,128)(2,1)}, u32[]{:S(2)}, u32[]{:S(2)}) async-start(bf16[16,192,384]{2,1,0:T(8,128)(2,1)} %copy-done.3), calls=%async_computation | async-start | bytes 4718592 | tf_op jit(solution)/shard_map/all_to_all | solution.py:261
  33.2 1.3 collective-permute-start.2
  34.5 2.6 %collective-permute-start.3 = (bf16[1024,128]{1,0:T(8,128)(2,1)}, bf16[1024,128]{1,0:T(8,128)(2,1)S(1)}, u32[]{:S(2)}, u32[]{:S(2)}) collective-permute-start(bf16[1024,128]{1,0:T(8,128)(2,1)} %bitcast.5.refs_0_), channel_id=1, source_target_pairs={{0,2},{1,3},{2,0},{3,1},{4,6},{5,7},{6,4},{7,5},{8,10},{9,11},{10,... | collective-permute-start | bytes 786440 | tf_op jit(solution)/shard_map/ppermute | solution.py:258
  37.1 25.1 %collective-permute-done.5.refs_4_ = bf16[1024,128]{1,0:T(8,128)(2,1)S(1)} collective-permute-done((bf16[1024,128]{1,0:T(8,128)(2,1)}, bf16[1024,128]{1,0:T(8,128)(2,1)S(1)}, u32[]{:S(2)}, u32[]{:S(2)}) %collective-permute-start.5) | collective-permute-done | bytes 262176 | tf_op jit(solution)/shard_map/ppermute | solution.py:257
  62.3 1.3 collective-permute-start.6
  63.5 2.6 %collective-permute-start.7 = (bf16[1024,128]{1,0:T(8,128)(2,1)S(1)}, bf16[1024,128]{1,0:T(8,128)(2,1)}, u32[]{:S(2)}, u32[]{:S(2)}) collective-permute-start(bf16[1024,128]{1,0:T(8,128)(2,1)S(1)} %collective-permute-done.5.refs_4_), channel_id=1, source_target_pairs={{0,2},{1,3},{2,0},{3,1},{4,6},{5,7},{6,4},{7,5},{8,10},{9,11},{10,... | collective-permute-start | bytes 786440 | tf_op jit(solution)/shard_map/ppermute | solution.py:259
  66.2 3.5 %collective-permute-done.6.refs_5_ = bf16[1024,128]{1,0:T(8,128)(2,1)} collective-permute-done((bf16[1024,128]{1,0:T(8,128)(2,1)S(1)}, bf16[1024,128]{1,0:T(8,128)(2,1)}, u32[]{:S(2)}, u32[]{:S(2)}) %collective-permute-start.6) | collective-permute-done | bytes 262176 | tf_op jit(solution)/shard_map/ppermute | solution.py:259
  69.7 8.1 %collective-permute-done.7.refs_6_ = bf16[1024,128]{1,0:T(8,128)(2,1)} collective-permute-done((bf16[1024,128]{1,0:T(8,128)(2,1)S(1)}, bf16[1024,128]{1,0:T(8,128)(2,1)}, u32[]{:S(2)}, u32[]{:S(2)}) %collective-permute-start.7) | collective-permute-done | bytes 262176 | tf_op jit(solution)/shard_map/ppermute | solution.py:259
  77.8 2.0 %collective-permute-done.8.refs_7_ = bf16[1024,128]{1,0:T(8,128)(2,1)} collective-permute-done((bf16[1024,128]{1,0:T(8,128)(2,1)S(1)}, bf16[1024,128]{1,0:T(8,128)(2,1)}, u32[]{:S(2)}, u32[]{:S(2)}) %collective-permute-start.8) | collective-permute-done | bytes 262176 | tf_op jit(solution)/shard_map/ppermute | solution.py:259
  79.8 23.5 %shard_map.97 = (bf16[8,2,48,384]{3,2,1,0:T(8,128)(2,1)}, bf16[1024,128]{1,0:T(8,128)(2,1)}, bf16[1024,128]{1,0:T(8,128)(2,1)}, bf16[1024,128]{1,0:T(8,128)(2,1)...) custom-call(s32[1]{0:T(128)} %bitcast.2.c_ref, ...), custom_call_target="tpu_custom_call" | custom-call | tf_op jit(solution)/shard_map/pallas_call | solution.py:205
  104.0 13.8 %all-to-all-start.2 = ((bf16[16,48,384]{2,1,0:T(8,128)(2,1)}), bf16[16,48,384]{2,1,0:T(8,128)(2,1)S(1)}, u32[]{:S(2)}, u32[]{:S(2)}) async-start(bf16[16,48,384]{2,1,0:T(8,128)(2,1)} %bitcast.21), calls=%async_computation.2 | async-start | bytes 1179648 | tf_op jit(solution)/shard_map/all_to_all | solution.py:267
  117.8 2.0 %collective-permute-start.13 = (bf16[1024,128]{1,0:T(8,128)(2,1)}, bf16[1024,128]{1,0:T(8,128)(2,1)}, u32[]{:S(2)}, u32[]{:S(2)}) collective-permute-start(bf16[1024,128]{1,0:T(8,128)(2,1)} %get-tuple-element.25), channel_id=1, source_target_pairs={{0,5},{1,4},{2,7},{3,6},{4,1},{5,0},{6,3},{7,2},{8,13},{9,12},{10,... | collective-permute-start | bytes 786440 | tf_op jit(solution)/shard_map/ppermute | solution.py:265
  119.8 1.9 %collective-permute-start.12 = (bf16[1024,128]{1,0:T(8,128)(2,1)}, bf16[1024,128]{1,0:T(8,128)(2,1)}, u32[]{:S(2)}, u32[]{:S(2)}) collective-permute-start(bf16[1024,128]{1,0:T(8,128)(2,1)} %get-tuple-element.24), channel_id=1, source_target_pairs={{0,4},{1,5},{2,6},{3,7},{4,0},{5,1},{6,2},{7,3},{8,12},{9,13},{10,... | collective-permute-start | bytes 786440 | tf_op jit(solution)/shard_map/ppermute | solution.py:265
  122.6 2.5 %collective-permute-start.9 = (bf16[1024,128]{1,0:T(8,128)(2,1)}, bf16[1024,128]{1,0:T(8,128)(2,1)}, u32[]{:S(2)}, u32[]{:S(2)}) collective-permute-start(bf16[1024,128]{1,0:T(8,128)(2,1)} %get-tuple-element.21), channel_id=1, source_target_pairs={{0,1},{1,0},{2,3},{3,2},{4,5},{5,4},{6,7},{7,6},{8,9},{9,8},{10,11... | collective-permute-start | bytes 786440 | tf_op jit(solution)/shard_map/ppermute | solution.py:265
  125.1 6.3 %collective-permute-done.13 = bf16[1024,128]{1,0:T(8,128)(2,1)} collective-permute-done((bf16[1024,128]{1,0:T(8,128)(2,1)}, bf16[1024,128]{1,0:T(8,128)(2,1)}, u32[]{:S(2)}, u32[]{:S(2)}) %collective-permute-start.13) | collective-permute-done | bytes 262176 | tf_op jit(solution)/shard_map/ppermute | solution.py:265
  131.4 6.1 %collective-permute-done.12 = bf16[1024,128]{1,0:T(8,128)(2,1)} collective-permute-done((bf16[1024,128]{1,0:T(8,128)(2,1)}, bf16[1024,128]{1,0:T(8,128)(2,1)}, u32[]{:S(2)}, u32[]{:S(2)}) %collective-permute-start.12) | collective-permute-done | bytes 262176 | tf_op jit(solution)/shard_map/ppermute | solution.py:265
  137.5 6.0 %collective-permute-done.9 = bf16[1024,128]{1,0:T(8,128)(2,1)} collective-permute-done((bf16[1024,128]{1,0:T(8,128)(2,1)}, bf16[1024,128]{1,0:T(8,128)(2,1)}, u32[]{:S(2)}, u32[]{:S(2)}) %collective-permute-start.9) | collective-permute-done | bytes 262176 | tf_op jit(solution)/shard_map/ppermute | solution.py:265
  143.5 2.5 %add_convert_fusion = bf16[1024,128]{1,0:T(8,128)(2,1)} fusion(bf16[1024,128]{1,0:T(8,128)(2,1)} %collective-permute-done.15, bf16[1024,128]{1,0:T(8,128)(2,1)} %collective-permute-done.14, bf16[1024,128]{1,0:T(8,128)(2,1)} %collective-permute-done.13, bf16[1024,128]{1,0:T(8,128)(2,1)} %collective-permute-done.12, ...), kind=kLoop, calls=%fused_computation.11 | loop fusion | flops 2097152 | bytes 2359296 | tf_op jit(solution)/shard_map/convert_element_type | solution.py:272
  146.0 2.0 %fusion.7 = (f32[384]{0:T(512)S(1)}, f32[384,768]{1,0:T(8,128)S(1)}) fusion(bf16[3,128,768]{2,1,0:T(8,128)(2,1)S(1)} %copy-done.7, bf16[768,384]{1,0:T(8,128)(2,1)S(1)} %bitcast.19, bf16[768,768]{1,0:T(8,128)(2,1)} %param.12), kind=kOutput, calls=%fused_computation.19 | convolution fusion | flops 453869184 | bytes 3540480 | tf_op jit(solution)/shard_map/dot_general | solution.py:228
  149.3 7.8 %all-to-all-start.3 = ((bf16[16,64,128]{2,1,0:T(8,128)(2,1)}), bf16[16,64,128]{2,1,0:T(8,128)(2,1)S(1)}, u32[]{:S(2)}, u32[]{:S(2)}) async-start(bf16[16,64,128]{2,1,0:T(8,128)(2,1)} %bitcast.20), calls=%async_computation.3 | async-start | bytes 524288 | tf_op jit(solution)/shard_map/all_to_all | solution.py:274
  157.1 4.8 %fusion.3 = f32[384,3072]{1,0:T(8,128)S(1)} fusion(bf16[768,3072]{1,0:T(8,128)(2,1)} %param.13, f32[384,768]{1,0:T(8,128)} %copy-done.9, f32[384]{0:T(512)S(1)} %add_rsqrt_fusion, f32[384]{0:T(512)S(1)} %broadcast_multiply_fusion), kind=kOutput, calls=%fused_computation.7 | convolution fusion | flops 1812824064 | bytes 10619904 | tf_op jit(solution)/shard_map/dot_general | solution.py:232
  162.0 1.4 fusion.1
  163.4 2.6 %all-to-all-done.3.grad_ref = bf16[16,64,128]{2,1,0:T(8,128)(2,1)S(1)} async-done(((bf16[16,64,128]{2,1,0:T(8,128)(2,1)}), bf16[16,64,128]{2,1,0:T(8,128)(2,1)S(1)}, u32[]{:S(2)}, u32[]{:S(2)}) %all-to-all-start.3) | async-done | bytes 262176 | tf_op jit(solution)/shard_map/all_to_all | solution.py:274
  166.5 1.6 copy-done.2
  168.1 6.5 %shard_map.98 = f32[64,128,128]{2,1,0:T(8,128)} custom-call(bf16[64,128,128]{2,1,0:T(8,128)(2,1)S(1)} %copy-done.2, bf16[16,64,128]{2,1,0:T(8,128)(2,1)S(1)} %all-to-all-done.3.grad_ref, bf16[16,128]{1,0:T(8,128)(2,1)S(1)} %bitcast.18), custom_call_target="tpu_custom_call" | custom-call | tf_op jit(solution)/shard_map/pallas_call | solution.py:60
  174.6 1.1 broadcast_select_fusion.1
  (55 shorter events, 6.6 us)
Async XLA Ops:
  0.6 161.3 %copy-start = (bf16[1536,768]{1,0:T(8,128)(2,1)S(1)}, bf16[1536,768]{1,0:T(8,128)(2,1)}, u32[]{:S(2)}) copy-start(bf16[1536,768]{1,0:T(8,128)(2,1)} %param.14) | copy-start | bytes 7077892
  0.6 15.7 %collective-permute-start = (bf16[6,64,768]{2,1,0:T(8,128)(2,1)}, bf16[6,64,768]{2,1,0:T(8,128)(2,1)}, u32[]{:S(2)}, u32[]{:S(2)}) collective-permute-start(bf16[6,64,768]{2,1,0:T(8,128)(2,1)} %single_ref.1), channel_id=1, source_target_pairs={{0,8},{8,0},{16,24},{24,16},{32,40},{40,32},{48,56},{56,48},{64,72... | collective-permute-start | bytes 1769480 | tf_op jit(solution)/shard_map/ppermute | solution.py:251
  2.1 14.2 %collective-permute-start.1 = (bf16[6,64,768]{2,1,0:T(8,128)(2,1)}, bf16[6,64,768]{2,1,0:T(8,128)(2,1)}, u32[]{:S(2)}, u32[]{:S(2)}) collective-permute-start(bf16[6,64,768]{2,1,0:T(8,128)(2,1)} %cot_ref.1), channel_id=1, source_target_pairs={{0,8},{8,0},{16,24},{24,16},{32,40},{40,32},{48,56},{56,48},{64,72... | collective-permute-start | bytes 1769480 | tf_op jit(solution)/shard_map/ppermute | solution.py:252
  4.6 11.7 %copy-start.4 = (bf16[6,64,768]{2,1,0:T(8,128)(2,1)S(1)}, bf16[6,64,768]{2,1,0:T(8,128)(2,1)}, u32[]{:S(2)}) copy-start(bf16[6,64,768]{2,1,0:T(8,128)(2,1)} %single_ref.1) | copy-start | bytes 1769476
  4.6 11.7 %copy-start.5 = (bf16[6,64,768]{2,1,0:T(8,128)(2,1)S(1)}, bf16[6,64,768]{2,1,0:T(8,128)(2,1)}, u32[]{:S(2)}) copy-start(bf16[6,64,768]{2,1,0:T(8,128)(2,1)} %cot_ref.1) | copy-start | bytes 1769476
  8.1 17.2 %all-to-all-start.1 = ((bf16[16,64,128]{2,1,0:T(8,128)(2,1)}), bf16[16,64,128]{2,1,0:T(8,128)(2,1)}, u32[]{:S(2)}, u32[]{:S(2)}) async-start(bf16[16,64,128]{2,1,0:T(8,128)(2,1)} %shard_map.96), calls=%async_computation.1 | async-start | bytes 524288 | tf_op jit(solution)/shard_map/all_to_all | solution.py:253
  25.3 54.5 %all-to-all-start = ((bf16[16,192,384]{2,1,0:T(8,128)(2,1)}), bf16[16,192,384]{2,1,0:T(8,128)(2,1)}, u32[]{:S(2)}, u32[]{:S(2)}) async-start(bf16[16,192,384]{2,1,0:T(8,128)(2,1)} %copy-done.3), calls=%async_computation | async-start | bytes 4718592 | tf_op jit(solution)/shard_map/all_to_all | solution.py:261
  32.5 29.8 %collective-permute-start.5 = (bf16[1024,128]{1,0:T(8,128)(2,1)}, bf16[1024,128]{1,0:T(8,128)(2,1)S(1)}, u32[]{:S(2)}, u32[]{:S(2)}) collective-permute-start(bf16[1024,128]{1,0:T(8,128)(2,1)} %bitcast.5.refs_0_), channel_id=1, source_target_pairs={{0,4},{1,5},{2,6},{3,7},{4,0},{5,1},{6,2},{7,3},{8,12},{9,13},{10,... | collective-permute-start | bytes 786440 | tf_op jit(solution)/shard_map/ppermute | solution.py:257
  33.2 33.0 %collective-permute-start.2 = (bf16[1024,128]{1,0:T(8,128)(2,1)}, bf16[1024,128]{1,0:T(8,128)(2,1)S(1)}, u32[]{:S(2)}, u32[]{:S(2)}) collective-permute-start(bf16[1024,128]{1,0:T(8,128)(2,1)} %bitcast.5.refs_0_), channel_id=1, source_target_pairs={{0,1},{1,0},{2,3},{3,2},{4,5},{5,4},{6,7},{7,6},{8,9},{9,8},{10,11... | collective-permute-start | bytes 786440 | tf_op jit(solution)/shard_map/ppermute | solution.py:258
  34.5 31.7 %collective-permute-start.3 = (bf16[1024,128]{1,0:T(8,128)(2,1)}, bf16[1024,128]{1,0:T(8,128)(2,1)S(1)}, u32[]{:S(2)}, u32[]{:S(2)}) collective-permute-start(bf16[1024,128]{1,0:T(8,128)(2,1)} %bitcast.5.refs_0_), channel_id=1, source_target_pairs={{0,2},{1,3},{2,0},{3,1},{4,6},{5,7},{6,4},{7,5},{8,10},{9,11},{10,... | collective-permute-start | bytes 786440 | tf_op jit(solution)/shard_map/ppermute | solution.py:258
  37.1 29.1 %collective-permute-start.4 = (bf16[1024,128]{1,0:T(8,128)(2,1)}, bf16[1024,128]{1,0:T(8,128)(2,1)S(1)}, u32[]{:S(2)}, u32[]{:S(2)}) collective-permute-start(bf16[1024,128]{1,0:T(8,128)(2,1)} %bitcast.5.refs_0_), channel_id=1, source_target_pairs={{0,3},{1,2},{2,1},{3,0},{4,7},{5,6},{6,5},{7,4},{8,11},{9,10},{10,... | collective-permute-start | bytes 786440 | tf_op jit(solution)/shard_map/ppermute | solution.py:258
  62.2 17.6 %copy-start.11 = (bf16[1024,128]{1,0:T(8,128)(2,1)}, bf16[1024,128]{1,0:T(8,128)(2,1)S(1)}, u32[]{:S(2)}) copy-start(bf16[1024,128]{1,0:T(8,128)(2,1)S(1)} %collective-permute-done.5.refs_4_) | copy-start | bytes 786436
  62.3 7.4 %collective-permute-start.6 = (bf16[1024,128]{1,0:T(8,128)(2,1)S(1)}, bf16[1024,128]{1,0:T(8,128)(2,1)}, u32[]{:S(2)}, u32[]{:S(2)}) collective-permute-start(bf16[1024,128]{1,0:T(8,128)(2,1)S(1)} %collective-permute-done.5.refs_4_), channel_id=1, source_target_pairs={{0,1},{1,0},{2,3},{3,2},{4,5},{5,4},{6,7},{7,6},{8,9},{9,8},{10,11... | collective-permute-start | bytes 786440 | tf_op jit(solution)/shard_map/ppermute | solution.py:259
  63.5 14.3 %collective-permute-start.7 = (bf16[1024,128]{1,0:T(8,128)(2,1)S(1)}, bf16[1024,128]{1,0:T(8,128)(2,1)}, u32[]{:S(2)}, u32[]{:S(2)}) collective-permute-start(bf16[1024,128]{1,0:T(8,128)(2,1)S(1)} %collective-permute-done.5.refs_4_), channel_id=1, source_target_pairs={{0,2},{1,3},{2,0},{3,1},{4,6},{5,7},{6,4},{7,5},{8,10},{9,11},{10,... | collective-permute-start | bytes 786440 | tf_op jit(solution)/shard_map/ppermute | solution.py:259
  66.2 13.7 %copy-start.12 = (bf16[1024,128]{1,0:T(8,128)(2,1)}, bf16[1024,128]{1,0:T(8,128)(2,1)S(1)}, u32[]{:S(2)}) copy-start(bf16[1024,128]{1,0:T(8,128)(2,1)S(1)} %collective-permute-done.2.refs_1_) | copy-start | bytes 786436
  66.2 13.6 %collective-permute-start.8 = (bf16[1024,128]{1,0:T(8,128)(2,1)S(1)}, bf16[1024,128]{1,0:T(8,128)(2,1)}, u32[]{:S(2)}, u32[]{:S(2)}) collective-permute-start(bf16[1024,128]{1,0:T(8,128)(2,1)S(1)} %collective-permute-done.5.refs_4_), channel_id=1, source_target_pairs={{0,3},{1,2},{2,1},{3,0},{4,7},{5,6},{6,5},{7,4},{8,11},{9,10},{10,... | collective-permute-start | bytes 786440 | tf_op jit(solution)/shard_map/ppermute | solution.py:259
  66.2 13.6 %copy-start.13 = (bf16[1024,128]{1,0:T(8,128)(2,1)}, bf16[1024,128]{1,0:T(8,128)(2,1)S(1)}, u32[]{:S(2)}) copy-start(bf16[1024,128]{1,0:T(8,128)(2,1)S(1)} %collective-permute-done.3.refs_2_) | copy-start | bytes 786436
  66.2 13.6 %copy-start.14 = (bf16[1024,128]{1,0:T(8,128)(2,1)}, bf16[1024,128]{1,0:T(8,128)(2,1)S(1)}, u32[]{:S(2)}) copy-start(bf16[1024,128]{1,0:T(8,128)(2,1)S(1)} %collective-permute-done.4.refs_3_) | copy-start | bytes 786436
  103.4 42.7 %copy-start.7 = (bf16[3,128,768]{2,1,0:T(8,128)(2,1)S(1)}, bf16[3,128,768]{2,1,0:T(8,128)(2,1)}, u32[]{:S(2)}) copy-start(bf16[3,128,768]{2,1,0:T(8,128)(2,1)} %copy-done.6) | copy-start | bytes 1769476
  103.4 18.4 %collective-permute-start.15 = (bf16[1024,128]{1,0:T(8,128)(2,1)}, bf16[1024,128]{1,0:T(8,128)(2,1)}, u32[]{:S(2)}, u32[]{:S(2)}) collective-permute-start(bf16[1024,128]{1,0:T(8,128)(2,1)} %get-tuple-element.27), channel_id=1, source_target_pairs={{0,7},{1,6},{2,5},{3,4},{4,3},{5,2},{6,1},{7,0},{8,15},{9,14},{10,... | collective-permute-start | bytes 786440 | tf_op jit(solution)/shard_map/ppermute | solution.py:265
  104.0 18.6 %collective-permute-start.14 = (bf16[1024,128]{1,0:T(8,128)(2,1)}, bf16[1024,128]{1,0:T(8,128)(2,1)}, u32[]{:S(2)}, u32[]{:S(2)}) collective-permute-start(bf16[1024,128]{1,0:T(8,128)(2,1)} %get-tuple-element.26), channel_id=1, source_target_pairs={{0,6},{1,7},{2,4},{3,5},{4,2},{5,3},{6,0},{7,1},{8,14},{9,15},{10,... | collective-permute-start | bytes 786440 | tf_op jit(solution)/shard_map/ppermute | solution.py:265
  104.0 42.0 %all-to-all-start.2 = ((bf16[16,48,384]{2,1,0:T(8,128)(2,1)}), bf16[16,48,384]{2,1,0:T(8,128)(2,1)S(1)}, u32[]{:S(2)}, u32[]{:S(2)}) async-start(bf16[16,48,384]{2,1,0:T(8,128)(2,1)} %bitcast.21), calls=%async_computation.2 | async-start | bytes 1179648 | tf_op jit(solution)/shard_map/all_to_all | solution.py:267
  117.8 13.6 %collective-permute-start.13 = (bf16[1024,128]{1,0:T(8,128)(2,1)}, bf16[1024,128]{1,0:T(8,128)(2,1)}, u32[]{:S(2)}, u32[]{:S(2)}) collective-permute-start(bf16[1024,128]{1,0:T(8,128)(2,1)} %get-tuple-element.25), channel_id=1, source_target_pairs={{0,5},{1,4},{2,7},{3,6},{4,1},{5,0},{6,3},{7,2},{8,13},{9,12},{10,... | collective-permute-start | bytes 786440 | tf_op jit(solution)/shard_map/ppermute | solution.py:265
  119.8 17.6 %collective-permute-start.12 = (bf16[1024,128]{1,0:T(8,128)(2,1)}, bf16[1024,128]{1,0:T(8,128)(2,1)}, u32[]{:S(2)}, u32[]{:S(2)}) collective-permute-start(bf16[1024,128]{1,0:T(8,128)(2,1)} %get-tuple-element.24), channel_id=1, source_target_pairs={{0,4},{1,5},{2,6},{3,7},{4,0},{5,1},{6,2},{7,3},{8,12},{9,13},{10,... | collective-permute-start | bytes 786440 | tf_op jit(solution)/shard_map/ppermute | solution.py:265
  121.8 15.7 %collective-permute-start.11 = (bf16[1024,128]{1,0:T(8,128)(2,1)}, bf16[1024,128]{1,0:T(8,128)(2,1)}, u32[]{:S(2)}, u32[]{:S(2)}) collective-permute-start(bf16[1024,128]{1,0:T(8,128)(2,1)} %get-tuple-element.23), channel_id=1, source_target_pairs={{0,3},{1,2},{2,1},{3,0},{4,7},{5,6},{6,5},{7,4},{8,11},{9,10},{10,... | collective-permute-start | bytes 786440 | tf_op jit(solution)/shard_map/ppermute | solution.py:265
  121.8 15.7 %collective-permute-start.10 = (bf16[1024,128]{1,0:T(8,128)(2,1)}, bf16[1024,128]{1,0:T(8,128)(2,1)}, u32[]{:S(2)}, u32[]{:S(2)}) collective-permute-start(bf16[1024,128]{1,0:T(8,128)(2,1)} %get-tuple-element.22), channel_id=1, source_target_pairs={{0,2},{1,3},{2,0},{3,1},{4,6},{5,7},{6,4},{7,5},{8,10},{9,11},{10,... | collective-permute-start | bytes 786440 | tf_op jit(solution)/shard_map/ppermute | solution.py:265
  122.6 20.9 %collective-permute-start.9 = (bf16[1024,128]{1,0:T(8,128)(2,1)}, bf16[1024,128]{1,0:T(8,128)(2,1)}, u32[]{:S(2)}, u32[]{:S(2)}) collective-permute-start(bf16[1024,128]{1,0:T(8,128)(2,1)} %get-tuple-element.21), channel_id=1, source_target_pairs={{0,1},{1,0},{2,3},{3,2},{4,5},{5,4},{6,7},{7,6},{8,9},{9,8},{10,11... | collective-permute-start | bytes 786440 | tf_op jit(solution)/shard_map/ppermute | solution.py:265
  149.3 16.7 %all-to-all-start.3 = ((bf16[16,64,128]{2,1,0:T(8,128)(2,1)}), bf16[16,64,128]{2,1,0:T(8,128)(2,1)S(1)}, u32[]{:S(2)}, u32[]{:S(2)}) async-start(bf16[16,64,128]{2,1,0:T(8,128)(2,1)} %bitcast.20), calls=%async_computation.3 | async-start | bytes 524288 | tf_op jit(solution)/shard_map/all_to_all | solution.py:274
  157.1 4.9 %copy-start.10 = (f32[384,768]{1,0:T(8,128)S(1)}, f32[384,768]{1,0:T(8,128)}, u32[]{:S(2)}) copy-start(f32[384,768]{1,0:T(8,128)} %copy-done.9) | copy-start | bytes 3538948
  162.0 4.5 %copy-start.8 = (bf16[128,16]{0,1:T(8,128)(2,1)S(1)}, bf16[128,16]{0,1:T(8,128)(2,1)}, u32[]{:S(2)}) copy-start(bf16[128,16]{0,1:T(8,128)(2,1)} %param.9) | copy-start | bytes 12292
  166.1 8.5 %collective-permute-start.16 = (bf16[3,64,768]{2,1,0:T(8,128)(2,1)S(1)}, bf16[3,64,768]{2,1,0:T(8,128)(2,1)}, u32[]{:S(2)}, u32[]{:S(2)}) collective-permute-start(bf16[3,64,768]{2,1,0:T(8,128)(2,1)S(1)} %constant_dynamic-slice_fusion), channel_id=1, source_target_pairs={{0,8},{8,0},{16,24},{24,16},{32,40},{40,32},{48,56},{56,48},{64,72... | collective-permute-start | bytes 884744 | tf_op jit(solution)/shard_map/ppermute | solution.py:283
  166.5 1.6 copy-start.2
  (4 other events, 4.8 us)

commit v3 on v2

--- a/solution.py
+++ b/solution.py
@@ -22,50 +22,58 @@
 
 def pair_kernel(pair_ref, w_ref, out_ref):
     rows, cols, chans = pair_ref.shape
-    heads = w_ref.shape[0]
+    heads = w_ref.shape[1]
     normed, _ = unit(pair_ref[...].astype(F32).reshape(rows * cols, chans))
     high = normed.astype(BF)
     low = (normed - high.astype(F32)).astype(BF)
+    weight = w_ref[...].astype(F32).T.astype(BF)
     both = jnp.concatenate([high, low], axis=1)
-    flat = lax.dot_general(w_ref[...], both, (((1,), (1,)), ((), ())), preferred_element_type=F32)
+    weight = jnp.concatenate([weight, weight], axis=1)
+    flat = lax.dot_general(weight, both, (((1,), (1,)), ((), ())), preferred_element_type=F32)
     out_ref[...] = flat.reshape(heads, rows, cols).astype(BF)
 
 def pair_bias(pair, bias_weight, step=16):
     rows, cols, chans = pair.shape
     heads = bias_weight.shape[1]
-    w = bias_weight.T
-    w = jnp.concatenate([w, w], axis=1)
     return pl.pallas_call(
         pair_kernel, grid=(rows // step,),
         in_specs=[pl.BlockSpec((step, cols, chans), lambda i: (i, 0, 0)),
-                  pl.BlockSpec((heads, 2 * chans), lambda i: (0, 0))],
+                  pl.BlockSpec((chans, heads), lambda i: (0, 0))],
         out_specs=pl.BlockSpec((heads, step, cols), lambda i: (0, i, 0)),
         out_shape=jax.ShapeDtypeStruct((heads, rows, cols), BF),
-        compiler_params=pltpu.CompilerParams(dimension_semantics=("arbitrary",), vmem_limit_bytes=48 << 20),
-    )(pair, w)
+        compiler_params=pltpu.CompilerParams(dimension_semantics=("arbitrary",), vmem_limit_bytes=60 << 20),
+    )(pair, bias_weight)
 
 def back_kernel(pair_ref, grad_ref, w_ref, out_ref):
     rows, cols, chans = pair_ref.shape
-    heads = w_ref.shape[0]
+    heads, parts = grad_ref.shape[:2]
     normed, scaled = unit(pair_ref[...].astype(F32).reshape(rows * cols, chans))
-    grad = grad_ref[...].reshape(heads, rows * cols)
-    normed_grad = lax.dot_general(grad, w_ref[...], (((0,), (0,)), ((), ())), preferred_element_type=F32)
+    grad = grad_ref[:, 0].astype(F32)
+    for g in range(1, parts):
+        grad = grad + grad_ref[:, g].astype(F32)
+    grad = grad.reshape(heads, rows * cols)
+    high = grad.astype(BF)
+    low = (grad - high.astype(F32)).astype(BF)
+    weight = w_ref[...].astype(F32).T.astype(BF)
+    both = jnp.concatenate([high, low], axis=0)
+    weight = jnp.concatenate([weight, weight], axis=0)
+    normed_grad = lax.dot_general(both, weight, (((0,), (0,)), ((), ())), preferred_element_type=F32)
     centred = normed_grad - jnp.mean(normed_grad, axis=-1, keepdims=True)
     along = jnp.mean(normed_grad * normed, axis=-1, keepdims=True)
     out_ref[...] = ((centred - normed * along) * scaled).reshape(rows, cols, chans)
 
 def pair_back(pair, grad, bias_weight, step=16):
     rows, cols, chans = pair.shape
-    heads = bias_weight.shape[1]
+    heads, parts = grad.shape[:2]
     return pl.pallas_call(
         back_kernel, grid=(rows // step,),
         in_specs=[pl.BlockSpec((step, cols, chans), lambda i: (i, 0, 0)),
-                  pl.BlockSpec((heads, step, cols), lambda i: (0, i, 0)),
-                  pl.BlockSpec((heads, chans), lambda i: (0, 0))],
+                  pl.BlockSpec((heads, parts, step, cols), lambda i: (0, 0, i, 0)),
+                  pl.BlockSpec((chans, heads), lambda i: (0, 0))],
         out_specs=pl.BlockSpec((step, cols, chans), lambda i: (i, 0, 0)),
         out_shape=jax.ShapeDtypeStruct((rows, cols, chans), F32),
-        compiler_params=pltpu.CompilerParams(dimension_semantics=("arbitrary",), vmem_limit_bytes=48 << 20),
-    )(pair, grad, bias_weight.T)
+        compiler_params=pltpu.CompilerParams(dimension_semantics=("arbitrary",), vmem_limit_bytes=60 << 20),
+    )(pair, grad, bias_weight)
 
 def project_kernel(core_ref, single_ref, got_ref, cot_ref, gotc_ref, w_ref, packed_ref, tokens_ref, normed, cotan):
     half, block, width = tokens_ref.shape
@@ -113,15 +121,16 @@
             scratch_shapes=[pltpu.VMEM((lanes, width), BF), pltpu.VMEM((half, block, width), BF)],
         ),
         out_shape=[jax.ShapeDtypeStruct((heads, 4 * size, lanes), BF), jax.ShapeDtypeStruct((half, block, width), BF)],
-        compiler_params=pltpu.CompilerParams(dimension_semantics=("arbitrary",), vmem_limit_bytes=48 << 20),
+        compiler_params=pltpu.CompilerParams(dimension_semantics=("arbitrary",), vmem_limit_bytes=60 << 20),
     )(core, single, got, cot, gotc, w_qkv)
 
 
 def attend_kernel(n_col, n_chip, n_samp, size, span, unroll, c_ref, blk_ref, *refs):
-    bias_refs = refs[:n_col]
-    att_ref = refs[n_col]
-    out_refs = refs[n_col + 1 : 2 * n_col + 1]
-    bias2, acc, kt, vt = refs[2 * n_col + 1 :]
+    bias_refs = refs[: n_col // 2]
+    att_ref = refs[n_col // 2]
+    out_refs = refs[n_col // 2 + 1 : n_col + 1]
+    bias2, acc, kt, vt = refs[n_col + 1 :]
+    half_rows = bias_refs[0].shape[1] // 2
     samp = pl.program_id(0)
     me = c_ref[0]
     block = blk_ref.shape[2]
@@ -130,7 +139,10 @@
     @pl.when(samp == 0)
     def _():
         for k in range(n_col):
-            bias2[:, k * block : (k + 1) * block] = bias_refs[k][...].astype(F32) * LOG2E
+            far = k // (n_col // 2)
+            part = bias_refs[k % (n_col // 2)][:, far * half_rows : (far + 1) * half_rows, :]
+            part = part.astype(F32).reshape(bias2.shape[0], block)
+            bias2[:, k * block : (k + 1) * block] = part * LOG2E
         acc[...] = jnp.zeros_like(acc)
         rest = block - 2 * size
         kt[2 * size :, :] = jnp.zeros((rest, wide), BF)
@@ -190,25 +202,30 @@
     @pl.when(samp == n_samp - 1)
     def _():
         for k in range(n_col):
-            out_refs[k][...] = acc[:, k * block : (k + 1) * block].astype(BF)
+            part = acc[:, k * block : (k + 1) * block].astype(BF)
+            out_ref = out_refs[k % (n_col // 2)]
+            far = jnp.bitwise_xor(me // (n_col // 2), k // (n_col // 2))
+            out_ref[:, far] = part.reshape(out_ref.shape[0], half_rows, block)
 
 
 def attend(me, qkvc, biases, n_samp, size, span=1, unroll=1):
     n_chip, _, _, lanes = qkvc.shape
     per = n_samp // 2
     block = lanes // per
-    n_col = len(biases)
+    n_col = 2 * len(biases)
+    n_row, both_rows, _ = biases[0].shape
     tokens = n_chip * block
     wide = n_col * block
-    whole = pl.BlockSpec((tokens, block), lambda s, c: (0, 0))
+    whole = pl.BlockSpec((n_row, both_rows, block), lambda s, c: (0, 0, 0))
+    parts = (n_row, 2, both_rows // 2, block)
     spec = lambda feats: pl.BlockSpec((n_chip, None, feats, block), lambda s, c: (0, s // per, 0, s % per))
     return pl.pallas_call(
         functools.partial(attend_kernel, n_col, n_chip, n_samp, size, span, unroll),
         grid_spec=pltpu.PrefetchScalarGridSpec(
             num_scalar_prefetch=1,
             grid=(n_samp,),
-            in_specs=[spec(4 * size)] + [whole] * n_col,
-            out_specs=[spec(size)] + [whole] * n_col,
+            in_specs=[spec(4 * size)] + [whole] * len(biases),
+            out_specs=[spec(size)] + [pl.BlockSpec(parts, lambda s, c: (0, 0, 0, 0))] * len(biases),
             scratch_shapes=[
                 pltpu.VMEM((tokens, wide), F32),
                 pltpu.VMEM((tokens, wide), F32),
@@ -217,7 +234,7 @@
             ],
         ),
         out_shape=[jax.ShapeDtypeStruct((n_chip, 2, size, lanes), BF)]
-        + [jax.ShapeDtypeStruct((tokens, block), BF)] * n_col,
+        + [jax.ShapeDtypeStruct(parts, BF)] * len(biases),
         compiler_params=pltpu.CompilerParams(
             dimension_semantics=("arbitrary",), vmem_limit_bytes=56 * 1024 * 1024
         ),
@@ -250,39 +267,38 @@
 
     got = lax.ppermute(single, "row", cores)
     got_cot = lax.ppermute(cotangent, "row", cores)
-    bias = lax.all_to_all(pair_bias(pair, bias_weight, 32), "row", 0, 0, tiled=True)
-    bias = bias.reshape(n_row * rows, pair.shape[1])
+    bias = pair_bias(pair, bias_weight, 16)
+    bias, got, got_cot = lax.optimization_barrier((bias, got, got_cot))
+    far = lax.ppermute(bias, "col", flip(n_col // 2))
     packed, tokens = project(core.reshape(1), single, got, cotangent, got_cot, w_qkv, heads)
-
-    far = lax.ppermute(bias, "col", flip(n_col // 2))
+    bias = lax.all_to_all(jnp.concatenate([bias, far], axis=1), "row", 0, 0, tiled=True)
     biases = [bias] + [lax.ppermute(bias, "col", flip(k)) for k in range(1, n_col // 2)]
-    biases += [far] + [lax.ppermute(far, "col", flip(k)) for k in range(1, n_col // 2)]
 
     packed = lax.all_to_all(packed, "row", 0, 0, tiled=True)
     packed = packed.reshape(n_chip, 2, 4 * size, half * block)
     attended, *grads = attend(me, packed, biases, samp, size, n_chip)
-
-    grads = [grads[0]] + [lax.ppermute(grads[k], "col", flip(k)) for k in range(1, n_col)]
+    grads = [grads[0]] + [lax.ppermute(grads[k], "col", flip(k)) for k in range(1, n_col // 2)]
     attended = attended.reshape(n_row, size, half * block)
     attended = lax.all_to_all(attended, "row", 0, 0, tiled=True)
-
-    bias_grad = grads[0].astype(F32)
-    for k in range(1, n_col):
-        bias_grad = bias_grad + grads[k].astype(F32)
-    attended, bias_grad = lax.optimization_barrier((attended, bias_grad.astype(BF)))
-    bias_grad = bias_grad.reshape(n_row, rows, pair.shape[1])
-    bias_grad = lax.all_to_all(bias_grad, "row", 0, 0, tiled=True)
+    total = grads[0].astype(F32)
+    for part in grads[1:]:
+        total = total + part.astype(F32)
+    attended, total = lax.optimization_barrier((attended, total.astype(BF)))
+    total = total.reshape(2 * n_row, rows, pair.shape[1])
+    groups = [[r * n_col + z * (n_col // 2) + y for r in range(n_row) for z in range(2)] for y in range(n_col // 2)]
+    total = lax.all_to_all(total, ("row", "col"), 0, 0, tiled=True, axis_index_groups=groups)
+    total = total.reshape(n_row, 2, rows, pair.shape[1])
 
     updated = transition(
         tokens.reshape(half * block, width), attended.reshape(width, half * block), w_out, w_gate_up, w_down
     )
-    updated, bias_grad = lax.optimization_barrier((updated, bias_grad))
+    updated, total = lax.optimization_barrier((updated, total))
     updated = updated.reshape(half, block, width)
     mine = lax.dynamic_slice_in_dim(updated, core * rows, rows, 1)
     theirs = lax.dynamic_slice_in_dim(updated, (1 - core) * rows, rows, 1)
     got = lax.ppermute(theirs, "row", cores)
     updated = jnp.concatenate([jnp.where(core == 0, mine, got), jnp.where(core == 0, got, mine)], axis=0)
-    pair_grad = pair_back(pair, bias_grad, bias_weight, 16)
+    pair_grad = pair_back(pair, total, bias_weight, 16)
     return (updated, pair_grad)
 
 

time: 177 us -> 165 us (0.932)
  starting transfers between devices: 55.4 us -> 42 us
  Pallas kernels: 40.2 us -> 45.2 us
  local copies, waits for them, and re-layouts: 6.46 us -> 3.22 us
    ppermute x3, waiting for transfers between devices: 0.01 us -> 25.1 us  [shards(): lax.ppermute(bias, 'col', flip(k))]
    ppermute x1, waiting for transfers between devices: 25.1 us -> 6.38 us  [shards(): far = lax.ppermute(bias, 'col', flip(n_col // 2))]
    ppermute x3 -> x0, waiting for transfers between devices: 13.6 us -> none  [shards(): lax.ppermute(far, 'col', flip(k))]
    all_to_all x1, starting transfers between devices: 13.8 us -> 7.07 us  [shards(): attended = lax.all_to_all(attended, 'row', 0, 0, tiled=True)]
    all_to_all x2, waiting for transfers between devices: 2.68 us -> 7.02 us  [the longest x1 4.51 us: shards(): lax.all_to_all(total, ('row', 'col'), 0, 0, tiled=True, axis_index_groups...]
    unnamed x30 -> x13, local copies, waits for them, and re-layouts: 6.44 us -> 2.24 us
    ppermute x7 -> x3, starting transfers between devices: 7.88 us -> 3.92 us  [shards(): lax.ppermute(grads[k], 'col', flip(k))]
    ppermute x3 -> x0, starting transfers between devices: 3.92 us -> none  [shards(): lax.ppermute(far, 'col', flip(k))]
  transfers between devices with their start and end apart: 21 -> 14, of which waited for: 9 -> 10; matrix products, arithmetic and copies ran while one was open for 5% -> 6% of each run, Pallas kernels for 9% -> 13%
where the time goes in v3:
time: 165 us; the launch traced here: 164 us
  waiting for transfers between devices  58.6 us (36%)
  Pallas kernels  45.2 us (27%)
  starting transfers between devices  42 us (25%)
  matrix products  8.95 us (5%)
  other arithmetic  5.57 us (3%)
  local copies, waits for them, and re-layouts  3.22 us (2%)
    ppermute x3, waiting for transfers between devices, shards(): lax.ppermute(bias, 'col', flip(k))  25.1 us
    pallas_call x1, Pallas kernels, attend(): pl.pallas_call(functools.partial(attend_kernel, n_col, n_chip, n_samp, si...  23.4 us
    ppermute x3, waiting for transfers between devices, shards(): lax.ppermute(grads[k], 'col', flip(k))  17.6 us
    all_to_all x1, starting transfers between devices, shards(): lax.all_to_all(total, ('row', 'col'), 0, 0, tiled=True, axis_index_groups...  8.67 us
    pallas_call x1, Pallas kernels, project(): pl.pallas_call(project_kernel, grid_spec=pltpu.PrefetchScalarGridSpec(num...  8.62 us
    all_to_all x1, starting transfers between devices, shards(): lax.all_to_all(jnp.concatenate([bias, far], axis=1), 'row', 0, 0, tiled=T...  8.53 us
    pallas_call x1, Pallas kernels, pair_back(): pl.pallas_call(back_kernel, grid=(rows // step,), in_specs=[pl.BlockSpec(...  7.72 us
    all_to_all x1, starting transfers between devices, shards(): attended = lax.all_to_all(attended, 'row', 0, 0, tiled=True)  7.07 us
  transfers between devices with their start and end apart: 14, of which 10 were waited for; matrix products, arithmetic and copies ran while one was open for 6% of the time, Pallas kernels for 13%

profile of v3, /device:TPU:1, one launch (start us, length us, event | category | flops | bytes accessed | tf_op | source)
XLA Modules:
  0.0 164.2 jit_solution(5806406988994247925)
XLA Ops:
  0.6 1.5 collective-permute-start
  2.2 1.4 copy.10.w_ref
  3.6 5.5 %shard_map.95 = bf16[16,64,128]{2,1,0:T(8,128)(2,1)} custom-call(bf16[64,128,128]{2,1,0:T(8,128)(2,1)} %pair_ref.3, bf16[128,16]{1,0:T(8,128)(2,1)} %copy.10.w_ref), custom_call_target="tpu_custom_call" | custom-call | tf_op jit(solution)/shard_map/pallas_call | solution.py:38
  9.1 1.8 %collective-permute-start.2 = (bf16[16,64,128]{2,1,0:T(8,128)(2,1)}, bf16[16,64,128]{2,1,0:T(8,128)(2,1)S(1)}, u32[]{:S(2)}, u32[]{:S(2)}) collective-permute-start(bf16[16,64,128]{2,1,0:T(8,128)(2,1)} %shard_map.95), channel_id=1, source_target_pairs={{0,4},{1,5},{2,6},{3,7},{4,0},{5,1},{6,2},{7,3},{8,12},{9,13},{10,... | collective-permute-start | bytes 786440 | tf_op jit(solution)/shard_map/ppermute | solution.py:272
  10.9 6.4 %collective-permute-done.2 = bf16[16,64,128]{2,1,0:T(8,128)(2,1)S(1)} collective-permute-done((bf16[16,64,128]{2,1,0:T(8,128)(2,1)}, bf16[16,64,128]{2,1,0:T(8,128)(2,1)S(1)}, u32[]{:S(2)}, u32[]{:S(2)}) %collective-permute-start.2) | collective-permute-done | bytes 262176 | tf_op jit(solution)/shard_map/ppermute | solution.py:272
  17.3 1.8 %pad_maximum_fusion.1 = bf16[16,128,128]{2,1,0:T(8,128)(2,1)} fusion(bf16[16,64,128]{2,1,0:T(8,128)(2,1)S(1)} %collective-permute-done.2, bf16[16,64,128]{2,1,0:T(8,128)(2,1)} %shard_map.95), kind=kLoop, calls=%fused_computation.12 | loop fusion | flops 1048576 | bytes 1048576 | tf_op jit(solution)/shard_map/concatenate | solution.py:274
  19.1 8.5 %all-to-all-start.1 = ((bf16[16,128,128]{2,1,0:T(8,128)(2,1)}), bf16[16,128,128]{2,1,0:T(8,128)(2,1)S(1)}, u32[]{:S(2)}, u32[]{:S(2)}) async-start(bf16[16,128,128]{2,1,0:T(8,128)(2,1)} %pad_maximum_fusion.1), calls=%async_computation.1 | async-start | bytes 1048576 | tf_op jit(solution)/shard_map/all_to_all | solution.py:274
  27.6 8.6 %shard_map.96 = (bf16[16,192,384]{2,1,0:T(8,128)(2,1)}, bf16[3,128,768]{2,1,0:T(8,128)(2,1)}) custom-call(s32[1]{0:T(128)} %bitcast.core_ref, bf16[6,64,768]{2,1,0:T(8,128)(2,1)} %single_ref.1, bf16[6,64,768]{2,1,0:T(8,128)(2,1)} %copy-done.3, bf16[6,64,768]{2,1,0:T(8,128)(2,1)} %cot_ref.1, bf16[6,64,768]{2,1,0:T(8,128)(2,1)} %collective-permute-done.1.gotc_ref, ...), custom_call_target="tpu_custom_call" | custom-call | tf_op jit(solution)/shard_map/pallas_call | solution.py:114
  36.3 2.5 %all-to-all-done.1.refs_0_ = bf16[16,128,128]{2,1,0:T(8,128)(2,1)S(1)} async-done(((bf16[16,128,128]{2,1,0:T(8,128)(2,1)}), bf16[16,128,128]{2,1,0:T(8,128)(2,1)S(1)}, u32[]{:S(2)}, u32[]{:S(2)}) %all-to-all-start.1) | async-done | bytes 524320 | tf_op jit(solution)/shard_map/all_to_all | solution.py:274
  38.8 5.5 %all-to-all-start = ((bf16[16,192,384]{2,1,0:T(8,128)(2,1)}), bf16[16,192,384]{2,1,0:T(8,128)(2,1)}, u32[]{:S(2)}, u32[]{:S(2)}) async-start(bf16[16,192,384]{2,1,0:T(8,128)(2,1)} %get-tuple-element.19), calls=%async_computation | async-start | bytes 4718592 | tf_op jit(solution)/shard_map/all_to_all | solution.py:277
  44.3 1.3 collective-permute-start.3
  45.6 2.6 %collective-permute-start.4 = (bf16[16,128,128]{2,1,0:T(8,128)(2,1)S(1)}, bf16[16,128,128]{2,1,0:T(8,128)(2,1)}, u32[]{:S(2)}, u32[]{:S(2)}) collective-permute-start(bf16[16,128,128]{2,1,0:T(8,128)(2,1)S(1)} %all-to-all-done.1.refs_0_), channel_id=1, source_target_pairs={{0,2},{1,3},{2,0},{3,1},{4,6},{5,7},{6,4},{7,5},{8,10},{9,11},{10,... | collective-permute-start | bytes 1572872 | tf_op jit(solution)/shard_map/ppermute | solution.py:275
  48.2 9.3 %collective-permute-done.3.refs_1_ = bf16[16,128,128]{2,1,0:T(8,128)(2,1)S(1)} collective-permute-done((bf16[16,128,128]{2,1,0:T(8,128)(2,1)S(1)}, bf16[16,128,128]{2,1,0:T(8,128)(2,1)S(1)}, u32[]{:S(2)}, u32[]{:S(2)}) %collective-permute-start.3) | collective-permute-done | bytes 524320 | tf_op jit(solution)/shard_map/ppermute | solution.py:275
  57.5 13.7 %collective-permute-done.4.refs_2_ = bf16[16,128,128]{2,1,0:T(8,128)(2,1)} collective-permute-done((bf16[16,128,128]{2,1,0:T(8,128)(2,1)S(1)}, bf16[16,128,128]{2,1,0:T(8,128)(2,1)}, u32[]{:S(2)}, u32[]{:S(2)}) %collective-permute-start.4) | collective-permute-done | bytes 524320 | tf_op jit(solution)/shard_map/ppermute | solution.py:275
  71.3 2.0 %collective-permute-done.5.refs_3_ = bf16[16,128,128]{2,1,0:T(8,128)(2,1)} collective-permute-done((bf16[16,128,128]{2,1,0:T(8,128)(2,1)S(1)}, bf16[16,128,128]{2,1,0:T(8,128)(2,1)}, u32[]{:S(2)}, u32[]{:S(2)}) %collective-permute-start.5) | collective-permute-done | bytes 524320 | tf_op jit(solution)/shard_map/ppermute | solution.py:275
  73.3 2.5 %all-to-all-done = bf16[16,192,384]{2,1,0:T(8,128)(2,1)} async-done(((bf16[16,192,384]{2,1,0:T(8,128)(2,1)}), bf16[16,192,384]{2,1,0:T(8,128)(2,1)}, u32[]{:S(2)}, u32[]{:S(2)}) %all-to-all-start) | async-done | bytes 2359328 | tf_op jit(solution)/shard_map/all_to_all | solution.py:277
  75.7 23.4 %shard_map.97 = (bf16[8,2,48,384]{3,2,1,0:T(8,128)(2,1)}, bf16[16,2,64,128]{3,2,1,0:T(8,128)(2,1)}, bf16[16,2,64,128]{3,2,1,0:T(8,128)(2,1)}, bf16[16,2,64,128]{3,2,1,0:T(8,128)(2,1)}, bf16[16,2,64,128]{3,2,1,0:T(8,128)(2,1)}) custom-call(s32[1]{0:T(128)} %bitcast.2.c_ref, bf16[8,2,192,384]{3,2,1,0:T(8,128)(2,1)} %bitcast.3.blk_ref, ...), custom_call_target="tpu_custom_call" | custom-call | tf_op jit(solution)/shard_map/pallas_call | solution.py:222
  99.2 1.3 collective-permute-start.6
  100.5 2.6 %collective-permute-start.7 = (bf16[16,2,64,128]{3,2,1,0:T(8,128)(2,1)}, bf16[16,2,64,128]{3,2,1,0:T(8,128)(2,1)}, u32[]{:S(2)}, u32[]{:S(2)}) collective-permute-start(bf16[16,2,64,128]{3,2,1,0:T(8,128)(2,1)} %get-tuple-element.24), channel_id=1, source_target_pairs={{0,2},{1,3},{2,0},{3,1},{4,6},{5,7},{6,4},{7,5},{8,10},{9,11},{10,... | collective-permute-start | bytes 1572872 | tf_op jit(solution)/shard_map/ppermute | solution.py:280
  103.1 7.1 %all-to-all-start.2 = ((bf16[16,48,384]{2,1,0:T(8,128)(2,1)}), bf16[16,48,384]{2,1,0:T(8,128)(2,1)S(1)}, u32[]{:S(2)}, u32[]{:S(2)}) async-start(bf16[16,48,384]{2,1,0:T(8,128)(2,1)} %bitcast.16), calls=%async_computation.2 | async-start | bytes 1179648 | tf_op jit(solution)/shard_map/all_to_all | solution.py:282
  110.1 1.8 %collective-permute-done.6 = bf16[16,2,64,128]{3,2,1,0:T(8,128)(2,1)S(1)} collective-permute-done((bf16[16,2,64,128]{3,2,1,0:T(8,128)(2,1)}, bf16[16,2,64,128]{3,2,1,0:T(8,128)(2,1)S(1)}, u32[]{:S(2)}, u32[]{:S(2)}) %collective-permute-start.6) | collective-permute-done | bytes 524320 | tf_op jit(solution)/shard_map/ppermute | solution.py:280
  112.0 13.7 %collective-permute-done.7 = bf16[16,2,64,128]{3,2,1,0:T(8,128)(2,1)} collective-permute-done((bf16[16,2,64,128]{3,2,1,0:T(8,128)(2,1)}, bf16[16,2,64,128]{3,2,1,0:T(8,128)(2,1)}, u32[]{:S(2)}, u32[]{:S(2)}) %collective-permute-start.7) | collective-permute-done | bytes 524320 | tf_op jit(solution)/shard_map/ppermute | solution.py:280
  125.7 2.1 %collective-permute-done.8 = bf16[16,2,64,128]{3,2,1,0:T(8,128)(2,1)} collective-permute-done((bf16[16,2,64,128]{3,2,1,0:T(8,128)(2,1)}, bf16[16,2,64,128]{3,2,1,0:T(8,128)(2,1)}, u32[]{:S(2)}, u32[]{:S(2)}) %collective-permute-start.8) | collective-permute-done | bytes 524320 | tf_op jit(solution)/shard_map/ppermute | solution.py:280
  127.8 2.5 %add_convert_fusion = bf16[16,2,64,128]{3,2,1,0:T(8,128)(2,1)} fusion(bf16[16,2,64,128]{3,2,1,0:T(8,128)(2,1)} %collective-permute-done.8, bf16[16,2,64,128]{3,2,1,0:T(8,128)(2,1)} %collective-permute-done.7, bf16[16,2,64,128]{3,2,1,0:T(8,128)(2,1)S(1)} %collective-permute-done.6, bf16[16,2,64,128]{3,2,1,0:T(8,128)(2,1)} %get-tuple-element.22), kind=kLoop, calls=%fused_computation.7 | loop fusion | flops 2097152 | bytes 2621440 | tf_op jit(solution)/shard_map/convert_element_type | solution.py:286
  131.1 2.3 %fusion.7 = (f32[384]{0:T(512)S(1)}, f32[384,768]{1,0:T(8,128)S(1)}) fusion(bf16[768,384]{1,0:T(8,128)(2,1)} %bitcast.14, bf16[768,768]{1,0:T(8,128)(2,1)} %param.12, bf16[384,768]{1,0:T(8,128)(2,1)} %bitcast.17), kind=kOutput, calls=%fused_computation.19 | convolution fusion | flops 453869184 | bytes 3540480 | tf_op jit(solution)/shard_map/dot_general | solution.py:245
  133.7 8.7 %all-to-all-start.3 = ((bf16[32,64,128]{2,1,0:T(8,128)(2,1)}), bf16[32,64,128]{2,1,0:T(8,128)(2,1)}, u32[]{:S(2)}, u32[]{:S(2)}) async-start(bf16[32,64,128]{2,1,0:T(8,128)(2,1)} %bitcast.15), calls=%async_computation.3 | async-start | bytes 1048576 | tf_op jit(solution)/shard_map/all_to_all | solution.py:289
  142.4 4.4 %fusion.3 = f32[384,3072]{1,0:T(8,128)S(1)} fusion(bf16[768,3072]{1,0:T(8,128)(2,1)} %param.13, f32[384,768]{1,0:T(8,128)S(1)} %get-tuple-element.33, f32[384]{0:T(512)S(1)} %add_rsqrt_fusion, f32[384]{0:T(512)S(1)} %broadcast_multiply_fusion), kind=kOutput, calls=%fused_computation.8 | convolution fusion | flops 1812824064 | bytes 10619904 | tf_op jit(solution)/shard_map/dot_general | solution.py:249
  146.8 2.2 %fusion.1 = bf16[384,768]{1,0:T(8,128)(2,1)} fusion(f32[384,768]{1,0:T(8,128)S(1)} %get-tuple-element.33, bf16[1536,768]{1,0:T(8,128)(2,1)S(1)} %copy-done, f32[384,3072]{1,0:T(8,128)S(1)} %fusion.3), kind=kOutput, calls=%fused_computation.4 | convolution fusion | flops 910098432 | bytes 8847360 | tf_op jit(solution)/shard_map/dot_general | solution.py:252
  149.0 4.5 %all-to-all-done.3 = bf16[32,64,128]{2,1,0:T(8,128)(2,1)} async-done(((bf16[32,64,128]{2,1,0:T(8,128)(2,1)}), bf16[32,64,128]{2,1,0:T(8,128)(2,1)}, u32[]{:S(2)}, u32[]{:S(2)}) %all-to-all-start.3) | async-done | bytes 524320 | tf_op jit(solution)/shard_map/all_to_all | solution.py:289
  153.5 1.0 constant_dynamic-slice_fusion
  154.5 0.9 collective-permute-start.9
  155.4 7.7 %shard_map.98 = f32[64,128,128]{2,1,0:T(8,128)} custom-call(bf16[64,128,128]{2,1,0:T(8,128)(2,1)} %pair_ref.3, bf16[16,2,64,128]{3,2,1,0:T(8,128)(2,1)} %bitcast.7.grad_ref, bf16[128,16]{1,0:T(8,128)(2,1)} %copy.10.w_ref), custom_call_target="tpu_custom_call" | custom-call | tf_op jit(solution)/shard_map/pallas_call | solution.py:68
  (24 shorter events, 2.2 us)
Async XLA Ops:
  0.6 146.1 %copy-start = (bf16[1536,768]{1,0:T(8,128)(2,1)S(1)}, bf16[1536,768]{1,0:T(8,128)(2,1)}, u32[]{:S(2)}) copy-start(bf16[1536,768]{1,0:T(8,128)(2,1)} %param.14) | copy-start | bytes 7077892
  0.6 8.5 %collective-permute-start = (bf16[6,64,768]{2,1,0:T(8,128)(2,1)}, bf16[6,64,768]{2,1,0:T(8,128)(2,1)S(1)}, u32[]{:S(2)}, u32[]{:S(2)}) collective-permute-start(bf16[6,64,768]{2,1,0:T(8,128)(2,1)} %single_ref.1), channel_id=1, source_target_pairs={{0,8},{8,0},{16,24},{24,16},{32,40},{40,32},{48,56},{56,48},{64,72... | collective-permute-start | bytes 1769480 | tf_op jit(solution)/shard_map/ppermute | solution.py:268
  2.1 7.0 %collective-permute-start.1 = (bf16[6,64,768]{2,1,0:T(8,128)(2,1)}, bf16[6,64,768]{2,1,0:T(8,128)(2,1)}, u32[]{:S(2)}, u32[]{:S(2)}) collective-permute-start(bf16[6,64,768]{2,1,0:T(8,128)(2,1)} %cot_ref.1), channel_id=1, source_target_pairs={{0,8},{8,0},{16,24},{24,16},{32,40},{40,32},{48,56},{56,48},{64,72... | collective-permute-start | bytes 1769480 | tf_op jit(solution)/shard_map/ppermute | solution.py:269
  9.1 18.5 %copy-start.3 = (bf16[6,64,768]{2,1,0:T(8,128)(2,1)}, bf16[6,64,768]{2,1,0:T(8,128)(2,1)S(1)}, u32[]{:S(2)}) copy-start(bf16[6,64,768]{2,1,0:T(8,128)(2,1)S(1)} %collective-permute-done.got_ref) | copy-start | bytes 1769476
  9.1 8.2 %collective-permute-start.2 = (bf16[16,64,128]{2,1,0:T(8,128)(2,1)}, bf16[16,64,128]{2,1,0:T(8,128)(2,1)S(1)}, u32[]{:S(2)}, u32[]{:S(2)}) collective-permute-start(bf16[16,64,128]{2,1,0:T(8,128)(2,1)} %shard_map.95), channel_id=1, source_target_pairs={{0,4},{1,5},{2,6},{3,7},{4,0},{5,1},{6,2},{7,3},{8,12},{9,13},{10,... | collective-permute-start | bytes 786440 | tf_op jit(solution)/shard_map/ppermute | solution.py:272
  19.1 19.7 %all-to-all-start.1 = ((bf16[16,128,128]{2,1,0:T(8,128)(2,1)}), bf16[16,128,128]{2,1,0:T(8,128)(2,1)S(1)}, u32[]{:S(2)}, u32[]{:S(2)}) async-start(bf16[16,128,128]{2,1,0:T(8,128)(2,1)} %pad_maximum_fusion.1), calls=%async_computation.1 | async-start | bytes 1048576 | tf_op jit(solution)/shard_map/all_to_all | solution.py:274
  38.8 9.4 %copy-start.2 = (bf16[16,128,128]{2,1,0:T(8,128)(2,1)}, bf16[16,128,128]{2,1,0:T(8,128)(2,1)S(1)}, u32[]{:S(2)}) copy-start(bf16[16,128,128]{2,1,0:T(8,128)(2,1)S(1)} %all-to-all-done.1.refs_0_) | copy-start | bytes 1572868
  38.8 36.9 %all-to-all-start = ((bf16[16,192,384]{2,1,0:T(8,128)(2,1)}), bf16[16,192,384]{2,1,0:T(8,128)(2,1)}, u32[]{:S(2)}, u32[]{:S(2)}) async-start(bf16[16,192,384]{2,1,0:T(8,128)(2,1)} %get-tuple-element.19), calls=%async_computation | async-start | bytes 4718592 | tf_op jit(solution)/shard_map/all_to_all | solution.py:277
  44.3 13.3 %collective-permute-start.3 = (bf16[16,128,128]{2,1,0:T(8,128)(2,1)S(1)}, bf16[16,128,128]{2,1,0:T(8,128)(2,1)S(1)}, u32[]{:S(2)}, u32[]{:S(2)}) collective-permute-start(bf16[16,128,128]{2,1,0:T(8,128)(2,1)S(1)} %all-to-all-done.1.refs_0_), channel_id=1, source_target_pairs={{0,1},{1,0},{2,3},{3,2},{4,5},{5,4},{6,7},{7,6},{8,9},{9,8},{10,11... | collective-permute-start | bytes 1572872 | tf_op jit(solution)/shard_map/ppermute | solution.py:275
  45.6 25.7 %collective-permute-start.4 = (bf16[16,128,128]{2,1,0:T(8,128)(2,1)S(1)}, bf16[16,128,128]{2,1,0:T(8,128)(2,1)}, u32[]{:S(2)}, u32[]{:S(2)}) collective-permute-start(bf16[16,128,128]{2,1,0:T(8,128)(2,1)S(1)} %all-to-all-done.1.refs_0_), channel_id=1, source_target_pairs={{0,2},{1,3},{2,0},{3,1},{4,6},{5,7},{6,4},{7,5},{8,10},{9,11},{10,... | collective-permute-start | bytes 1572872 | tf_op jit(solution)/shard_map/ppermute | solution.py:275
  48.2 25.1 %collective-permute-start.5 = (bf16[16,128,128]{2,1,0:T(8,128)(2,1)S(1)}, bf16[16,128,128]{2,1,0:T(8,128)(2,1)}, u32[]{:S(2)}, u32[]{:S(2)}) collective-permute-start(bf16[16,128,128]{2,1,0:T(8,128)(2,1)S(1)} %all-to-all-done.1.refs_0_), channel_id=1, source_target_pairs={{0,3},{1,2},{2,1},{3,0},{4,7},{5,6},{6,5},{7,4},{8,11},{9,10},{10,... | collective-permute-start | bytes 1572872 | tf_op jit(solution)/shard_map/ppermute | solution.py:275
  57.5 18.2 %copy-start.5 = (bf16[16,128,128]{2,1,0:T(8,128)(2,1)}, bf16[16,128,128]{2,1,0:T(8,128)(2,1)S(1)}, u32[]{:S(2)}) copy-start(bf16[16,128,128]{2,1,0:T(8,128)(2,1)S(1)} %collective-permute-done.3.refs_1_) | copy-start | bytes 1572868
  99.2 12.8 %collective-permute-start.6 = (bf16[16,2,64,128]{3,2,1,0:T(8,128)(2,1)}, bf16[16,2,64,128]{3,2,1,0:T(8,128)(2,1)S(1)}, u32[]{:S(2)}, u32[]{:S(2)}) collective-permute-start(bf16[16,2,64,128]{3,2,1,0:T(8,128)(2,1)} %get-tuple-element.23), channel_id=1, source_target_pairs={{0,1},{1,0},{2,3},{3,2},{4,5},{5,4},{6,7},{7,6},{8,9},{9,8},{10,11... | collective-permute-start | bytes 1572872 | tf_op jit(solution)/shard_map/ppermute | solution.py:280
  100.5 25.3 %collective-permute-start.7 = (bf16[16,2,64,128]{3,2,1,0:T(8,128)(2,1)}, bf16[16,2,64,128]{3,2,1,0:T(8,128)(2,1)}, u32[]{:S(2)}, u32[]{:S(2)}) collective-permute-start(bf16[16,2,64,128]{3,2,1,0:T(8,128)(2,1)} %get-tuple-element.24), channel_id=1, source_target_pairs={{0,2},{1,3},{2,0},{3,1},{4,6},{5,7},{6,4},{7,5},{8,10},{9,11},{10,... | collective-permute-start | bytes 1572872 | tf_op jit(solution)/shard_map/ppermute | solution.py:280
  103.1 24.7 %collective-permute-start.8 = (bf16[16,2,64,128]{3,2,1,0:T(8,128)(2,1)}, bf16[16,2,64,128]{3,2,1,0:T(8,128)(2,1)}, u32[]{:S(2)}, u32[]{:S(2)}) collective-permute-start(bf16[16,2,64,128]{3,2,1,0:T(8,128)(2,1)} %get-tuple-element.25), channel_id=1, source_target_pairs={{0,3},{1,2},{2,1},{3,0},{4,7},{5,6},{6,5},{7,4},{8,11},{9,10},{10,... | collective-permute-start | bytes 1572872 | tf_op jit(solution)/shard_map/ppermute | solution.py:280
  103.1 27.2 %all-to-all-start.2 = ((bf16[16,48,384]{2,1,0:T(8,128)(2,1)}), bf16[16,48,384]{2,1,0:T(8,128)(2,1)S(1)}, u32[]{:S(2)}, u32[]{:S(2)}) async-start(bf16[16,48,384]{2,1,0:T(8,128)(2,1)} %bitcast.16), calls=%async_computation.2 | async-start | bytes 1179648 | tf_op jit(solution)/shard_map/all_to_all | solution.py:282
  130.3 0.8 copy-start.1
  133.7 19.8 %all-to-all-start.3 = ((bf16[32,64,128]{2,1,0:T(8,128)(2,1)}), bf16[32,64,128]{2,1,0:T(8,128)(2,1)}, u32[]{:S(2)}, u32[]{:S(2)}) async-start(bf16[32,64,128]{2,1,0:T(8,128)(2,1)} %bitcast.15), calls=%async_computation.3 | async-start | bytes 1048576 | tf_op jit(solution)/shard_map/all_to_all | solution.py:289
  154.5 8.7 %collective-permute-start.9 = (bf16[3,64,768]{2,1,0:T(8,128)(2,1)S(1)}, bf16[3,64,768]{2,1,0:T(8,128)(2,1)S(1)}, u32[]{:S(2)}, u32[]{:S(2)}) collective-permute-start(bf16[3,64,768]{2,1,0:T(8,128)(2,1)S(1)} %constant_dynamic-slice_fusion), channel_id=1, source_target_pairs={{0,8},{8,0},{16,24},{24,16},{32,40},{40,32},{48,56},{56,48},{64,72... | collective-permute-start | bytes 884744 | tf_op jit(solution)/shard_map/ppermute | solution.py:299
  155.4 7.7 %copy-start.4 = (bf16[384,768]{1,0:T(8,128)(2,1)S(1)}, bf16[384,768]{1,0:T(8,128)(2,1)}, u32[]{:S(2)}) copy-start(bf16[384,768]{1,0:T(8,128)(2,1)} %fusion.1) | copy-start | bytes 1769476

commit v4 on v3

--- a/solution.py
+++ b/solution.py
@@ -22,15 +22,17 @@
 
 def pair_kernel(pair_ref, w_ref, out_ref):
     rows, cols, chans = pair_ref.shape
-    heads = w_ref.shape[1]
+    heads = w_ref.shape[0]
     normed, _ = unit(pair_ref[...].astype(F32).reshape(rows * cols, chans))
     high = normed.astype(BF)
     low = (normed - high.astype(F32)).astype(BF)
-    weight = w_ref[...].astype(F32).T.astype(BF)
+    weight = w_ref[...]
     both = jnp.concatenate([high, low], axis=1)
     weight = jnp.concatenate([weight, weight], axis=1)
     flat = lax.dot_general(weight, both, (((1,), (1,)), ((), ())), preferred_element_type=F32)
-    out_ref[...] = flat.reshape(heads, rows, cols).astype(BF)
+    flat = flat.reshape(heads, rows, cols).astype(BF)
+    out_ref[:, 0] = flat
+    out_ref[:, 1] = flat
 
 def pair_bias(pair, bias_weight, step=16):
     rows, cols, chans = pair.shape
@@ -38,11 +40,11 @@
     return pl.pallas_call(
         pair_kernel, grid=(rows // step,),
         in_specs=[pl.BlockSpec((step, cols, chans), lambda i: (i, 0, 0)),
-                  pl.BlockSpec((chans, heads), lambda i: (0, 0))],
-        out_specs=pl.BlockSpec((heads, step, cols), lambda i: (0, i, 0)),
-        out_shape=jax.ShapeDtypeStruct((heads, rows, cols), BF),
+                  pl.BlockSpec((heads, chans), lambda i: (0, 0))],
+        out_specs=pl.BlockSpec((heads, 2, step, cols), lambda i: (0, 0, i, 0)),
+        out_shape=jax.ShapeDtypeStruct((heads, 2, rows, cols), BF),
         compiler_params=pltpu.CompilerParams(dimension_semantics=("arbitrary",), vmem_limit_bytes=60 << 20),
-    )(pair, bias_weight)
+    )(pair, bias_weight.T)
 
 def back_kernel(pair_ref, grad_ref, w_ref, out_ref):
     rows, cols, chans = pair_ref.shape
@@ -54,7 +56,7 @@
     grad = grad.reshape(heads, rows * cols)
     high = grad.astype(BF)
     low = (grad - high.astype(F32)).astype(BF)
-    weight = w_ref[...].astype(F32).T.astype(BF)
+    weight = w_ref[...]
     both = jnp.concatenate([high, low], axis=0)
     weight = jnp.concatenate([weight, weight], axis=0)
     normed_grad = lax.dot_general(both, weight, (((0,), (0,)), ((), ())), preferred_element_type=F32)
@@ -69,11 +71,11 @@
         back_kernel, grid=(rows // step,),
         in_specs=[pl.BlockSpec((step, cols, chans), lambda i: (i, 0, 0)),
                   pl.BlockSpec((heads, parts, step, cols), lambda i: (0, 0, i, 0)),
-                  pl.BlockSpec((chans, heads), lambda i: (0, 0))],
+                  pl.BlockSpec((heads, chans), lambda i: (0, 0))],
         out_specs=pl.BlockSpec((step, cols, chans), lambda i: (i, 0, 0)),
         out_shape=jax.ShapeDtypeStruct((rows, cols, chans), F32),
         compiler_params=pltpu.CompilerParams(dimension_semantics=("arbitrary",), vmem_limit_bytes=60 << 20),
-    )(pair, grad, bias_weight)
+    )(pair, grad, bias_weight.T)
 
 def project_kernel(core_ref, single_ref, got_ref, cot_ref, gotc_ref, w_ref, packed_ref, tokens_ref, normed, cotan):
     half, block, width = tokens_ref.shape
@@ -124,13 +126,65 @@
         compiler_params=pltpu.CompilerParams(dimension_semantics=("arbitrary",), vmem_limit_bytes=60 << 20),
     )(core, single, got, cot, gotc, w_qkv)
 
+def transition_kernel(core_ref, tokens_ref, att_ref, wo_ref, wg_ref, wu_ref, wd_ref, mine_ref, theirs_ref, mid, normed, done):
+    half, block, width = tokens_ref.shape
+    rows = block // 2
+    step = pl.program_id(0)
+
+    @pl.when(step == 0)
+    def _():
+        attended = att_ref[...].astype(F32).T.astype(BF)
+        flat = tokens_ref[...].reshape(half * block, width).astype(F32)
+        flat = flat + jnp.dot(attended, wo_ref[...], preferred_element_type=F32)
+        mid[...] = flat
+        normed[...] = unit(flat)[0].astype(BF)
+
+    gate = jnp.dot(normed[...], wg_ref[...], preferred_element_type=F32)
+    up = jnp.dot(normed[...], wu_ref[...], preferred_element_type=F32)
+    hidden = (jax.nn.silu(gate) * up).astype(BF)
+    mid[...] += jnp.dot(hidden, wd_ref[...], preferred_element_type=F32)
+
+    @pl.when(step == pl.num_programs(0) - 1)
+    def _():
+        done[...] = mid[...].astype(BF).reshape(half, block, width)
+        core = core_ref[0]
+        mine = pl.ds(pl.multiple_of(core * rows, rows), rows)
+        other = pl.ds(pl.multiple_of((1 - core) * rows, rows), rows)
+        for u in range(half):
+            mine_ref[u] = done[u, mine, :]
+            theirs_ref[u] = done[u, other, :]
+
+def transition(core, tokens, attended_t, w_out, w_gate_up, w_down, steps=4):
+    half, block, width = tokens.shape
+    lanes = half * block
+    inner = w_down.shape[0]
+    part = inner // steps
+    out = pl.BlockSpec((half, block // 2, width), lambda i, c: (0, 0, 0))
+    return pl.pallas_call(
+        transition_kernel,
+        grid_spec=pltpu.PrefetchScalarGridSpec(
+            num_scalar_prefetch=1, grid=(steps,),
+            in_specs=[pl.BlockSpec((half, block, width), lambda i, c: (0, 0, 0)),
+                      pl.BlockSpec((width, lanes), lambda i, c: (0, 0)),
+                      pl.BlockSpec((width, width), lambda i, c: (0, 0)),
+                      pl.BlockSpec((width, part), lambda i, c: (0, i)),
+                      pl.BlockSpec((width, part), lambda i, c: (0, i + steps)),
+                      pl.BlockSpec((part, width), lambda i, c: (i, 0))],
+            out_specs=[out, out],
+            scratch_shapes=[pltpu.VMEM((lanes, width), F32), pltpu.VMEM((lanes, width), BF),
+                            pltpu.VMEM((half, block, width), BF)],
+        ),
+        out_shape=[jax.ShapeDtypeStruct((half, block // 2, width), BF)] * 2,
+        compiler_params=pltpu.CompilerParams(dimension_semantics=("arbitrary",), vmem_limit_bytes=60 << 20),
+    )(core, tokens, attended_t, w_out, w_gate_up, w_gate_up, w_down)
+
 
 def attend_kernel(n_col, n_chip, n_samp, size, span, unroll, c_ref, blk_ref, *refs):
     bias_refs = refs[: n_col // 2]
     att_ref = refs[n_col // 2]
     out_refs = refs[n_col // 2 + 1 : n_col + 1]
     bias2, acc, kt, vt = refs[n_col + 1 :]
-    half_rows = bias_refs[0].shape[1] // 2
+    side = c_ref[0] // (n_col // 2)
     samp = pl.program_id(0)
     me = c_ref[0]
     block = blk_ref.shape[2]
@@ -139,8 +193,8 @@
     @pl.when(samp == 0)
     def _():
         for k in range(n_col):
-            far = k // (n_col // 2)
-            part = bias_refs[k % (n_col // 2)][:, far * half_rows : (far + 1) * half_rows, :]
+            far = jnp.bitwise_xor(side, k // (n_col // 2))
+            part = bias_refs[k % (n_col // 2)][:, far]
             part = part.astype(F32).reshape(bias2.shape[0], block)
             bias2[:, k * block : (k + 1) * block] = part * LOG2E
         acc[...] = jnp.zeros_like(acc)
@@ -204,8 +258,8 @@
         for k in range(n_col):
             part = acc[:, k * block : (k + 1) * block].astype(BF)
             out_ref = out_refs[k % (n_col // 2)]
-            far = jnp.bitwise_xor(me // (n_col // 2), k // (n_col // 2))
-            out_ref[:, far] = part.reshape(out_ref.shape[0], half_rows, block)
+            far = jnp.bitwise_xor(side, k // (n_col // 2))
+            out_ref[:, far] = part.reshape(out_ref.shape[0], out_ref.shape[2], block)
 
 
 def attend(me, qkvc, biases, n_samp, size, span=1, unroll=1):
@@ -213,11 +267,10 @@
     per = n_samp // 2
     block = lanes // per
     n_col = 2 * len(biases)
-    n_row, both_rows, _ = biases[0].shape
     tokens = n_chip * block
     wide = n_col * block
-    whole = pl.BlockSpec((n_row, both_rows, block), lambda s, c: (0, 0, 0))
-    parts = (n_row, 2, both_rows // 2, block)
+    parts = biases[0].shape
+    whole = pl.BlockSpec(parts, lambda s, c: (0, 0, 0, 0))
     spec = lambda feats: pl.BlockSpec((n_chip, None, feats, block), lambda s, c: (0, s // per, 0, s % per))
     return pl.pallas_call(
         functools.partial(attend_kernel, n_col, n_chip, n_samp, size, span, unroll),
@@ -225,7 +278,7 @@
             num_scalar_prefetch=1,
             grid=(n_samp,),
             in_specs=[spec(4 * size)] + [whole] * len(biases),
-            out_specs=[spec(size)] + [pl.BlockSpec(parts, lambda s, c: (0, 0, 0, 0))] * len(biases),
+            out_specs=[spec(size)] + [whole] * len(biases),
             scratch_shapes=[
                 pltpu.VMEM((tokens, wide), F32),
                 pltpu.VMEM((tokens, wide), F32),
@@ -239,18 +292,6 @@
             dimension_semantics=("arbitrary",), vmem_limit_bytes=56 * 1024 * 1024
         ),
     )(me, qkvc, *biases)
-
-
-def transition(flat_in, attended_t, w_out, w_gate_up, w_down):
-    mid = flat_in.astype(F32) + lax.dot_general(
-        attended_t, w_out, (((0,), (0,)), ((), ())), preferred_element_type=F32
-    )
-    normed_mid = unit(mid)[0].astype(BF)
-    gate_up = jnp.dot(normed_mid, w_gate_up, preferred_element_type=F32)
-    half = gate_up.shape[1] // 2
-    hidden = (jax.nn.silu(gate_up[:, :half]) * gate_up[:, half:]).astype(BF)
-    result = mid + jnp.dot(hidden, w_down, preferred_element_type=F32)
-    return result.astype(BF)
 
 
 def shards(n_row, n_col, pair, bias_weight, single, w_qkv, w_out, w_gate_up, w_down, cotangent):
@@ -267,11 +308,12 @@
 
     got = lax.ppermute(single, "row", cores)
     got_cot = lax.ppermute(cotangent, "row", cores)
-    bias = pair_bias(pair, bias_weight, 16)
-    bias, got, got_cot = lax.optimization_barrier((bias, got, got_cot))
-    far = lax.ppermute(bias, "col", flip(n_col // 2))
+    groups = [[r * n_col + z * (n_col // 2) + y for r in range(n_row) for z in range(2)] for y in range(n_col // 2)]
+    share = lambda v: lax.all_to_all(
+        v.reshape(2 * n_row, rows, pair.shape[1]), ("row", "col"), 0, 0, tiled=True, axis_index_groups=groups
+    ).reshape(n_row, 2, rows, pair.shape[1])
+    bias = share(pair_bias(pair, bias_weight, 16))
     packed, tokens = project(core.reshape(1), single, got, cotangent, got_cot, w_qkv, heads)
-    bias = lax.all_to_all(jnp.concatenate([bias, far], axis=1), "row", 0, 0, tiled=True)
     biases = [bias] + [lax.ppermute(bias, "col", flip(k)) for k in range(1, n_col // 2)]
 
     packed = lax.all_to_all(packed, "row", 0, 0, tiled=True)
@@ -284,18 +326,11 @@
     for part in grads[1:]:
         total = total + part.astype(F32)
     attended, total = lax.optimization_barrier((attended, total.astype(BF)))
-    total = total.reshape(2 * n_row, rows, pair.shape[1])
-    groups = [[r * n_col + z * (n_col // 2) + y for r in range(n_row) for z in range(2)] for y in range(n_col // 2)]
-    total = lax.all_to_all(total, ("row", "col"), 0, 0, tiled=True, axis_index_groups=groups)
-    total = total.reshape(n_row, 2, rows, pair.shape[1])
-
-    updated = transition(
-        tokens.reshape(half * block, width), attended.reshape(width, half * block), w_out, w_gate_up, w_down
+    total = share(total)
+    mine, theirs = transition(
+        core.reshape(1), tokens, attended.reshape(width, half * block), w_out, w_gate_up, w_down
     )
-    updated, total = lax.optimization_barrier((updated, total))
-    updated = updated.reshape(half, block, width)
-    mine = lax.dynamic_slice_in_dim(updated, core * rows, rows, 1)
-    theirs = lax.dynamic_slice_in_dim(updated, (1 - core) * rows, rows, 1)
+    mine, theirs, total = lax.optimization_barrier((mine, theirs, total))
     got = lax.ppermute(theirs, "row", cores)
     updated = jnp.concatenate([jnp.where(core == 0, mine, got), jnp.where(core == 0, got, mine)], axis=0)
     pair_grad = pair_back(pair, total, bias_weight, 16)

time: 165 us -> 147 us (0.89)
  waiting for transfers between devices: 58.6 us -> 45.8 us
  Pallas kernels: 45.2 us -> 54.5 us
  matrix products: 8.95 us -> 0 us
  starting transfers between devices: 42 us -> 39.4 us
  other arithmetic: 5.57 us -> 3.11 us
    pallas_call x0 -> x1, Pallas kernels: none -> 9.42 us  [transition(): pl.pallas_call(transition_kernel, grid_spec=pltpu.PrefetchScalarGridSpec(...]
    dot_general x3 -> x0, matrix products: 8.95 us -> none  [the longest x1 4.38 us: transition(): gate_up = jnp.dot(normed_mid, w_gate_up, preferred_element_type=F32)]
    ppermute x1 -> x0, waiting for transfers between devices: 6.38 us -> none  [shards(): far = lax.ppermute(bias, 'col', flip(n_col // 2))]
    all_to_all x2, waiting for transfers between devices: 7.02 us -> 3.1 us  [shards(): lax.all_to_all(v.reshape(2 * n_row, rows, pair.shape[1]), ('row', 'col'),...]
    ppermute x3, waiting for transfers between devices: 17.6 us -> 15.3 us  [shards(): lax.ppermute(grads[k], 'col', flip(k))]
    ppermute x1 -> x0, starting transfers between devices: 1.8 us -> none  [shards(): far = lax.ppermute(bias, 'col', flip(n_col // 2))]
    concatenate x1 -> x0, other arithmetic: 1.79 us -> none  [shards(): jnp.concatenate([bias, far], axis=1)]
  transfers between devices with their start and end apart: 14 -> 13, of which waited for: 10 -> 8; matrix products, arithmetic and copies ran while one was open for 6% -> 2% of each run, Pallas kernels for 13% -> 21%
where the time goes in v4:
time: 147 us; the launch traced here: 146 us
  Pallas kernels  54.5 us (37%)
  waiting for transfers between devices  45.8 us (31%)
  starting transfers between devices  39.4 us (27%)
  other arithmetic  3.11 us (2%)
  local copies, waits for them, and re-layouts  2.42 us (2%)
    ppermute x3, waiting for transfers between devices, shards(): lax.ppermute(bias, 'col', flip(k))  25.3 us
    pallas_call x1, Pallas kernels, attend(): pl.pallas_call(functools.partial(attend_kernel, n_col, n_chip, n_samp, si...  23.4 us
    all_to_all x2, starting transfers between devices, shards(): lax.all_to_all(v.reshape(2 * n_row, rows, pair.shape[1]), ('row', 'col'),...  16.6 us
    ppermute x3, waiting for transfers between devices, shards(): lax.ppermute(grads[k], 'col', flip(k))  15.3 us
    pallas_call x1, Pallas kernels, transition(): pl.pallas_call(transition_kernel, grid_spec=pltpu.PrefetchScalarGridSpec(...  9.42 us
    pallas_call x1, Pallas kernels, project(): pl.pallas_call(project_kernel, grid_spec=pltpu.PrefetchScalarGridSpec(num...  8.62 us
    pallas_call x1, Pallas kernels, pair_back(): pl.pallas_call(back_kernel, grid=(rows // step,), in_specs=[pl.BlockSpec(...  7.66 us
    all_to_all x1, starting transfers between devices, shards(): attended = lax.all_to_all(attended, 'row', 0, 0, tiled=True)  7.12 us
  transfers between devices with their start and end apart: 13, of which 8 were waited for; matrix products, arithmetic and copies ran while one was open for 2% of the time, Pallas kernels for 21%

profile of v4, /device:TPU:1, one launch (start us, length us, event | category | flops | bytes accessed | tf_op | source)
XLA Modules:
  0.0 145.9 jit_solution(11115534663053453155)
XLA Ops:
  0.6 1.5 %collective-permute-start = (bf16[6,64,768]{2,1,0:T(8,128)(2,1)}, bf16[6,64,768]{2,1,0:T(8,128)(2,1)S(1)}, u32[]{:S(2)}, u32[]{:S(2)}) collective-permute-start(bf16[6,64,768]{2,1,0:T(8,128)(2,1)} %single_ref.1), channel_id=1, source_target_pairs={{0,8},{8,0},{16,24},{24,16},{32,40},{40,32},{48,56},{56,48},{64,72... | collective-permute-start | bytes 1769480 | tf_op jit(solution)/shard_map/ppermute | solution.py:309
  2.1 0.1 collective-permute-start.1
  2.2 5.4 %shard_map.96 = bf16[16,2,64,128]{3,2,1,0:T(8,128)(2,1)} custom-call(bf16[64,128,128]{2,1,0:T(8,128)(2,1)} %pair_ref.3, bf16[16,128]{1,0:T(8,128)(2,1)} %bitcast.19), custom_call_target="tpu_custom_call" | custom-call | tf_op jit(solution)/shard_map/pallas_call | solution.py:40
  7.6 8.4 %all-to-all-start.1 = ((bf16[32,64,128]{2,1,0:T(8,128)(2,1)}), bf16[32,64,128]{2,1,0:T(8,128)(2,1)S(1)}, u32[]{:S(2)}, u32[]{:S(2)}) async-start(bf16[32,64,128]{2,1,0:T(8,128)(2,1)} %bitcast.16), calls=%async_computation.1 | async-start | bytes 1048576 | tf_op jit(solution)/shard_map/all_to_all | solution.py:312
  16.1 0.0 copy-start.4
  16.1 0.0 collective-permute-done.1.gotc_ref
  16.1 0.8 copy-done.4
  16.9 0.2 copy-done.5
  17.1 8.6 %shard_map.95 = (bf16[16,192,384]{2,1,0:T(8,128)(2,1)}, bf16[3,128,768]{2,1,0:T(8,128)(2,1)}) custom-call(s32[1]{0:T(128)} %bitcast.core_ref, bf16[6,64,768]{2,1,0:T(8,128)(2,1)} %single_ref.1, bf16[6,64,768]{2,1,0:T(8,128)(2,1)} %copy-done.4, bf16[6,64,768]{2,1,0:T(8,128)(2,1)} %cot_ref.1, bf16[6,64,768]{2,1,0:T(8,128)(2,1)} %copy-done.5, ...), custom_call_target="tpu_custom_call" | custom-call | tf_op jit(solution)/shard_map/pallas_call | solution.py:116
  25.7 1.4 all-to-all-done.1
  27.2 5.8 %all-to-all-start = ((bf16[16,192,384]{2,1,0:T(8,128)(2,1)}), bf16[16,192,384]{2,1,0:T(8,128)(2,1)S(1)}, u32[]{:S(2)}, u32[]{:S(2)}) async-start(bf16[16,192,384]{2,1,0:T(8,128)(2,1)} %get-tuple-element.17), calls=%async_computation | async-start | bytes 4718592 | tf_op jit(solution)/shard_map/all_to_all | solution.py:319
  33.0 1.3 collective-permute-start.2
  34.3 2.6 %collective-permute-start.3 = (bf16[16,2,64,128]{3,2,1,0:T(8,128)(2,1)S(1)}, bf16[16,2,64,128]{3,2,1,0:T(8,128)(2,1)}, u32[]{:S(2)}, u32[]{:S(2)}) collective-permute-start(bf16[16,2,64,128]{3,2,1,0:T(8,128)(2,1)S(1)} %bitcast.13), channel_id=1, source_target_pairs={{0,2},{1,3},{2,0},{3,1},{4,6},{5,7},{6,4},{7,5},{8,10},{9,11},{10,... | collective-permute-start | bytes 1572872 | tf_op jit(solution)/shard_map/ppermute | solution.py:317
  36.9 9.5 %collective-permute-done.2.refs_1_ = bf16[16,2,64,128]{3,2,1,0:T(8,128)(2,1)S(1)} collective-permute-done((bf16[16,2,64,128]{3,2,1,0:T(8,128)(2,1)S(1)}, bf16[16,2,64,128]{3,2,1,0:T(8,128)(2,1)S(1)}, u32[]{:S(2)}, u32[]{:S(2)}) %collective-permute-start.2) | collective-permute-done | bytes 524320 | tf_op jit(solution)/shard_map/ppermute | solution.py:317
  46.4 13.7 %collective-permute-done.3.refs_2_ = bf16[16,2,64,128]{3,2,1,0:T(8,128)(2,1)} collective-permute-done((bf16[16,2,64,128]{3,2,1,0:T(8,128)(2,1)S(1)}, bf16[16,2,64,128]{3,2,1,0:T(8,128)(2,1)}, u32[]{:S(2)}, u32[]{:S(2)}) %collective-permute-start.3) | collective-permute-done | bytes 524320 | tf_op jit(solution)/shard_map/ppermute | solution.py:317
  60.2 2.0 %collective-permute-done.4.refs_3_ = bf16[16,2,64,128]{3,2,1,0:T(8,128)(2,1)} collective-permute-done((bf16[16,2,64,128]{3,2,1,0:T(8,128)(2,1)S(1)}, bf16[16,2,64,128]{3,2,1,0:T(8,128)(2,1)}, u32[]{:S(2)}, u32[]{:S(2)}) %collective-permute-start.4) | collective-permute-done | bytes 524320 | tf_op jit(solution)/shard_map/ppermute | solution.py:317
  62.2 2.1 %all-to-all-done = bf16[16,192,384]{2,1,0:T(8,128)(2,1)S(1)} async-done(((bf16[16,192,384]{2,1,0:T(8,128)(2,1)}), bf16[16,192,384]{2,1,0:T(8,128)(2,1)S(1)}, u32[]{:S(2)}, u32[]{:S(2)}) %all-to-all-start) | async-done | bytes 2359328 | tf_op jit(solution)/shard_map/all_to_all | solution.py:319
  64.2 1.4 copy-done
  65.6 23.4 %shard_map.97 = (bf16[8,2,48,384]{3,2,1,0:T(8,128)(2,1)}, bf16[16,2,64,128]{3,2,1,0:T(8,128)(2,1)}, bf16[16,2,64,128]{3,2,1,0:T(8,128)(2,1)}, bf16[16,2,64,128]{3,2,1,0:T(8,128)(2,1)}, bf16[16,2,64,128]{3,2,1,0:T(8,128)(2,1)}) custom-call(s32[1]{0:T(128)} %bitcast.1.c_ref, bf16[8,2,192,384]{3,2,1,0:T(8,128)(2,1)} %bitcast.10, ...), custom_call_target="tpu_custom_call" | custom-call | tf_op jit(solution)/shard_map/pallas_call | solution.py:275
  89.1 2.7 %collective-permute-start.7 = (bf16[16,2,64,128]{3,2,1,0:T(8,128)(2,1)}, bf16[16,2,64,128]{3,2,1,0:T(8,128)(2,1)S(1)}, u32[]{:S(2)}, u32[]{:S(2)}) collective-permute-start(bf16[16,2,64,128]{3,2,1,0:T(8,128)(2,1)} %get-tuple-element.22), channel_id=1, source_target_pairs={{0,3},{1,2},{2,1},{3,0},{4,7},{5,6},{6,5},{7,4},{8,11},{9,10},{10,... | collective-permute-start | bytes 1572872 | tf_op jit(solution)/shard_map/ppermute | solution.py:322
  91.8 0.3 collective-permute-start.6
  92.2 0.3 collective-permute-start.5
  92.5 7.1 %all-to-all-start.2 = ((bf16[16,48,384]{2,1,0:T(8,128)(2,1)}), bf16[16,48,384]{2,1,0:T(8,128)(2,1)S(1)}, u32[]{:S(2)}, u32[]{:S(2)}) async-start(bf16[16,48,384]{2,1,0:T(8,128)(2,1)} %bitcast.18), calls=%async_computation.2 | async-start | bytes 1179648 | tf_op jit(solution)/shard_map/all_to_all | solution.py:324
  99.6 15.0 %collective-permute-done.7 = bf16[16,2,64,128]{3,2,1,0:T(8,128)(2,1)S(1)} collective-permute-done((bf16[16,2,64,128]{3,2,1,0:T(8,128)(2,1)}, bf16[16,2,64,128]{3,2,1,0:T(8,128)(2,1)S(1)}, u32[]{:S(2)}, u32[]{:S(2)}) %collective-permute-start.7) | collective-permute-done | bytes 524320 | tf_op jit(solution)/shard_map/ppermute | solution.py:322
  114.6 0.3 collective-permute-done.5
  114.9 2.2 %add_convert_fusion = bf16[16,2,64,128]{3,2,1,0:T(8,128)(2,1)} fusion(bf16[16,2,64,128]{3,2,1,0:T(8,128)(2,1)S(1)} %collective-permute-done.7, bf16[16,2,64,128]{3,2,1,0:T(8,128)(2,1)S(1)} %collective-permute-done.6, bf16[16,2,64,128]{3,2,1,0:T(8,128)(2,1)S(1)} %collective-permute-done.5, bf16[16,2,64,128]{3,2,1,0:T(8,128)(2,1)} %get-tuple-element.19), kind=kLoop, calls=%fused_computation | loop fusion | flops 2097152 | bytes 2621440 | tf_op jit(solution)/shard_map/convert_element_type | solution.py:328
  117.1 8.2 %all-to-all-start.3 = ((bf16[32,64,128]{2,1,0:T(8,128)(2,1)}), bf16[32,64,128]{2,1,0:T(8,128)(2,1)S(1)}, u32[]{:S(2)}, u32[]{:S(2)}) async-start(bf16[32,64,128]{2,1,0:T(8,128)(2,1)} %bitcast.8), calls=%async_computation.3 | async-start | bytes 1048576 | tf_op jit(solution)/shard_map/all_to_all | solution.py:312
  125.4 9.4 %shard_map.98 = (bf16[3,64,768]{2,1,0:T(8,128)(2,1)}, bf16[3,64,768]{2,1,0:T(8,128)(2,1)}) custom-call(s32[1]{0:T(128)} %bitcast.core_ref, bf16[3,128,768]{2,1,0:T(8,128)(2,1)} %get-tuple-element.16.tokens_ref, bf16[768,384]{1,0:T(8,128)(2,1)} %bitcast.11, bf16[768,768]{1,0:T(8,128)(2,1)} %wo_ref.1, bf16[768,3072]{1,0:T(8,128)(2,1)} %wu_ref.1, ...), custom_call_target="tpu_custom_call" | custom-call | tf_op jit(solution)/shard_map/pallas_call | solution.py:163
  134.8 1.7 %all-to-all-done.3 = bf16[32,64,128]{2,1,0:T(8,128)(2,1)S(1)} async-done(((bf16[32,64,128]{2,1,0:T(8,128)(2,1)}), bf16[32,64,128]{2,1,0:T(8,128)(2,1)S(1)}, u32[]{:S(2)}, u32[]{:S(2)}) %all-to-all-start.3) | async-done | bytes 524320 | tf_op jit(solution)/shard_map/all_to_all | solution.py:312
  136.4 0.9 collective-permute-start.8
  137.3 7.7 %shard_map.99 = f32[64,128,128]{2,1,0:T(8,128)} custom-call(bf16[64,128,128]{2,1,0:T(8,128)(2,1)} %pair_ref.3, bf16[16,2,64,128]{3,2,1,0:T(8,128)(2,1)} %bitcast.17, bf16[16,128]{1,0:T(8,128)(2,1)} %bitcast.20), custom_call_target="tpu_custom_call" | custom-call | tf_op jit(solution)/shard_map/pallas_call | solution.py:70
  145.0 0.9 pad_maximum_fusion
  (18 shorter events, 0.1 us)
Async XLA Ops:
  0.6 15.4 %collective-permute-start = (bf16[6,64,768]{2,1,0:T(8,128)(2,1)}, bf16[6,64,768]{2,1,0:T(8,128)(2,1)S(1)}, u32[]{:S(2)}, u32[]{:S(2)}) collective-permute-start(bf16[6,64,768]{2,1,0:T(8,128)(2,1)} %single_ref.1), channel_id=1, source_target_pairs={{0,8},{8,0},{16,24},{24,16},{32,40},{40,32},{48,56},{56,48},{64,72... | collective-permute-start | bytes 1769480 | tf_op jit(solution)/shard_map/ppermute | solution.py:309
  2.1 13.9 %collective-permute-start.1 = (bf16[6,64,768]{2,1,0:T(8,128)(2,1)}, bf16[6,64,768]{2,1,0:T(8,128)(2,1)S(1)}, u32[]{:S(2)}, u32[]{:S(2)}) collective-permute-start(bf16[6,64,768]{2,1,0:T(8,128)(2,1)} %cot_ref.1), channel_id=1, source_target_pairs={{0,8},{8,0},{16,24},{24,16},{32,40},{40,32},{48,56},{56,48},{64,72... | collective-permute-start | bytes 1769480 | tf_op jit(solution)/shard_map/ppermute | solution.py:310
  7.6 19.5 %all-to-all-start.1 = ((bf16[32,64,128]{2,1,0:T(8,128)(2,1)}), bf16[32,64,128]{2,1,0:T(8,128)(2,1)S(1)}, u32[]{:S(2)}, u32[]{:S(2)}) async-start(bf16[32,64,128]{2,1,0:T(8,128)(2,1)} %bitcast.16), calls=%async_computation.1 | async-start | bytes 1048576 | tf_op jit(solution)/shard_map/all_to_all | solution.py:312
  16.1 0.8 copy-start.4
  16.1 1.0 copy-start.5
  27.2 9.7 %copy-start.2 = (bf16[32,64,128]{2,1,0:T(8,128)(2,1)}, bf16[32,64,128]{2,1,0:T(8,128)(2,1)S(1)}, u32[]{:S(2)}) copy-start(bf16[32,64,128]{2,1,0:T(8,128)(2,1)S(1)} %all-to-all-done.1) | copy-start | bytes 1572868
  27.2 37.1 %all-to-all-start = ((bf16[16,192,384]{2,1,0:T(8,128)(2,1)}), bf16[16,192,384]{2,1,0:T(8,128)(2,1)S(1)}, u32[]{:S(2)}, u32[]{:S(2)}) async-start(bf16[16,192,384]{2,1,0:T(8,128)(2,1)} %get-tuple-element.17), calls=%async_computation | async-start | bytes 4718592 | tf_op jit(solution)/shard_map/all_to_all | solution.py:319
  33.0 13.5 %collective-permute-start.2 = (bf16[16,2,64,128]{3,2,1,0:T(8,128)(2,1)S(1)}, bf16[16,2,64,128]{3,2,1,0:T(8,128)(2,1)S(1)}, u32[]{:S(2)}, u32[]{:S(2)}) collective-permute-start(bf16[16,2,64,128]{3,2,1,0:T(8,128)(2,1)S(1)} %bitcast.12), channel_id=1, source_target_pairs={{0,1},{1,0},{2,3},{3,2},{4,5},{5,4},{6,7},{7,6},{8,9},{9,8},{10,11... | collective-permute-start | bytes 1572872 | tf_op jit(solution)/shard_map/ppermute | solution.py:317
  34.3 25.9 %collective-permute-start.3 = (bf16[16,2,64,128]{3,2,1,0:T(8,128)(2,1)S(1)}, bf16[16,2,64,128]{3,2,1,0:T(8,128)(2,1)}, u32[]{:S(2)}, u32[]{:S(2)}) collective-permute-start(bf16[16,2,64,128]{3,2,1,0:T(8,128)(2,1)S(1)} %bitcast.13), channel_id=1, source_target_pairs={{0,2},{1,3},{2,0},{3,1},{4,6},{5,7},{6,4},{7,5},{8,10},{9,11},{10,... | collective-permute-start | bytes 1572872 | tf_op jit(solution)/shard_map/ppermute | solution.py:317
  36.9 25.3 %collective-permute-start.4 = (bf16[16,2,64,128]{3,2,1,0:T(8,128)(2,1)S(1)}, bf16[16,2,64,128]{3,2,1,0:T(8,128)(2,1)}, u32[]{:S(2)}, u32[]{:S(2)}) collective-permute-start(bf16[16,2,64,128]{3,2,1,0:T(8,128)(2,1)S(1)} %bitcast.14), channel_id=1, source_target_pairs={{0,3},{1,2},{2,1},{3,0},{4,7},{5,6},{6,5},{7,4},{8,11},{9,10},{10,... | collective-permute-start | bytes 1572872 | tf_op jit(solution)/shard_map/ppermute | solution.py:317
  46.4 17.8 %copy-start.6 = (bf16[16,2,64,128]{3,2,1,0:T(8,128)(2,1)}, bf16[16,2,64,128]{3,2,1,0:T(8,128)(2,1)S(1)}, u32[]{:S(2)}) copy-start(bf16[16,2,64,128]{3,2,1,0:T(8,128)(2,1)S(1)} %collective-permute-done.2.refs_1_) | copy-start | bytes 1572868
  64.2 1.4 copy-start
  89.1 25.5 %collective-permute-start.7 = (bf16[16,2,64,128]{3,2,1,0:T(8,128)(2,1)}, bf16[16,2,64,128]{3,2,1,0:T(8,128)(2,1)S(1)}, u32[]{:S(2)}, u32[]{:S(2)}) collective-permute-start(bf16[16,2,64,128]{3,2,1,0:T(8,128)(2,1)} %get-tuple-element.22), channel_id=1, source_target_pairs={{0,3},{1,2},{2,1},{3,0},{4,7},{5,6},{6,5},{7,4},{8,11},{9,10},{10,... | collective-permute-start | bytes 1572872 | tf_op jit(solution)/shard_map/ppermute | solution.py:322
  91.8 22.8 %collective-permute-start.6 = (bf16[16,2,64,128]{3,2,1,0:T(8,128)(2,1)}, bf16[16,2,64,128]{3,2,1,0:T(8,128)(2,1)S(1)}, u32[]{:S(2)}, u32[]{:S(2)}) collective-permute-start(bf16[16,2,64,128]{3,2,1,0:T(8,128)(2,1)} %get-tuple-element.21), channel_id=1, source_target_pairs={{0,2},{1,3},{2,0},{3,1},{4,6},{5,7},{6,4},{7,5},{8,10},{9,11},{10,... | collective-permute-start | bytes 1572872 | tf_op jit(solution)/shard_map/ppermute | solution.py:322
  92.2 22.8 %collective-permute-start.5 = (bf16[16,2,64,128]{3,2,1,0:T(8,128)(2,1)}, bf16[16,2,64,128]{3,2,1,0:T(8,128)(2,1)S(1)}, u32[]{:S(2)}, u32[]{:S(2)}) collective-permute-start(bf16[16,2,64,128]{3,2,1,0:T(8,128)(2,1)} %get-tuple-element.20), channel_id=1, source_target_pairs={{0,1},{1,0},{2,3},{3,2},{4,5},{5,4},{6,7},{7,6},{8,9},{9,8},{10,11... | collective-permute-start | bytes 1572872 | tf_op jit(solution)/shard_map/ppermute | solution.py:322
  92.5 24.6 %all-to-all-start.2 = ((bf16[16,48,384]{2,1,0:T(8,128)(2,1)}), bf16[16,48,384]{2,1,0:T(8,128)(2,1)S(1)}, u32[]{:S(2)}, u32[]{:S(2)}) async-start(bf16[16,48,384]{2,1,0:T(8,128)(2,1)} %bitcast.18), calls=%async_computation.2 | async-start | bytes 1179648 | tf_op jit(solution)/shard_map/all_to_all | solution.py:324
  117.1 8.2 %copy-start.1 = (bf16[16,48,384]{2,1,0:T(8,128)(2,1)}, bf16[16,48,384]{2,1,0:T(8,128)(2,1)S(1)}, u32[]{:S(2)}) copy-start(bf16[16,48,384]{2,1,0:T(8,128)(2,1)S(1)} %all-to-all-done.2) | copy-start | bytes 1769476
  117.1 19.3 %all-to-all-start.3 = ((bf16[32,64,128]{2,1,0:T(8,128)(2,1)}), bf16[32,64,128]{2,1,0:T(8,128)(2,1)S(1)}, u32[]{:S(2)}, u32[]{:S(2)}) async-start(bf16[32,64,128]{2,1,0:T(8,128)(2,1)} %bitcast.8), calls=%async_computation.3 | async-start | bytes 1048576 | tf_op jit(solution)/shard_map/all_to_all | solution.py:312
  136.4 0.9 copy-start.3
  136.4 8.5 %collective-permute-start.8 = (bf16[3,64,768]{2,1,0:T(8,128)(2,1)}, bf16[3,64,768]{2,1,0:T(8,128)(2,1)S(1)}, u32[]{:S(2)}, u32[]{:S(2)}) collective-permute-start(bf16[3,64,768]{2,1,0:T(8,128)(2,1)} %get-tuple-element.28), channel_id=1, source_target_pairs={{0,8},{8,0},{16,24},{24,16},{32,40},{40,32},{48,56},{56,48},{64,72... | collective-permute-start | bytes 884744 | tf_op jit(solution)/shard_map/ppermute | solution.py:334
  137.3 7.7 %copy-start.7 = (bf16[3,64,768]{2,1,0:T(8,128)(2,1)S(1)}, bf16[3,64,768]{2,1,0:T(8,128)(2,1)}, u32[]{:S(2)}) copy-start(bf16[3,64,768]{2,1,0:T(8,128)(2,1)} %get-tuple-element.27) | copy-start | bytes 884740

commit v5 on v4

--- a/solution.py
+++ b/solution.py
@@ -12,7 +12,6 @@
 F32 = jnp.float32
 LOG2E = 1.4426950408889634
 
-
 def unit(values):
     mean_val = jnp.mean(values, axis=-1, keepdims=True)
     centred = values - mean_val
@@ -20,17 +19,23 @@
     scaled = lax.rsqrt(variance + 1e-05)
     return centred * scaled, scaled
 
+def halves(v):
+    high = v.astype(BF)
+    return high, (v - high.astype(F32)).astype(BF)
+
+def across(lhs, rhs):
+    return lax.dot_general(lhs, rhs, (((1,), (1,)), ((), ())), preferred_element_type=F32)
+
 def pair_kernel(pair_ref, w_ref, out_ref):
     rows, cols, chans = pair_ref.shape
     heads = w_ref.shape[0]
-    normed, _ = unit(pair_ref[...].astype(F32).reshape(rows * cols, chans))
-    high = normed.astype(BF)
-    low = (normed - high.astype(F32)).astype(BF)
+    values = pair_ref[...].astype(F32).reshape(rows * cols, chans)
+    centred = values - jnp.mean(values, axis=-1, keepdims=True)
     weight = w_ref[...]
-    both = jnp.concatenate([high, low], axis=1)
-    weight = jnp.concatenate([weight, weight], axis=1)
-    flat = lax.dot_general(weight, both, (((1,), (1,)), ((), ())), preferred_element_type=F32)
-    flat = flat.reshape(heads, rows, cols).astype(BF)
+    flat = across(jnp.concatenate([weight, weight], axis=1), jnp.concatenate(halves(centred), axis=1))
+    ones = jnp.full((8, 2 * chans), 1.0 / chans, BF)
+    variance = across(ones, jnp.concatenate(halves(centred * centred), axis=1))[:1]
+    flat = (flat * lax.rsqrt(variance + 1e-05)).reshape(heads, rows, cols).astype(BF)
     out_ref[:, 0] = flat
     out_ref[:, 1] = flat
 
@@ -46,36 +51,55 @@
         compiler_params=pltpu.CompilerParams(dimension_semantics=("arbitrary",), vmem_limit_bytes=60 << 20),
     )(pair, bias_weight.T)
 
-def back_kernel(pair_ref, grad_ref, w_ref, out_ref):
+def stats_kernel(pair_ref, normed_ref, scaled_ref):
     rows, cols, chans = pair_ref.shape
+    normed, scaled = unit(pair_ref[...].astype(F32).reshape(rows * cols, chans))
+    normed_ref[...] = normed.reshape(rows, cols, chans)
+    lanes = jnp.broadcast_to(scaled, (rows * cols, chans)).reshape(rows, cols, chans)
+    for i in range(rows):
+        scaled_ref[i : i + 1] = lanes[i].T[:1]
+
+def pair_stats(pair, step=16):
+    rows, cols, chans = pair.shape
+    return pl.pallas_call(
+        stats_kernel, grid=(rows // step,),
+        in_specs=[pl.BlockSpec((step, cols, chans), lambda i: (i, 0, 0))],
+        out_specs=[pl.BlockSpec((step, cols, chans), lambda i: (i, 0, 0)), pl.BlockSpec((step, cols), lambda i: (i, 0))],
+        out_shape=[jax.ShapeDtypeStruct((rows, cols, chans), F32), jax.ShapeDtypeStruct((rows, cols), F32)],
+        compiler_params=pltpu.CompilerParams(dimension_semantics=("arbitrary",), vmem_limit_bytes=60 << 20),
+    )(pair)
+
+def back_kernel(normed_ref, scaled_ref, grad_ref, w_ref, out_ref):
+    rows, cols, chans = normed_ref.shape
     heads, parts = grad_ref.shape[:2]
-    normed, scaled = unit(pair_ref[...].astype(F32).reshape(rows * cols, chans))
     grad = grad_ref[:, 0].astype(F32)
     for g in range(1, parts):
         grad = grad + grad_ref[:, g].astype(F32)
-    grad = grad.reshape(heads, rows * cols)
-    high = grad.astype(BF)
-    low = (grad - high.astype(F32)).astype(BF)
-    weight = w_ref[...]
-    both = jnp.concatenate([high, low], axis=0)
-    weight = jnp.concatenate([weight, weight], axis=0)
-    normed_grad = lax.dot_general(both, weight, (((0,), (0,)), ((), ())), preferred_element_type=F32)
-    centred = normed_grad - jnp.mean(normed_grad, axis=-1, keepdims=True)
-    along = jnp.mean(normed_grad * normed, axis=-1, keepdims=True)
-    out_ref[...] = ((centred - normed * along) * scaled).reshape(rows, cols, chans)
-
-def pair_back(pair, grad, bias_weight, step=16):
-    rows, cols, chans = pair.shape
+    grad = (grad * scaled_ref[...][None]).reshape(heads, rows * cols)
+    high, low = halves(grad)
+    weight = w_ref[...].astype(F32)
+    w_high, w_low = halves(weight - jnp.mean(weight, axis=1, keepdims=True))
+    both = jnp.concatenate([high, low, high, low], axis=0)
+    weight = jnp.concatenate([w_high, w_high, w_low, w_low], axis=0)
+    centred = lax.dot_general(both, weight, (((0,), (0,)), ((), ())), preferred_element_type=F32)
+    normed = normed_ref[...].reshape(rows * cols, chans)
+    along = jnp.mean(centred * normed, axis=-1, keepdims=True)
+    out_ref[...] = (centred - normed * along).reshape(rows, cols, chans)
+
+def pair_back(stats, grad, bias_weight, step=16):
+    normed, scaled = stats
+    rows, cols, chans = normed.shape
     heads, parts = grad.shape[:2]
     return pl.pallas_call(
         back_kernel, grid=(rows // step,),
         in_specs=[pl.BlockSpec((step, cols, chans), lambda i: (i, 0, 0)),
+                  pl.BlockSpec((step, cols), lambda i: (i, 0)),
                   pl.BlockSpec((heads, parts, step, cols), lambda i: (0, 0, i, 0)),
                   pl.BlockSpec((heads, chans), lambda i: (0, 0))],
         out_specs=pl.BlockSpec((step, cols, chans), lambda i: (i, 0, 0)),
         out_shape=jax.ShapeDtypeStruct((rows, cols, chans), F32),
         compiler_params=pltpu.CompilerParams(dimension_semantics=("arbitrary",), vmem_limit_bytes=60 << 20),
-    )(pair, grad, bias_weight.T)
+    )(normed, scaled, grad, bias_weight.T)
 
 def project_kernel(core_ref, single_ref, got_ref, cot_ref, gotc_ref, w_ref, packed_ref, tokens_ref, normed, cotan):
     half, block, width = tokens_ref.shape
@@ -178,82 +202,94 @@
         compiler_params=pltpu.CompilerParams(dimension_semantics=("arbitrary",), vmem_limit_bytes=60 << 20),
     )(core, tokens, attended_t, w_out, w_gate_up, w_gate_up, w_down)
 
-
-def attend_kernel(n_col, n_chip, n_samp, size, span, unroll, c_ref, blk_ref, *refs):
+def split(v):
+    high = v.astype(BF).astype(F32)
+    return high, v - high
+
+def attend_kernel(n_col, n_chip, per, size, c_ref, blk_ref, *refs):
     bias_refs = refs[: n_col // 2]
     att_ref = refs[n_col // 2]
     out_refs = refs[n_col // 2 + 1 : n_col + 1]
     bias2, acc, kt, vt = refs[n_col + 1 :]
-    side = c_ref[0] // (n_col // 2)
-    samp = pl.program_id(0)
+    step = pl.program_id(0)
     me = c_ref[0]
-    block = blk_ref.shape[2]
+    side = me // (n_col // 2)
+    block = blk_ref.shape[3]
     wide = block * n_col
-
-    @pl.when(samp == 0)
+    rest = block - 2 * size
+
+    @pl.when(step == 0)
     def _():
         for k in range(n_col):
             far = jnp.bitwise_xor(side, k // (n_col // 2))
             part = bias_refs[k % (n_col // 2)][:, far]
             part = part.astype(F32).reshape(bias2.shape[0], block)
             bias2[:, k * block : (k + 1) * block] = part * LOG2E
-        acc[...] = jnp.zeros_like(acc)
-        rest = block - 2 * size
-        kt[2 * size :, :] = jnp.zeros((rest, wide), BF)
         row = lax.broadcasted_iota(jnp.int32, (rest, wide), 0)
-        vt[2 * size :, :] = jnp.where(row < 3, 1.0, 0.0).astype(BF)
-
-    for k in range(n_col):
-        owner = jnp.bitwise_xor(me, k)
-        cols = slice(k * block, (k + 1) * block)
-        keys = blk_ref[owner, size : 2 * size, :]
-        kt[:size, cols] = keys
-        kt[size : 2 * size, cols] = keys
-        vals = blk_ref[owner, 2 * size : 3 * size, :]
-        vt[:size, cols] = vals
-        vt[size : 2 * size, cols] = vals
+        for h in range(2):
+            kt[h, 2 * size :, :] = jnp.zeros((rest, wide), BF)
+            vt[h, 2 * size :, :] = jnp.where(row < 3, 1.0, 0.0).astype(BF)
 
     scale = LOG2E / math.sqrt(size)
-    rest = block - 2 * size
     row = lax.broadcasted_iota(jnp.int32, (rest, block), 0)
 
-    def split(v):
-        high = v.astype(BF).astype(F32)
-        return high, v - high
-
-    def one_block(b, carry):
-        rows = pl.ds(pl.multiple_of(b * (block * span), block * span), block * span)
+    def prepare(h):
+        for k in range(n_col):
+            owner = jnp.bitwise_xor(me, k)
+            cols = slice(k * block, (k + 1) * block)
+            keys = blk_ref[owner, h, size : 2 * size, :]
+            kt[h, :size, cols] = keys
+            kt[h, size : 2 * size, cols] = keys
+            vals = blk_ref[owner, h, 2 * size : 3 * size, :]
+            vt[h, :size, cols] = vals
+            vt[h, size : 2 * size, cols] = vals
         lhs = []
-        for i in range(span):
-            high, low = split(blk_ref[b * span + i, :size, :].astype(F32) * scale)
+        for b in range(n_chip):
+            high, low = split(blk_ref[b, h, :size, :].astype(F32) * scale)
             lhs.append(jnp.concatenate([high, low, jnp.zeros((rest, block), F32)], axis=0).T.astype(BF))
-        lhs = jnp.concatenate(lhs, axis=0) if span > 1 else lhs[0]
-        scores = jnp.dot(lhs, kt[...], preferred_element_type=F32) + bias2[rows, :]
+        return jnp.concatenate(lhs, axis=0)
+
+    def softmax(h, lhs):
+        scores = jnp.dot(lhs, kt[h], preferred_element_type=F32) + bias2[...]
         top = jnp.max(scores, axis=1, keepdims=True)
-        probs = jnp.exp2(scores - top)
+        return jnp.exp2(scores - top)
+
+    def mix(h, probs):
         mixed = lax.dot_general(
-            probs.astype(BF), vt[...], (((1,), (1,)), ((), ())), preferred_element_type=F32
+            probs.astype(BF), vt[h], (((1,), (1,)), ((), ())), preferred_element_type=F32
         )
-        lhs2 = []
-        for i in range(span):
-            mixed_t = mixed[i * block : (i + 1) * block].T
+        lhs = []
+        for b in range(n_chip):
+            mixed_t = mixed[b * block : (b + 1) * block].T
             inv = 1.0 / mixed_t[2 * size : 2 * size + 1]
             att = mixed_t[:size] * inv
-            att_ref[b * span + i, :, :] = att.astype(BF)
-            cotan = blk_ref[b * span + i, 3 * size :, :].astype(F32)
+            att_ref[b, h, :, :] = att.astype(BF)
+            cotan = blk_ref[b, h, 3 * size :, :].astype(F32)
             delta = -jnp.sum(cotan * att, axis=0, keepdims=True) * inv
             high, low = split(cotan * inv)
             d0, rem = split(delta)
             d1, d2 = split(rem)
             tail = jnp.where(row == 0, d0, jnp.where(row == 1, d1, jnp.where(row == 2, d2, 0.0)))
-            lhs2.append(jnp.concatenate([high, low, tail], axis=0).T.astype(BF))
-        lhs2 = jnp.concatenate(lhs2, axis=0) if span > 1 else lhs2[0]
-        acc[rows, :] += probs * jnp.dot(lhs2, vt[...], preferred_element_type=F32)
-        return carry
-
-    lax.fori_loop(0, n_chip // span, one_block, 0, unroll=unroll)
-
-    @pl.when(samp == n_samp - 1)
+            lhs.append(jnp.concatenate([high, low, tail], axis=0).T.astype(BF))
+        return jnp.concatenate(lhs, axis=0)
+
+    def grad(h, probs, lhs):
+        return probs * jnp.dot(lhs, vt[h], preferred_element_type=F32)
+
+    lhs = [prepare(h) for h in range(2)]
+    probs = [softmax(h, lhs[h]) for h in range(2)]
+    lhs = [mix(h, probs[h]) for h in range(2)]
+    term = grad(0, probs[0], lhs[0]) + grad(1, probs[1], lhs[1])
+
+    @pl.when(step == 0)
+    def _():
+        acc[...] = term
+
+    @pl.when(step > 0)
+    def _():
+        acc[...] += term
+
+    @pl.when(step == per - 1)
     def _():
         for k in range(n_col):
             part = acc[:, k * block : (k + 1) * block].astype(BF)
@@ -262,7 +298,7 @@
             out_ref[:, far] = part.reshape(out_ref.shape[0], out_ref.shape[2], block)
 
 
-def attend(me, qkvc, biases, n_samp, size, span=1, unroll=1):
+def attend(me, qkvc, biases, n_samp, size, limit=56):
     n_chip, _, _, lanes = qkvc.shape
     per = n_samp // 2
     block = lanes // per
@@ -271,25 +307,25 @@
     wide = n_col * block
     parts = biases[0].shape
     whole = pl.BlockSpec(parts, lambda s, c: (0, 0, 0, 0))
-    spec = lambda feats: pl.BlockSpec((n_chip, None, feats, block), lambda s, c: (0, s // per, 0, s % per))
-    return pl.pallas_call(
-        functools.partial(attend_kernel, n_col, n_chip, n_samp, size, span, unroll),
+    spec = lambda feats: pl.BlockSpec((n_chip, 2, feats, block), lambda s, c: (0, 0, 0, s))
+    return pl.pallas_call(
+        functools.partial(attend_kernel, n_col, n_chip, per, size),
         grid_spec=pltpu.PrefetchScalarGridSpec(
             num_scalar_prefetch=1,
-            grid=(n_samp,),
+            grid=(per,),
             in_specs=[spec(4 * size)] + [whole] * len(biases),
             out_specs=[spec(size)] + [whole] * len(biases),
             scratch_shapes=[
                 pltpu.VMEM((tokens, wide), F32),
                 pltpu.VMEM((tokens, wide), F32),
-                pltpu.VMEM((block, wide), BF),
-                pltpu.VMEM((block, wide), BF),
+                pltpu.VMEM((2, block, wide), BF),
+                pltpu.VMEM((2, block, wide), BF),
             ],
         ),
         out_shape=[jax.ShapeDtypeStruct((n_chip, 2, size, lanes), BF)]
         + [jax.ShapeDtypeStruct(parts, BF)] * len(biases),
         compiler_params=pltpu.CompilerParams(
-            dimension_semantics=("arbitrary",), vmem_limit_bytes=56 * 1024 * 1024
+            dimension_semantics=("arbitrary",), vmem_limit_bytes=limit * 1024 * 1024
         ),
     )(me, qkvc, *biases)
 
@@ -312,13 +348,16 @@
     share = lambda v: lax.all_to_all(
         v.reshape(2 * n_row, rows, pair.shape[1]), ("row", "col"), 0, 0, tiled=True, axis_index_groups=groups
     ).reshape(n_row, 2, rows, pair.shape[1])
-    bias = share(pair_bias(pair, bias_weight, 16))
+    bias = share(pair_bias(pair, bias_weight, 32))
     packed, tokens = project(core.reshape(1), single, got, cotangent, got_cot, w_qkv, heads)
     biases = [bias] + [lax.ppermute(bias, "col", flip(k)) for k in range(1, n_col // 2)]
 
+    later, _ = lax.optimization_barrier((pair, bias))
+    stats = pair_stats(later, 16)
     packed = lax.all_to_all(packed, "row", 0, 0, tiled=True)
+    packed, stats = lax.optimization_barrier((packed, stats))
     packed = packed.reshape(n_chip, 2, 4 * size, half * block)
-    attended, *grads = attend(me, packed, biases, samp, size, n_chip)
+    attended, *grads = attend(me, packed, biases, samp, size)
     grads = [grads[0]] + [lax.ppermute(grads[k], "col", flip(k)) for k in range(1, n_col // 2)]
     attended = attended.reshape(n_row, size, half * block)
     attended = lax.all_to_all(attended, "row", 0, 0, tiled=True)
@@ -333,7 +372,7 @@
     mine, theirs, total = lax.optimization_barrier((mine, theirs, total))
     got = lax.ppermute(theirs, "row", cores)
     updated = jnp.concatenate([jnp.where(core == 0, mine, got), jnp.where(core == 0, got, mine)], axis=0)
-    pair_grad = pair_back(pair, total, bias_weight, 16)
+    pair_grad = pair_back(stats, total, bias_weight, 32)
     return (updated, pair_grad)
 
 

time: 147 us -> 139 us (0.946)
  waiting for transfers between devices: 45.8 us -> 40.3 us
  Pallas kernels: 54.5 us -> 52.3 us
    ppermute x3, waiting for transfers between devices: 25.3 us -> 0.01 us  [shards(): lax.ppermute(bias, 'col', flip(k))]
    all_to_all x1, waiting for transfers between devices: 2.07 us -> 21.7 us  [shards(): packed = lax.all_to_all(packed, 'row', 0, 0, tiled=True)]
    pallas_call x1, Pallas kernels: 7.66 us -> 5.24 us  [pair_back(): pl.pallas_call(back_kernel, grid=(rows // step,), in_specs=[pl.BlockSpec(...]
    pallas_call x1 -> x2, Pallas kernels: 23.4 us -> 24.4 us  [the longest x1 18.8 us: attend(): pl.pallas_call(functools.partial(attend_kernel, n_col, n_chip, per, size)...]
  transfers between devices with their start and end apart: 13 -> 13, of which waited for: 8 -> 5; matrix products, arithmetic and copies ran while one was open for 2% -> 2% of each run, Pallas kernels for 21% -> 24%
where the time goes in v5:
time: 139 us; the launch traced here: 138 us
  Pallas kernels  52.3 us (38%)
  waiting for transfers between devices  40.3 us (29%)
  starting transfers between devices  39.2 us (28%)
  other arithmetic  3.11 us (2%)
  local copies, waits for them, and re-layouts  2.57 us (2%)
    all_to_all x1, waiting for transfers between devices, shards(): packed = lax.all_to_all(packed, 'row', 0, 0, tiled=True)  21.7 us
    pallas_call x1, Pallas kernels, attend(): pl.pallas_call(functools.partial(attend_kernel, n_col, n_chip, per, size)...  18.8 us
    all_to_all x2, starting transfers between devices, shards(): lax.all_to_all(v.reshape(2 * n_row, rows, pair.shape[1]), ('row', 'col'),...  16.6 us
    ppermute x3, waiting for transfers between devices, shards(): lax.ppermute(grads[k], 'col', flip(k))  15.4 us
    pallas_call x1, Pallas kernels, transition(): pl.pallas_call(transition_kernel, grid_spec=pltpu.PrefetchScalarGridSpec(...  9.42 us
    pallas_call x1, Pallas kernels, project(): pl.pallas_call(project_kernel, grid_spec=pltpu.PrefetchScalarGridSpec(num...  8.6 us
    all_to_all x1, starting transfers between devices, shards(): attended = lax.all_to_all(attended, 'row', 0, 0, tiled=True)  7.03 us
    all_to_all x1, starting transfers between devices, shards(): packed = lax.all_to_all(packed, 'row', 0, 0, tiled=True)  5.79 us
  transfers between devices with their start and end apart: 13, of which 5 were waited for; matrix products, arithmetic and copies ran while one was open for 2% of the time, Pallas kernels for 24%

profile of v5, /device:TPU:1, one launch (start us, length us, event | category | flops | bytes accessed | tf_op | source)
XLA Modules:
  0.0 138.2 jit_solution(561895050925153277)
XLA Ops:
  0.6 1.5 %collective-permute-start = (bf16[6,64,768]{2,1,0:T(8,128)(2,1)}, bf16[6,64,768]{2,1,0:T(8,128)(2,1)S(1)}, u32[]{:S(2)}, u32[]{:S(2)}) collective-permute-start(bf16[6,64,768]{2,1,0:T(8,128)(2,1)} %single_ref.1), channel_id=1, source_target_pairs={{0,8},{8,0},{16,24},{24,16},{32,40},{40,32},{48,56},{56,48},{64,72... | collective-permute-start | bytes 1769480 | tf_op jit(solution)/shard_map/ppermute | solution.py:345
  2.1 0.1 collective-permute-start.1
  2.2 4.6 %shard_map.96 = bf16[16,2,64,128]{3,2,1,0:T(8,128)(2,1)} custom-call(bf16[64,128,128]{2,1,0:T(8,128)(2,1)} %pair_ref.2, bf16[16,128]{1,0:T(8,128)(2,1)} %bitcast.19), custom_call_target="tpu_custom_call" | custom-call | tf_op jit(solution)/shard_map/pallas_call | solution.py:45
  6.9 8.4 %all-to-all-start.1 = ((bf16[32,64,128]{2,1,0:T(8,128)(2,1)}), bf16[32,64,128]{2,1,0:T(8,128)(2,1)S(1)}, u32[]{:S(2)}, u32[]{:S(2)}) async-start(bf16[32,64,128]{2,1,0:T(8,128)(2,1)} %bitcast.16), calls=%async_computation.1 | async-start | bytes 1048576 | tf_op jit(solution)/shard_map/all_to_all | solution.py:348
  15.3 0.0 collective-permute-done.got_ref
  15.3 0.0 copy-start.4
  15.3 0.8 copy-done.4
  16.1 0.2 copy-done.5
  16.3 8.6 %shard_map.95 = (bf16[16,192,384]{2,1,0:T(8,128)(2,1)}, bf16[3,128,768]{2,1,0:T(8,128)(2,1)}) custom-call(s32[1]{0:T(128)} %bitcast.core_ref, bf16[6,64,768]{2,1,0:T(8,128)(2,1)} %single_ref.1, bf16[6,64,768]{2,1,0:T(8,128)(2,1)} %copy-done.4, bf16[6,64,768]{2,1,0:T(8,128)(2,1)} %cot_ref.1, bf16[6,64,768]{2,1,0:T(8,128)(2,1)} %copy-done.5, ...), custom_call_target="tpu_custom_call" | custom-call | tf_op jit(solution)/shard_map/pallas_call | solution.py:140
  24.9 1.5 %all-to-all-done.1 = bf16[32,64,128]{2,1,0:T(8,128)(2,1)S(1)} async-done(((bf16[32,64,128]{2,1,0:T(8,128)(2,1)}), bf16[32,64,128]{2,1,0:T(8,128)(2,1)S(1)}, u32[]{:S(2)}, u32[]{:S(2)}) %all-to-all-start.1) | async-done | bytes 524320 | tf_op jit(solution)/shard_map/all_to_all | solution.py:348
  26.4 5.8 %all-to-all-start = ((bf16[16,192,384]{2,1,0:T(8,128)(2,1)}), bf16[16,192,384]{2,1,0:T(8,128)(2,1)S(1)}, u32[]{:S(2)}, u32[]{:S(2)}) async-start(bf16[16,192,384]{2,1,0:T(8,128)(2,1)} %get-tuple-element.23), calls=%async_computation | async-start | bytes 4718592 | tf_op jit(solution)/shard_map/all_to_all | solution.py:357
  32.2 1.3 collective-permute-start.2
  33.5 2.6 %collective-permute-start.3 = (bf16[16,2,64,128]{3,2,1,0:T(8,128)(2,1)S(1)}, bf16[16,2,64,128]{3,2,1,0:T(8,128)(2,1)}, u32[]{:S(2)}, u32[]{:S(2)}) collective-permute-start(bf16[16,2,64,128]{3,2,1,0:T(8,128)(2,1)S(1)} %bitcast.13), channel_id=1, source_target_pairs={{0,2},{1,3},{2,0},{3,1},{4,6},{5,7},{6,4},{7,5},{8,10},{9,11},{10,... | collective-permute-start | bytes 1572872 | tf_op jit(solution)/shard_map/ppermute | solution.py:353
  36.1 0.0 collective-permute-start.4
  36.1 5.6 %shard_map.97 = (f32[64,128,128]{2,1,0:T(8,128)}, f32[64,128]{1,0:T(8,128)}) custom-call(bf16[64,128,128]{2,1,0:T(8,128)(2,1)} %pair_ref.2), custom_call_target="tpu_custom_call" | custom-call | tf_op jit(solution)/shard_map/pallas_call | solution.py:64
  41.7 21.7 %all-to-all-done = bf16[16,192,384]{2,1,0:T(8,128)(2,1)S(1)} async-done(((bf16[16,192,384]{2,1,0:T(8,128)(2,1)}), bf16[16,192,384]{2,1,0:T(8,128)(2,1)S(1)}, u32[]{:S(2)}, u32[]{:S(2)}) %all-to-all-start) | async-done | bytes 2359328 | tf_op jit(solution)/shard_map/all_to_all | solution.py:357
  63.5 1.4 copy-done
  64.9 0.2 copy-done.6
  65.0 18.8 %shard_map.98 = (bf16[8,2,48,384]{3,2,1,0:T(8,128)(2,1)}, bf16[16,2,64,128]{3,2,1,0:T(8,128)(2,1)}, bf16[16,2,64,128]{3,2,1,0:T(8,128)(2,1)}, bf16[16,2,64,128]{3,2,1,0:T(8,128)(2,1)}, bf16[16,2,64,128]{3,2,1,0:T(8,128)(2,1)}) custom-call(s32[1]{0:T(128)} %bitcast.1.c_ref, bf16[8,2,192,384]{3,2,1,0:T(8,128)(2,1)} %bitcast.10, ...), custom_call_target="tpu_custom_call" | custom-call | tf_op jit(solution)/shard_map/pallas_call | solution.py:311
  83.8 2.7 %collective-permute-start.7 = (bf16[16,2,64,128]{3,2,1,0:T(8,128)(2,1)}, bf16[16,2,64,128]{3,2,1,0:T(8,128)(2,1)S(1)}, u32[]{:S(2)}, u32[]{:S(2)}) collective-permute-start(bf16[16,2,64,128]{3,2,1,0:T(8,128)(2,1)} %get-tuple-element.32), channel_id=1, source_target_pairs={{0,3},{1,2},{2,1},{3,0},{4,7},{5,6},{6,5},{7,4},{8,11},{9,10},{10,... | collective-permute-start | bytes 1572872 | tf_op jit(solution)/shard_map/ppermute | solution.py:361
  86.6 0.3 collective-permute-start.6
  86.9 0.3 collective-permute-start.5
  87.2 7.0 %all-to-all-start.2 = ((bf16[16,48,384]{2,1,0:T(8,128)(2,1)}), bf16[16,48,384]{2,1,0:T(8,128)(2,1)S(1)}, u32[]{:S(2)}, u32[]{:S(2)}) async-start(bf16[16,48,384]{2,1,0:T(8,128)(2,1)} %bitcast.18), calls=%async_computation.2 | async-start | bytes 1179648 | tf_op jit(solution)/shard_map/all_to_all | solution.py:363
  94.3 15.1 %collective-permute-done.7 = bf16[16,2,64,128]{3,2,1,0:T(8,128)(2,1)S(1)} collective-permute-done((bf16[16,2,64,128]{3,2,1,0:T(8,128)(2,1)}, bf16[16,2,64,128]{3,2,1,0:T(8,128)(2,1)S(1)}, u32[]{:S(2)}, u32[]{:S(2)}) %collective-permute-start.7) | collective-permute-done | bytes 524320 | tf_op jit(solution)/shard_map/ppermute | solution.py:361
  109.3 0.3 collective-permute-done.5
  109.7 2.2 %add_convert_fusion = bf16[16,2,64,128]{3,2,1,0:T(8,128)(2,1)} fusion(bf16[16,2,64,128]{3,2,1,0:T(8,128)(2,1)S(1)} %collective-permute-done.7, bf16[16,2,64,128]{3,2,1,0:T(8,128)(2,1)S(1)} %collective-permute-done.6, bf16[16,2,64,128]{3,2,1,0:T(8,128)(2,1)S(1)} %collective-permute-done.5, bf16[16,2,64,128]{3,2,1,0:T(8,128)(2,1)} %get-tuple-element.29), kind=kLoop, calls=%fused_computation | loop fusion | flops 2097152 | bytes 2621440 | tf_op jit(solution)/shard_map/convert_element_type | solution.py:367
  111.9 8.2 %all-to-all-start.3 = ((bf16[32,64,128]{2,1,0:T(8,128)(2,1)}), bf16[32,64,128]{2,1,0:T(8,128)(2,1)S(1)}, u32[]{:S(2)}, u32[]{:S(2)}) async-start(bf16[32,64,128]{2,1,0:T(8,128)(2,1)} %bitcast.8), calls=%async_computation.3 | async-start | bytes 1048576 | tf_op jit(solution)/shard_map/all_to_all | solution.py:348
  120.1 9.4 %shard_map.99 = (bf16[3,64,768]{2,1,0:T(8,128)(2,1)}, bf16[3,64,768]{2,1,0:T(8,128)(2,1)}) custom-call(s32[1]{0:T(128)} %bitcast.core_ref, bf16[3,128,768]{2,1,0:T(8,128)(2,1)} %get-tuple-element.22.tokens_ref, bf16[768,384]{1,0:T(8,128)(2,1)} %bitcast.11, bf16[768,768]{1,0:T(8,128)(2,1)} %wo_ref.1, bf16[768,3072]{1,0:T(8,128)(2,1)} %wu_ref.1, ...), custom_call_target="tpu_custom_call" | custom-call | tf_op jit(solution)/shard_map/pallas_call | solution.py:187
  129.5 1.7 %all-to-all-done.3 = bf16[32,64,128]{2,1,0:T(8,128)(2,1)S(1)} async-done(((bf16[32,64,128]{2,1,0:T(8,128)(2,1)}), bf16[32,64,128]{2,1,0:T(8,128)(2,1)S(1)}, u32[]{:S(2)}, u32[]{:S(2)}) %all-to-all-start.3) | async-done | bytes 524320 | tf_op jit(solution)/shard_map/all_to_all | solution.py:348
  131.2 0.9 collective-permute-start.8
  132.1 5.2 %shard_map.100 = f32[64,128,128]{2,1,0:T(8,128)} custom-call(f32[64,128,128]{2,1,0:T(8,128)} %get-tuple-element.39.normed_ref, f32[64,128]{1,0:T(8,128)} %get-tuple-element.40.scaled_ref, bf16[16,2,64,128]{3,2,1,0:T(8,128)(2,1)} %bitcast.17, bf16[16,128]{1,0:T(8,128)(2,1)} %bitcast.20), custom_call_target="tpu_custom_call" | custom-call | tf_op jit(solution)/shard_map/pallas_call | solution.py:93
  137.4 0.9 pad_maximum_fusion
  (19 shorter events, 0.1 us)
Async XLA Ops:
  0.6 14.7 %collective-permute-start = (bf16[6,64,768]{2,1,0:T(8,128)(2,1)}, bf16[6,64,768]{2,1,0:T(8,128)(2,1)S(1)}, u32[]{:S(2)}, u32[]{:S(2)}) collective-permute-start(bf16[6,64,768]{2,1,0:T(8,128)(2,1)} %single_ref.1), channel_id=1, source_target_pairs={{0,8},{8,0},{16,24},{24,16},{32,40},{40,32},{48,56},{56,48},{64,72... | collective-permute-start | bytes 1769480 | tf_op jit(solution)/shard_map/ppermute | solution.py:345
  2.1 13.2 %collective-permute-start.1 = (bf16[6,64,768]{2,1,0:T(8,128)(2,1)}, bf16[6,64,768]{2,1,0:T(8,128)(2,1)S(1)}, u32[]{:S(2)}, u32[]{:S(2)}) collective-permute-start(bf16[6,64,768]{2,1,0:T(8,128)(2,1)} %cot_ref.1), channel_id=1, source_target_pairs={{0,8},{8,0},{16,24},{24,16},{32,40},{40,32},{48,56},{56,48},{64,72... | collective-permute-start | bytes 1769480 | tf_op jit(solution)/shard_map/ppermute | solution.py:346
  6.9 19.5 %all-to-all-start.1 = ((bf16[32,64,128]{2,1,0:T(8,128)(2,1)}), bf16[32,64,128]{2,1,0:T(8,128)(2,1)S(1)}, u32[]{:S(2)}, u32[]{:S(2)}) async-start(bf16[32,64,128]{2,1,0:T(8,128)(2,1)} %bitcast.16), calls=%async_computation.1 | async-start | bytes 1048576 | tf_op jit(solution)/shard_map/all_to_all | solution.py:348
  15.3 0.8 copy-start.4
  15.3 1.0 copy-start.5
  26.4 9.7 %copy-start.2 = (bf16[32,64,128]{2,1,0:T(8,128)(2,1)}, bf16[32,64,128]{2,1,0:T(8,128)(2,1)S(1)}, u32[]{:S(2)}) copy-start(bf16[32,64,128]{2,1,0:T(8,128)(2,1)S(1)} %all-to-all-done.1) | copy-start | bytes 1572868
  26.4 37.0 %all-to-all-start = ((bf16[16,192,384]{2,1,0:T(8,128)(2,1)}), bf16[16,192,384]{2,1,0:T(8,128)(2,1)S(1)}, u32[]{:S(2)}, u32[]{:S(2)}) async-start(bf16[16,192,384]{2,1,0:T(8,128)(2,1)} %get-tuple-element.23), calls=%async_computation | async-start | bytes 4718592 | tf_op jit(solution)/shard_map/all_to_all | solution.py:357
  32.2 31.3 %collective-permute-start.2 = (bf16[16,2,64,128]{3,2,1,0:T(8,128)(2,1)S(1)}, bf16[16,2,64,128]{3,2,1,0:T(8,128)(2,1)S(1)}, u32[]{:S(2)}, u32[]{:S(2)}) collective-permute-start(bf16[16,2,64,128]{3,2,1,0:T(8,128)(2,1)S(1)} %bitcast.12), channel_id=1, source_target_pairs={{0,1},{1,0},{2,3},{3,2},{4,5},{5,4},{6,7},{7,6},{8,9},{9,8},{10,11... | collective-permute-start | bytes 1572872 | tf_op jit(solution)/shard_map/ppermute | solution.py:353
  33.5 30.0 %collective-permute-start.3 = (bf16[16,2,64,128]{3,2,1,0:T(8,128)(2,1)S(1)}, bf16[16,2,64,128]{3,2,1,0:T(8,128)(2,1)}, u32[]{:S(2)}, u32[]{:S(2)}) collective-permute-start(bf16[16,2,64,128]{3,2,1,0:T(8,128)(2,1)S(1)} %bitcast.13), channel_id=1, source_target_pairs={{0,2},{1,3},{2,0},{3,1},{4,6},{5,7},{6,4},{7,5},{8,10},{9,11},{10,... | collective-permute-start | bytes 1572872 | tf_op jit(solution)/shard_map/ppermute | solution.py:353
  36.1 27.4 %collective-permute-start.4 = (bf16[16,2,64,128]{3,2,1,0:T(8,128)(2,1)S(1)}, bf16[16,2,64,128]{3,2,1,0:T(8,128)(2,1)}, u32[]{:S(2)}, u32[]{:S(2)}) collective-permute-start(bf16[16,2,64,128]{3,2,1,0:T(8,128)(2,1)S(1)} %bitcast.14), channel_id=1, source_target_pairs={{0,3},{1,2},{2,1},{3,0},{4,7},{5,6},{6,5},{7,4},{8,11},{9,10},{10,... | collective-permute-start | bytes 1572872 | tf_op jit(solution)/shard_map/ppermute | solution.py:353
  63.5 1.4 %copy-start = (bf16[16,192,384]{2,1,0:T(8,128)(2,1)}, bf16[16,192,384]{2,1,0:T(8,128)(2,1)S(1)}, u32[]{:S(2)}) copy-start(bf16[16,192,384]{2,1,0:T(8,128)(2,1)S(1)} %all-to-all-done) | copy-start | bytes 7077892
  63.5 1.6 %copy-start.6 = (bf16[16,2,64,128]{3,2,1,0:T(8,128)(2,1)}, bf16[16,2,64,128]{3,2,1,0:T(8,128)(2,1)S(1)}, u32[]{:S(2)}) copy-start(bf16[16,2,64,128]{3,2,1,0:T(8,128)(2,1)S(1)} %collective-permute-done.2.refs_1_) | copy-start | bytes 1572868
  83.8 25.5 %collective-permute-start.7 = (bf16[16,2,64,128]{3,2,1,0:T(8,128)(2,1)}, bf16[16,2,64,128]{3,2,1,0:T(8,128)(2,1)S(1)}, u32[]{:S(2)}, u32[]{:S(2)}) collective-permute-start(bf16[16,2,64,128]{3,2,1,0:T(8,128)(2,1)} %get-tuple-element.32), channel_id=1, source_target_pairs={{0,3},{1,2},{2,1},{3,0},{4,7},{5,6},{6,5},{7,4},{8,11},{9,10},{10,... | collective-permute-start | bytes 1572872 | tf_op jit(solution)/shard_map/ppermute | solution.py:361
  86.6 22.8 %collective-permute-start.6 = (bf16[16,2,64,128]{3,2,1,0:T(8,128)(2,1)}, bf16[16,2,64,128]{3,2,1,0:T(8,128)(2,1)S(1)}, u32[]{:S(2)}, u32[]{:S(2)}) collective-permute-start(bf16[16,2,64,128]{3,2,1,0:T(8,128)(2,1)} %get-tuple-element.31), channel_id=1, source_target_pairs={{0,2},{1,3},{2,0},{3,1},{4,6},{5,7},{6,4},{7,5},{8,10},{9,11},{10,... | collective-permute-start | bytes 1572872 | tf_op jit(solution)/shard_map/ppermute | solution.py:361
  86.9 22.7 %collective-permute-start.5 = (bf16[16,2,64,128]{3,2,1,0:T(8,128)(2,1)}, bf16[16,2,64,128]{3,2,1,0:T(8,128)(2,1)S(1)}, u32[]{:S(2)}, u32[]{:S(2)}) collective-permute-start(bf16[16,2,64,128]{3,2,1,0:T(8,128)(2,1)} %get-tuple-element.30), channel_id=1, source_target_pairs={{0,1},{1,0},{2,3},{3,2},{4,5},{5,4},{6,7},{7,6},{8,9},{9,8},{10,11... | collective-permute-start | bytes 1572872 | tf_op jit(solution)/shard_map/ppermute | solution.py:361
  87.2 24.6 %all-to-all-start.2 = ((bf16[16,48,384]{2,1,0:T(8,128)(2,1)}), bf16[16,48,384]{2,1,0:T(8,128)(2,1)S(1)}, u32[]{:S(2)}, u32[]{:S(2)}) async-start(bf16[16,48,384]{2,1,0:T(8,128)(2,1)} %bitcast.18), calls=%async_computation.2 | async-start | bytes 1179648 | tf_op jit(solution)/shard_map/all_to_all | solution.py:363
  111.9 8.2 %copy-start.1 = (bf16[16,48,384]{2,1,0:T(8,128)(2,1)}, bf16[16,48,384]{2,1,0:T(8,128)(2,1)S(1)}, u32[]{:S(2)}) copy-start(bf16[16,48,384]{2,1,0:T(8,128)(2,1)S(1)} %all-to-all-done.2) | copy-start | bytes 1769476
  111.9 19.3 %all-to-all-start.3 = ((bf16[32,64,128]{2,1,0:T(8,128)(2,1)}), bf16[32,64,128]{2,1,0:T(8,128)(2,1)S(1)}, u32[]{:S(2)}, u32[]{:S(2)}) async-start(bf16[32,64,128]{2,1,0:T(8,128)(2,1)} %bitcast.8), calls=%async_computation.3 | async-start | bytes 1048576 | tf_op jit(solution)/shard_map/all_to_all | solution.py:348
  131.2 0.9 copy-start.3
  131.2 6.1 %collective-permute-start.8 = (bf16[3,64,768]{2,1,0:T(8,128)(2,1)}, bf16[3,64,768]{2,1,0:T(8,128)(2,1)S(1)}, u32[]{:S(2)}, u32[]{:S(2)}) collective-permute-start(bf16[3,64,768]{2,1,0:T(8,128)(2,1)} %get-tuple-element.38), channel_id=1, source_target_pairs={{0,8},{8,0},{16,24},{24,16},{32,40},{40,32},{48,56},{56,48},{64,72... | collective-permute-start | bytes 884744 | tf_op jit(solution)/shard_map/ppermute | solution.py:373
  132.1 5.2 %copy-start.7 = (bf16[3,64,768]{2,1,0:T(8,128)(2,1)S(1)}, bf16[3,64,768]{2,1,0:T(8,128)(2,1)}, u32[]{:S(2)}) copy-start(bf16[3,64,768]{2,1,0:T(8,128)(2,1)} %get-tuple-element.37) | copy-start | bytes 884740

commit v6 on v5

--- a/solution.py
+++ b/solution.py
@@ -33,8 +33,8 @@
     centred = values - jnp.mean(values, axis=-1, keepdims=True)
     weight = w_ref[...]
     flat = across(jnp.concatenate([weight, weight], axis=1), jnp.concatenate(halves(centred), axis=1))
-    ones = jnp.full((8, 2 * chans), 1.0 / chans, BF)
-    variance = across(ones, jnp.concatenate(halves(centred * centred), axis=1))[:1]
+    ones = jnp.full((8, chans), 1.0 / chans, BF)
+    variance = across(ones, (centred * centred).astype(BF))[:1]
     flat = (flat * lax.rsqrt(variance + 1e-05)).reshape(heads, rows, cols).astype(BF)
     out_ref[:, 0] = flat
     out_ref[:, 1] = flat
@@ -298,7 +298,7 @@
             out_ref[:, far] = part.reshape(out_ref.shape[0], out_ref.shape[2], block)
 
 
-def attend(me, qkvc, biases, n_samp, size, limit=56):
+def attend(me, qkvc, biases, n_samp, size, limit=48):
     n_chip, _, _, lanes = qkvc.shape
     per = n_samp // 2
     block = lanes // per

time: 139 us -> 135 us (0.971)
  Pallas kernels: 52.3 us -> 50.7 us
  local copies, waits for them, and re-layouts: 2.57 us -> 1.03 us
    unnamed x16 -> x10, local copies, waits for them, and re-layouts: 2.57 us -> 1.03 us
  transfers between devices with their start and end apart: 13 -> 13, of which waited for: 5 -> 5; matrix products, arithmetic and copies ran while one was open for 2% -> 1% of each run, Pallas kernels for 24% -> 25%
where the time goes in v6:
time: 135 us; the launch traced here: 134 us
  Pallas kernels  50.7 us (38%)
  waiting for transfers between devices  40.3 us (30%)
  starting transfers between devices  39.3 us (29%)
  other arithmetic  2.11 us (2%)
    all_to_all x1, waiting for transfers between devices, shards(): packed = lax.all_to_all(packed, 'row', 0, 0, tiled=True)  21.8 us
    pallas_call x1, Pallas kernels, attend(): pl.pallas_call(functools.partial(attend_kernel, n_col, n_chip, per, size)...  17.7 us
    all_to_all x2, starting transfers between devices, shards(): lax.all_to_all(v.reshape(2 * n_row, rows, pair.shape[1]), ('row', 'col'),...  16.7 us
    ppermute x3, waiting for transfers between devices, shards(): lax.ppermute(grads[k], 'col', flip(k))  15.4 us
    pallas_call x1, Pallas kernels, transition(): pl.pallas_call(transition_kernel, grid_spec=pltpu.PrefetchScalarGridSpec(...  9.43 us
    pallas_call x1, Pallas kernels, project(): pl.pallas_call(project_kernel, grid_spec=pltpu.PrefetchScalarGridSpec(num...  8.59 us
    all_to_all x1, starting transfers between devices, shards(): attended = lax.all_to_all(attended, 'row', 0, 0, tiled=True)  7.06 us
    all_to_all x1, starting transfers between devices, shards(): packed = lax.all_to_all(packed, 'row', 0, 0, tiled=True)  5.79 us
  transfers between devices with their start and end apart: 13, of which 5 were waited for; matrix products, arithmetic and copies ran while one was open for 1% of the time, Pallas kernels for 25%

profile of v6, /device:TPU:1, one launch (start us, length us, event | category | flops | bytes accessed | tf_op | source)
XLA Modules:
  0.0 134.1 jit_solution(8324380161318172887)
XLA Ops:
  0.6 1.5 %collective-permute-start = (bf16[6,64,768]{2,1,0:T(8,128)(2,1)}, bf16[6,64,768]{2,1,0:T(8,128)(2,1)S(1)}, u32[]{:S(2)}, u32[]{:S(2)}) collective-permute-start(bf16[6,64,768]{2,1,0:T(8,128)(2,1)} %single_ref.1), channel_id=1, source_target_pairs={{0,8},{8,0},{16,24},{24,16},{32,40},{40,32},{48,56},{56,48},{64,72... | collective-permute-start | bytes 1769480 | tf_op jit(solution)/shard_map/ppermute | solution.py:345
  2.1 0.1 collective-permute-start.1
  2.2 4.1 %shard_map.96 = bf16[16,2,64,128]{3,2,1,0:T(8,128)(2,1)} custom-call(bf16[64,128,128]{2,1,0:T(8,128)(2,1)} %pair_ref.2, bf16[16,128]{1,0:T(8,128)(2,1)} %bitcast.17), custom_call_target="tpu_custom_call" | custom-call | tf_op jit(solution)/shard_map/pallas_call | solution.py:45
  6.3 8.4 %all-to-all-start.1 = ((bf16[32,64,128]{2,1,0:T(8,128)(2,1)}), bf16[32,64,128]{2,1,0:T(8,128)(2,1)S(1)}, u32[]{:S(2)}, u32[]{:S(2)}) async-start(bf16[32,64,128]{2,1,0:T(8,128)(2,1)} %bitcast.15), calls=%async_computation.1 | async-start | bytes 1048576 | tf_op jit(solution)/shard_map/all_to_all | solution.py:348
  14.7 0.0 collective-permute-done.got_ref
  14.8 0.0 copy-start.2
  14.8 0.8 copy-done.2
  15.6 0.2 copy-done.3
  15.8 8.6 %shard_map.95 = (bf16[16,192,384]{2,1,0:T(8,128)(2,1)}, bf16[3,128,768]{2,1,0:T(8,128)(2,1)}) custom-call(s32[1]{0:T(128)} %bitcast.core_ref, bf16[6,64,768]{2,1,0:T(8,128)(2,1)} %single_ref.1, bf16[6,64,768]{2,1,0:T(8,128)(2,1)} %copy-done.2, bf16[6,64,768]{2,1,0:T(8,128)(2,1)} %cot_ref.1, bf16[6,64,768]{2,1,0:T(8,128)(2,1)} %copy-done.3, ...), custom_call_target="tpu_custom_call" | custom-call | tf_op jit(solution)/shard_map/pallas_call | solution.py:140
  24.4 1.5 %all-to-all-done.1 = bf16[32,64,128]{2,1,0:T(8,128)(2,1)S(1)} async-done(((bf16[32,64,128]{2,1,0:T(8,128)(2,1)}), bf16[32,64,128]{2,1,0:T(8,128)(2,1)S(1)}, u32[]{:S(2)}, u32[]{:S(2)}) %all-to-all-start.1) | async-done | bytes 524320 | tf_op jit(solution)/shard_map/all_to_all | solution.py:348
  25.8 5.8 %all-to-all-start = ((bf16[16,192,384]{2,1,0:T(8,128)(2,1)}), bf16[16,192,384]{2,1,0:T(8,128)(2,1)}, u32[]{:S(2)}, u32[]{:S(2)}) async-start(bf16[16,192,384]{2,1,0:T(8,128)(2,1)} %get-tuple-element.23), calls=%async_computation | async-start | bytes 4718592 | tf_op jit(solution)/shard_map/all_to_all | solution.py:357
  31.6 1.3 collective-permute-start.2
  32.9 2.6 %collective-permute-start.3 = (bf16[16,2,64,128]{3,2,1,0:T(8,128)(2,1)S(1)}, bf16[16,2,64,128]{3,2,1,0:T(8,128)(2,1)S(1)}, u32[]{:S(2)}, u32[]{:S(2)}) collective-permute-start(bf16[16,2,64,128]{3,2,1,0:T(8,128)(2,1)S(1)} %bitcast.11), channel_id=1, source_target_pairs={{0,2},{1,3},{2,0},{3,1},{4,6},{5,7},{6,4},{7,5},{8,10},{9,11},{10,... | collective-permute-start | bytes 1572872 | tf_op jit(solution)/shard_map/ppermute | solution.py:353
  35.6 0.0 collective-permute-start.4
  35.6 5.6 %shard_map.97 = (f32[64,128,128]{2,1,0:T(8,128)}, f32[64,128]{1,0:T(8,128)}) custom-call(bf16[64,128,128]{2,1,0:T(8,128)(2,1)} %pair_ref.2), custom_call_target="tpu_custom_call" | custom-call | tf_op jit(solution)/shard_map/pallas_call | solution.py:64
  41.2 21.8 %all-to-all-done = bf16[16,192,384]{2,1,0:T(8,128)(2,1)} async-done(((bf16[16,192,384]{2,1,0:T(8,128)(2,1)}), bf16[16,192,384]{2,1,0:T(8,128)(2,1)}, u32[]{:S(2)}, u32[]{:S(2)}) %all-to-all-start) | async-done | bytes 2359328 | tf_op jit(solution)/shard_map/all_to_all | solution.py:357
  63.0 0.0 collective-permute-done.2.refs_1_
  63.0 0.0 collective-permute-done.3.refs_2_
  63.0 17.7 %shard_map.98 = (bf16[8,2,48,384]{3,2,1,0:T(8,128)(2,1)}, bf16[16,2,64,128]{3,2,1,0:T(8,128)(2,1)S(1)}, bf16[16,2,64,128]{3,2,1,0:T(8,128)(2,1)S(1)}, bf16[16,2,...) custom-call(s32[1]{0:T(128)} %bitcast.1.c_ref, bf16[8,2,192,384]{3,2,1,0:T(8,128)(2,1)} %bitcast.5.blk_ref, ...), custom_call_target="tpu_custom_call" | custom-call | tf_op jit(solution)/shard_map/pallas_call | solution.py:311
  80.7 2.7 %collective-permute-start.7 = (bf16[16,2,64,128]{3,2,1,0:T(8,128)(2,1)}, bf16[16,2,64,128]{3,2,1,0:T(8,128)(2,1)S(1)}, u32[]{:S(2)}, u32[]{:S(2)}) collective-permute-start(bf16[16,2,64,128]{3,2,1,0:T(8,128)(2,1)} %get-tuple-element.32), channel_id=1, source_target_pairs={{0,3},{1,2},{2,1},{3,0},{4,7},{5,6},{6,5},{7,4},{8,11},{9,10},{10,... | collective-permute-start | bytes 1572872 | tf_op jit(solution)/shard_map/ppermute | solution.py:361
  83.5 0.3 collective-permute-start.6
  83.8 0.3 collective-permute-start.5
  84.1 7.1 %all-to-all-start.2 = ((bf16[16,48,384]{2,1,0:T(8,128)(2,1)}), bf16[16,48,384]{2,1,0:T(8,128)(2,1)S(1)}, u32[]{:S(2)}, u32[]{:S(2)}) async-start(bf16[16,48,384]{2,1,0:T(8,128)(2,1)} %bitcast.6), calls=%async_computation.2 | async-start | bytes 1179648 | tf_op jit(solution)/shard_map/all_to_all | solution.py:363
  91.2 15.1 %collective-permute-done.7 = bf16[16,2,64,128]{3,2,1,0:T(8,128)(2,1)S(1)} collective-permute-done((bf16[16,2,64,128]{3,2,1,0:T(8,128)(2,1)}, bf16[16,2,64,128]{3,2,1,0:T(8,128)(2,1)S(1)}, u32[]{:S(2)}, u32[]{:S(2)}) %collective-permute-start.7) | collective-permute-done | bytes 524320 | tf_op jit(solution)/shard_map/ppermute | solution.py:361
  106.2 0.3 collective-permute-done.5
  106.5 1.2 add_convert_fusion
  107.8 8.2 %all-to-all-start.3 = ((bf16[32,64,128]{2,1,0:T(8,128)(2,1)}), bf16[32,64,128]{2,1,0:T(8,128)(2,1)S(1)}, u32[]{:S(2)}, u32[]{:S(2)}) async-start(bf16[32,64,128]{2,1,0:T(8,128)(2,1)} %bitcast.8), calls=%async_computation.3 | async-start | bytes 1048576 | tf_op jit(solution)/shard_map/all_to_all | solution.py:348
  116.0 9.4 %shard_map.99 = (bf16[3,64,768]{2,1,0:T(8,128)(2,1)}, bf16[3,64,768]{2,1,0:T(8,128)(2,1)}) custom-call(s32[1]{0:T(128)} %bitcast.core_ref, bf16[3,128,768]{2,1,0:T(8,128)(2,1)} %get-tuple-element.22.tokens_ref, bf16[768,384]{1,0:T(8,128)(2,1)} %bitcast.14, bf16[768,768]{1,0:T(8,128)(2,1)} %wo_ref.1, bf16[768,3072]{1,0:T(8,128)(2,1)} %wu_ref.1, ...), custom_call_target="tpu_custom_call" | custom-call | tf_op jit(solution)/shard_map/pallas_call | solution.py:187
  125.4 1.7 %all-to-all-done.3 = bf16[32,64,128]{2,1,0:T(8,128)(2,1)S(1)} async-done(((bf16[32,64,128]{2,1,0:T(8,128)(2,1)}), bf16[32,64,128]{2,1,0:T(8,128)(2,1)S(1)}, u32[]{:S(2)}, u32[]{:S(2)}) %all-to-all-start.3) | async-done | bytes 524320 | tf_op jit(solution)/shard_map/all_to_all | solution.py:348
  127.1 0.9 collective-permute-start.8
  128.0 5.2 %shard_map.100 = f32[64,128,128]{2,1,0:T(8,128)} custom-call(f32[64,128,128]{2,1,0:T(8,128)} %get-tuple-element.39.normed_ref, f32[64,128]{1,0:T(8,128)} %get-tuple-element.40.scaled_ref, bf16[16,2,64,128]{3,2,1,0:T(8,128)(2,1)} %bitcast.16, bf16[16,128]{1,0:T(8,128)(2,1)} %bitcast.18), custom_call_target="tpu_custom_call" | custom-call | tf_op jit(solution)/shard_map/pallas_call | solution.py:93
  133.3 0.9 pad_maximum_fusion
  (13 shorter events, 0.1 us)
Async XLA Ops:
  0.6 14.1 %collective-permute-start = (bf16[6,64,768]{2,1,0:T(8,128)(2,1)}, bf16[6,64,768]{2,1,0:T(8,128)(2,1)S(1)}, u32[]{:S(2)}, u32[]{:S(2)}) collective-permute-start(bf16[6,64,768]{2,1,0:T(8,128)(2,1)} %single_ref.1), channel_id=1, source_target_pairs={{0,8},{8,0},{16,24},{24,16},{32,40},{40,32},{48,56},{56,48},{64,72... | collective-permute-start | bytes 1769480 | tf_op jit(solution)/shard_map/ppermute | solution.py:345
  2.1 12.6 %collective-permute-start.1 = (bf16[6,64,768]{2,1,0:T(8,128)(2,1)}, bf16[6,64,768]{2,1,0:T(8,128)(2,1)S(1)}, u32[]{:S(2)}, u32[]{:S(2)}) collective-permute-start(bf16[6,64,768]{2,1,0:T(8,128)(2,1)} %cot_ref.1), channel_id=1, source_target_pairs={{0,8},{8,0},{16,24},{24,16},{32,40},{40,32},{48,56},{56,48},{64,72... | collective-permute-start | bytes 1769480 | tf_op jit(solution)/shard_map/ppermute | solution.py:346
  6.3 19.5 %all-to-all-start.1 = ((bf16[32,64,128]{2,1,0:T(8,128)(2,1)}), bf16[32,64,128]{2,1,0:T(8,128)(2,1)S(1)}, u32[]{:S(2)}, u32[]{:S(2)}) async-start(bf16[32,64,128]{2,1,0:T(8,128)(2,1)} %bitcast.15), calls=%async_computation.1 | async-start | bytes 1048576 | tf_op jit(solution)/shard_map/all_to_all | solution.py:348
  14.8 0.8 copy-start.2
  14.8 1.0 copy-start.3
  25.8 37.1 %all-to-all-start = ((bf16[16,192,384]{2,1,0:T(8,128)(2,1)}), bf16[16,192,384]{2,1,0:T(8,128)(2,1)}, u32[]{:S(2)}, u32[]{:S(2)}) async-start(bf16[16,192,384]{2,1,0:T(8,128)(2,1)} %get-tuple-element.23), calls=%async_computation | async-start | bytes 4718592 | tf_op jit(solution)/shard_map/all_to_all | solution.py:357
  31.6 31.4 %collective-permute-start.2 = (bf16[16,2,64,128]{3,2,1,0:T(8,128)(2,1)S(1)}, bf16[16,2,64,128]{3,2,1,0:T(8,128)(2,1)S(1)}, u32[]{:S(2)}, u32[]{:S(2)}) collective-permute-start(bf16[16,2,64,128]{3,2,1,0:T(8,128)(2,1)S(1)} %bitcast.10), channel_id=1, source_target_pairs={{0,1},{1,0},{2,3},{3,2},{4,5},{5,4},{6,7},{7,6},{8,9},{9,8},{10,11... | collective-permute-start | bytes 1572872 | tf_op jit(solution)/shard_map/ppermute | solution.py:353
  32.9 30.1 %collective-permute-start.3 = (bf16[16,2,64,128]{3,2,1,0:T(8,128)(2,1)S(1)}, bf16[16,2,64,128]{3,2,1,0:T(8,128)(2,1)S(1)}, u32[]{:S(2)}, u32[]{:S(2)}) collective-permute-start(bf16[16,2,64,128]{3,2,1,0:T(8,128)(2,1)S(1)} %bitcast.11), channel_id=1, source_target_pairs={{0,2},{1,3},{2,0},{3,1},{4,6},{5,7},{6,4},{7,5},{8,10},{9,11},{10,... | collective-permute-start | bytes 1572872 | tf_op jit(solution)/shard_map/ppermute | solution.py:353
  35.6 27.5 %collective-permute-start.4 = (bf16[16,2,64,128]{3,2,1,0:T(8,128)(2,1)S(1)}, bf16[16,2,64,128]{3,2,1,0:T(8,128)(2,1)S(1)}, u32[]{:S(2)}, u32[]{:S(2)}) collective-permute-start(bf16[16,2,64,128]{3,2,1,0:T(8,128)(2,1)S(1)} %bitcast.12), channel_id=1, source_target_pairs={{0,3},{1,2},{2,1},{3,0},{4,7},{5,6},{6,5},{7,4},{8,11},{9,10},{10,... | collective-permute-start | bytes 1572872 | tf_op jit(solution)/shard_map/ppermute | solution.py:353
  80.7 25.5 %collective-permute-start.7 = (bf16[16,2,64,128]{3,2,1,0:T(8,128)(2,1)}, bf16[16,2,64,128]{3,2,1,0:T(8,128)(2,1)S(1)}, u32[]{:S(2)}, u32[]{:S(2)}) collective-permute-start(bf16[16,2,64,128]{3,2,1,0:T(8,128)(2,1)} %get-tuple-element.32), channel_id=1, source_target_pairs={{0,3},{1,2},{2,1},{3,0},{4,7},{5,6},{6,5},{7,4},{8,11},{9,10},{10,... | collective-permute-start | bytes 1572872 | tf_op jit(solution)/shard_map/ppermute | solution.py:361
  83.5 22.8 %collective-permute-start.6 = (bf16[16,2,64,128]{3,2,1,0:T(8,128)(2,1)}, bf16[16,2,64,128]{3,2,1,0:T(8,128)(2,1)S(1)}, u32[]{:S(2)}, u32[]{:S(2)}) collective-permute-start(bf16[16,2,64,128]{3,2,1,0:T(8,128)(2,1)} %get-tuple-element.31), channel_id=1, source_target_pairs={{0,2},{1,3},{2,0},{3,1},{4,6},{5,7},{6,4},{7,5},{8,10},{9,11},{10,... | collective-permute-start | bytes 1572872 | tf_op jit(solution)/shard_map/ppermute | solution.py:361
  83.8 22.7 %collective-permute-start.5 = (bf16[16,2,64,128]{3,2,1,0:T(8,128)(2,1)S(1)}, bf16[16,2,64,128]{3,2,1,0:T(8,128)(2,1)S(1)}, u32[]{:S(2)}, u32[]{:S(2)}) collective-permute-start(bf16[16,2,64,128]{3,2,1,0:T(8,128)(2,1)S(1)} %get-tuple-element.30), channel_id=1, source_target_pairs={{0,1},{1,0},{2,3},{3,2},{4,5},{5,4},{6,7},{7,6},{8,9},{9,8},{10,11... | collective-permute-start | bytes 1572872 | tf_op jit(solution)/shard_map/ppermute | solution.py:361
  84.1 23.6 %all-to-all-start.2 = ((bf16[16,48,384]{2,1,0:T(8,128)(2,1)}), bf16[16,48,384]{2,1,0:T(8,128)(2,1)S(1)}, u32[]{:S(2)}, u32[]{:S(2)}) async-start(bf16[16,48,384]{2,1,0:T(8,128)(2,1)} %bitcast.6), calls=%async_computation.2 | async-start | bytes 1179648 | tf_op jit(solution)/shard_map/all_to_all | solution.py:363
  107.7 8.2 %copy-start = (bf16[16,48,384]{2,1,0:T(8,128)(2,1)}, bf16[16,48,384]{2,1,0:T(8,128)(2,1)S(1)}, u32[]{:S(2)}) copy-start(bf16[16,48,384]{2,1,0:T(8,128)(2,1)S(1)} %all-to-all-done.2) | copy-start | bytes 1769476
  107.8 19.3 %all-to-all-start.3 = ((bf16[32,64,128]{2,1,0:T(8,128)(2,1)}), bf16[32,64,128]{2,1,0:T(8,128)(2,1)S(1)}, u32[]{:S(2)}, u32[]{:S(2)}) async-start(bf16[32,64,128]{2,1,0:T(8,128)(2,1)} %bitcast.8), calls=%async_computation.3 | async-start | bytes 1048576 | tf_op jit(solution)/shard_map/all_to_all | solution.py:348
  127.1 0.9 copy-start.1
  127.1 6.1 %collective-permute-start.8 = (bf16[3,64,768]{2,1,0:T(8,128)(2,1)}, bf16[3,64,768]{2,1,0:T(8,128)(2,1)S(1)}, u32[]{:S(2)}, u32[]{:S(2)}) collective-permute-start(bf16[3,64,768]{2,1,0:T(8,128)(2,1)} %get-tuple-element.38), channel_id=1, source_target_pairs={{0,8},{8,0},{16,24},{24,16},{32,40},{40,32},{48,56},{56,48},{64,72... | collective-permute-start | bytes 884744 | tf_op jit(solution)/shard_map/ppermute | solution.py:373
  128.0 5.2 %copy-start.4 = (bf16[3,64,768]{2,1,0:T(8,128)(2,1)S(1)}, bf16[3,64,768]{2,1,0:T(8,128)(2,1)}, u32[]{:S(2)}) copy-start(bf16[3,64,768]{2,1,0:T(8,128)(2,1)} %get-tuple-element.37) | copy-start | bytes 884740

commit v7 on v6

--- a/solution.py
+++ b/solution.py
@@ -211,60 +211,57 @@
     att_ref = refs[n_col // 2]
     out_refs = refs[n_col // 2 + 1 : n_col + 1]
     bias2, acc, kt, vt = refs[n_col + 1 :]
-    step = pl.program_id(0)
     me = c_ref[0]
     side = me // (n_col // 2)
-    block = blk_ref.shape[3]
+    block = blk_ref.shape[3] // per
     wide = block * n_col
     rest = block - 2 * size
 
-    @pl.when(step == 0)
-    def _():
-        for k in range(n_col):
-            far = jnp.bitwise_xor(side, k // (n_col // 2))
-            part = bias_refs[k % (n_col // 2)][:, far]
-            part = part.astype(F32).reshape(bias2.shape[0], block)
-            bias2[:, k * block : (k + 1) * block] = part * LOG2E
-        row = lax.broadcasted_iota(jnp.int32, (rest, wide), 0)
-        for h in range(2):
-            kt[h, 2 * size :, :] = jnp.zeros((rest, wide), BF)
-            vt[h, 2 * size :, :] = jnp.where(row < 3, 1.0, 0.0).astype(BF)
+    for k in range(n_col):
+        far = jnp.bitwise_xor(side, k // (n_col // 2))
+        part = bias_refs[k % (n_col // 2)][:, far]
+        part = part.astype(F32).reshape(bias2.shape[0], block)
+        bias2[:, k * block : (k + 1) * block] = part * LOG2E
+    row = lax.broadcasted_iota(jnp.int32, (rest, wide), 0)
+    for h in range(2 * per):
+        kt[h, 2 * size :, :] = jnp.zeros((rest, wide), BF)
+        vt[h, 2 * size :, :] = jnp.where(row < 3, 1.0, 0.0).astype(BF)
 
     scale = LOG2E / math.sqrt(size)
     row = lax.broadcasted_iota(jnp.int32, (rest, block), 0)
 
-    def prepare(h):
+    def prepare(u, h):
         for k in range(n_col):
             owner = jnp.bitwise_xor(me, k)
             cols = slice(k * block, (k + 1) * block)
-            keys = blk_ref[owner, h, size : 2 * size, :]
-            kt[h, :size, cols] = keys
-            kt[h, size : 2 * size, cols] = keys
-            vals = blk_ref[owner, h, 2 * size : 3 * size, :]
-            vt[h, :size, cols] = vals
-            vt[h, size : 2 * size, cols] = vals
+            keys = blk_ref[owner, h, size : 2 * size, u * block : (u + 1) * block]
+            kt[2 * u + h, :size, cols] = keys
+            kt[2 * u + h, size : 2 * size, cols] = keys
+            vals = blk_ref[owner, h, 2 * size : 3 * size, u * block : (u + 1) * block]
+            vt[2 * u + h, :size, cols] = vals
+            vt[2 * u + h, size : 2 * size, cols] = vals
         lhs = []
         for b in range(n_chip):
-            high, low = split(blk_ref[b, h, :size, :].astype(F32) * scale)
+            high, low = split(blk_ref[b, h, :size, u * block : (u + 1) * block].astype(F32) * scale)
             lhs.append(jnp.concatenate([high, low, jnp.zeros((rest, block), F32)], axis=0).T.astype(BF))
         return jnp.concatenate(lhs, axis=0)
 
-    def softmax(h, lhs):
-        scores = jnp.dot(lhs, kt[h], preferred_element_type=F32) + bias2[...]
+    def softmax(u, h, lhs):
+        scores = jnp.dot(lhs, kt[2 * u + h], preferred_element_type=F32) + bias2[...]
         top = jnp.max(scores, axis=1, keepdims=True)
         return jnp.exp2(scores - top)
 
-    def mix(h, probs):
+    def mix(u, h, probs):
         mixed = lax.dot_general(
-            probs.astype(BF), vt[h], (((1,), (1,)), ((), ())), preferred_element_type=F32
+            probs.astype(BF), vt[2 * u + h], (((1,), (1,)), ((), ())), preferred_element_type=F32
         )
         lhs = []
         for b in range(n_chip):
             mixed_t = mixed[b * block : (b + 1) * block].T
             inv = 1.0 / mixed_t[2 * size : 2 * size + 1]
             att = mixed_t[:size] * inv
-            att_ref[b, h, :, :] = att.astype(BF)
-            cotan = blk_ref[b, h, 3 * size :, :].astype(F32)
+            att_ref[b, h, :, u * block : (u + 1) * block] = att.astype(BF)
+            cotan = blk_ref[b, h, 3 * size :, u * block : (u + 1) * block].astype(F32)
             delta = -jnp.sum(cotan * att, axis=0, keepdims=True) * inv
             high, low = split(cotan * inv)
             d0, rem = split(delta)
@@ -273,29 +270,25 @@
             lhs.append(jnp.concatenate([high, low, tail], axis=0).T.astype(BF))
         return jnp.concatenate(lhs, axis=0)
 
-    def grad(h, probs, lhs):
-        return probs * jnp.dot(lhs, vt[h], preferred_element_type=F32)
-
-    lhs = [prepare(h) for h in range(2)]
-    probs = [softmax(h, lhs[h]) for h in range(2)]
-    lhs = [mix(h, probs[h]) for h in range(2)]
-    term = grad(0, probs[0], lhs[0]) + grad(1, probs[1], lhs[1])
-
-    @pl.when(step == 0)
-    def _():
-        acc[...] = term
-
-    @pl.when(step > 0)
-    def _():
-        acc[...] += term
-
-    @pl.when(step == per - 1)
-    def _():
-        for k in range(n_col):
-            part = acc[:, k * block : (k + 1) * block].astype(BF)
-            out_ref = out_refs[k % (n_col // 2)]
-            far = jnp.bitwise_xor(side, k // (n_col // 2))
-            out_ref[:, far] = part.reshape(out_ref.shape[0], out_ref.shape[2], block)
+    def grad(u, h, probs, lhs):
+        return probs * jnp.dot(lhs, vt[2 * u + h], preferred_element_type=F32)
+
+    for u in range(per):
+        lhs = [prepare(u, h) for h in range(2)]
+        probs = [softmax(u, h, lhs[h]) for h in range(2)]
+        lhs = [mix(u, h, probs[h]) for h in range(2)]
+        term = grad(u, 0, probs[0], lhs[0]) + grad(u, 1, probs[1], lhs[1])
+        if u == 0:
+            acc[...] = term
+        elif u < per - 1:
+            acc[...] += term
+        else:
+            term = (acc[...] + term).astype(BF)
+            for k in range(n_col):
+                part = term[:, k * block : (k + 1) * block]
+                out_ref = out_refs[k % (n_col // 2)]
+                far = jnp.bitwise_xor(side, k // (n_col // 2))
+                out_ref[:, far] = part.reshape(out_ref.shape[0], out_ref.shape[2], block)
 
 
 def attend(me, qkvc, biases, n_samp, size, limit=48):
@@ -307,19 +300,19 @@
     wide = n_col * block
     parts = biases[0].shape
     whole = pl.BlockSpec(parts, lambda s, c: (0, 0, 0, 0))
-    spec = lambda feats: pl.BlockSpec((n_chip, 2, feats, block), lambda s, c: (0, 0, 0, s))
+    spec = lambda feats: pl.BlockSpec((n_chip, 2, feats, lanes), lambda s, c: (0, 0, 0, 0))
     return pl.pallas_call(
         functools.partial(attend_kernel, n_col, n_chip, per, size),
         grid_spec=pltpu.PrefetchScalarGridSpec(
             num_scalar_prefetch=1,
-            grid=(per,),
+            grid=(1,),
             in_specs=[spec(4 * size)] + [whole] * len(biases),
             out_specs=[spec(size)] + [whole] * len(biases),
             scratch_shapes=[
                 pltpu.VMEM((tokens, wide), F32),
                 pltpu.VMEM((tokens, wide), F32),
-                pltpu.VMEM((2, block, wide), BF),
-                pltpu.VMEM((2, block, wide), BF),
+                pltpu.VMEM((n_samp, block, wide), BF),
+                pltpu.VMEM((n_samp, block, wide), BF),
             ],
         ),
         out_shape=[jax.ShapeDtypeStruct((n_chip, 2, size, lanes), BF)]

time: 135 us -> 134 us (level)
  no operation moved by 1% of the time
where the time goes in v7:
time: 134 us; the launch traced here: 133 us
  Pallas kernels  49.6 us (37%)
  waiting for transfers between devices  40.2 us (30%)
  starting transfers between devices  39.4 us (29%)
  other arithmetic  2.11 us (2%)
    all_to_all x1, waiting for transfers between devices, shards(): packed = lax.all_to_all(packed, 'row', 0, 0, tiled=True)  21.8 us
    all_to_all x2, starting transfers between devices, shards(): lax.all_to_all(v.reshape(2 * n_row, rows, pair.shape[1]), ('row', 'col'),...  16.7 us
    pallas_call x1, Pallas kernels, attend(): pl.pallas_call(functools.partial(attend_kernel, n_col, n_chip, per, size)...  16.6 us
    ppermute x3, waiting for transfers between devices, shards(): lax.ppermute(grads[k], 'col', flip(k))  15.2 us
    pallas_call x1, Pallas kernels, transition(): pl.pallas_call(transition_kernel, grid_spec=pltpu.PrefetchScalarGridSpec(...  9.43 us
    pallas_call x1, Pallas kernels, project(): pl.pallas_call(project_kernel, grid_spec=pltpu.PrefetchScalarGridSpec(num...  8.59 us
    all_to_all x1, starting transfers between devices, shards(): attended = lax.all_to_all(attended, 'row', 0, 0, tiled=True)  7.15 us
    all_to_all x1, starting transfers between devices, shards(): packed = lax.all_to_all(packed, 'row', 0, 0, tiled=True)  5.79 us
  transfers between devices with their start and end apart: 13, of which 5 were waited for; matrix products, arithmetic and copies ran while one was open for 1% of the time, Pallas kernels for 25%

profile of v7, /device:TPU:1, one launch (start us, length us, event | category | flops | bytes accessed | tf_op | source)
XLA Modules:
  0.0 133.0 jit_solution(2954614515660021008)
XLA Ops:
  0.6 1.5 %collective-permute-start = (bf16[6,64,768]{2,1,0:T(8,128)(2,1)}, bf16[6,64,768]{2,1,0:T(8,128)(2,1)S(1)}, u32[]{:S(2)}, u32[]{:S(2)}) collective-permute-start(bf16[6,64,768]{2,1,0:T(8,128)(2,1)} %single_ref.1), channel_id=1, source_target_pairs={{0,8},{8,0},{16,24},{24,16},{32,40},{40,32},{48,56},{56,48},{64,72... | collective-permute-start | bytes 1769480 | tf_op jit(solution)/shard_map/ppermute | solution.py:338
  2.1 0.1 collective-permute-start.1
  2.2 4.1 %shard_map.96 = bf16[16,2,64,128]{3,2,1,0:T(8,128)(2,1)} custom-call(bf16[64,128,128]{2,1,0:T(8,128)(2,1)} %pair_ref.2, bf16[16,128]{1,0:T(8,128)(2,1)} %bitcast.17), custom_call_target="tpu_custom_call" | custom-call | tf_op jit(solution)/shard_map/pallas_call | solution.py:45
  6.3 8.4 %all-to-all-start.1 = ((bf16[32,64,128]{2,1,0:T(8,128)(2,1)}), bf16[32,64,128]{2,1,0:T(8,128)(2,1)S(1)}, u32[]{:S(2)}, u32[]{:S(2)}) async-start(bf16[32,64,128]{2,1,0:T(8,128)(2,1)} %bitcast.15), calls=%async_computation.1 | async-start | bytes 1048576 | tf_op jit(solution)/shard_map/all_to_all | solution.py:341
  14.8 0.0 copy-start.2
  14.8 0.0 collective-permute-done.1.gotc_ref
  14.8 0.8 copy-done.2
  15.6 0.2 copy-done.3
  15.8 8.6 %shard_map.95 = (bf16[16,192,384]{2,1,0:T(8,128)(2,1)}, bf16[3,128,768]{2,1,0:T(8,128)(2,1)}) custom-call(s32[1]{0:T(128)} %bitcast.core_ref, bf16[6,64,768]{2,1,0:T(8,128)(2,1)} %single_ref.1, bf16[6,64,768]{2,1,0:T(8,128)(2,1)} %copy-done.2, bf16[6,64,768]{2,1,0:T(8,128)(2,1)} %cot_ref.1, bf16[6,64,768]{2,1,0:T(8,128)(2,1)} %copy-done.3, ...), custom_call_target="tpu_custom_call" | custom-call | tf_op jit(solution)/shard_map/pallas_call | solution.py:140
  24.4 1.5 %all-to-all-done.1 = bf16[32,64,128]{2,1,0:T(8,128)(2,1)S(1)} async-done(((bf16[32,64,128]{2,1,0:T(8,128)(2,1)}), bf16[32,64,128]{2,1,0:T(8,128)(2,1)S(1)}, u32[]{:S(2)}, u32[]{:S(2)}) %all-to-all-start.1) | async-done | bytes 524320 | tf_op jit(solution)/shard_map/all_to_all | solution.py:341
  25.8 5.8 %all-to-all-start = ((bf16[16,192,384]{2,1,0:T(8,128)(2,1)}), bf16[16,192,384]{2,1,0:T(8,128)(2,1)}, u32[]{:S(2)}, u32[]{:S(2)}) async-start(bf16[16,192,384]{2,1,0:T(8,128)(2,1)} %get-tuple-element.23), calls=%async_computation | async-start | bytes 4718592 | tf_op jit(solution)/shard_map/all_to_all | solution.py:350
  31.6 1.3 collective-permute-start.2
  32.9 2.6 %collective-permute-start.3 = (bf16[16,2,64,128]{3,2,1,0:T(8,128)(2,1)S(1)}, bf16[16,2,64,128]{3,2,1,0:T(8,128)(2,1)S(1)}, u32[]{:S(2)}, u32[]{:S(2)}) collective-permute-start(bf16[16,2,64,128]{3,2,1,0:T(8,128)(2,1)S(1)} %bitcast.11), channel_id=1, source_target_pairs={{0,2},{1,3},{2,0},{3,1},{4,6},{5,7},{6,4},{7,5},{8,10},{9,11},{10,... | collective-permute-start | bytes 1572872 | tf_op jit(solution)/shard_map/ppermute | solution.py:346
  35.6 5.6 %shard_map.97 = (f32[64,128,128]{2,1,0:T(8,128)}, f32[64,128]{1,0:T(8,128)}) custom-call(bf16[64,128,128]{2,1,0:T(8,128)(2,1)} %pair_ref.2), custom_call_target="tpu_custom_call" | custom-call | tf_op jit(solution)/shard_map/pallas_call | solution.py:64
  41.2 21.8 %all-to-all-done = bf16[16,192,384]{2,1,0:T(8,128)(2,1)} async-done(((bf16[16,192,384]{2,1,0:T(8,128)(2,1)}), bf16[16,192,384]{2,1,0:T(8,128)(2,1)}, u32[]{:S(2)}, u32[]{:S(2)}) %all-to-all-start) | async-done | bytes 2359328 | tf_op jit(solution)/shard_map/all_to_all | solution.py:350
  63.0 0.0 collective-permute-done.2.refs_1_
  63.0 0.0 collective-permute-done.3.refs_2_
  63.0 0.0 collective-permute-done.4.refs_3_
  63.0 16.6 %shard_map.98 = (bf16[8,2,48,384]{3,2,1,0:T(8,128)(2,1)}, bf16[16,2,64,128]{3,2,1,0:T(8,128)(2,1)S(1)}, bf16[16,2,64,128]{3,2,1,0:T(8,128)(2,1)S(1)}, bf16[16,2,...) custom-call(s32[1]{0:T(128)} %bitcast.1.c_ref, bf16[8,2,192,384]{3,2,1,0:T(8,128)(2,1)} %bitcast.5.blk_ref, ...), custom_call_target="tpu_custom_call" | custom-call | tf_op jit(solution)/shard_map/pallas_call | solution.py:304
  79.6 2.7 %collective-permute-start.7 = (bf16[16,2,64,128]{3,2,1,0:T(8,128)(2,1)}, bf16[16,2,64,128]{3,2,1,0:T(8,128)(2,1)S(1)}, u32[]{:S(2)}, u32[]{:S(2)}) collective-permute-start(bf16[16,2,64,128]{3,2,1,0:T(8,128)(2,1)} %get-tuple-element.32), channel_id=1, source_target_pairs={{0,3},{1,2},{2,1},{3,0},{4,7},{5,6},{6,5},{7,4},{8,11},{9,10},{10,... | collective-permute-start | bytes 1572872 | tf_op jit(solution)/shard_map/ppermute | solution.py:354
  82.4 0.3 collective-permute-start.6
  82.7 0.2 collective-permute-start.5
  83.0 7.2 %all-to-all-start.2 = ((bf16[16,48,384]{2,1,0:T(8,128)(2,1)}), bf16[16,48,384]{2,1,0:T(8,128)(2,1)S(1)}, u32[]{:S(2)}, u32[]{:S(2)}) async-start(bf16[16,48,384]{2,1,0:T(8,128)(2,1)} %bitcast.6), calls=%async_computation.2 | async-start | bytes 1179648 | tf_op jit(solution)/shard_map/all_to_all | solution.py:356
  90.1 15.1 %collective-permute-done.7 = bf16[16,2,64,128]{3,2,1,0:T(8,128)(2,1)S(1)} collective-permute-done((bf16[16,2,64,128]{3,2,1,0:T(8,128)(2,1)}, bf16[16,2,64,128]{3,2,1,0:T(8,128)(2,1)S(1)}, u32[]{:S(2)}, u32[]{:S(2)}) %collective-permute-start.7) | collective-permute-done | bytes 524320 | tf_op jit(solution)/shard_map/ppermute | solution.py:354
  105.2 0.1 collective-permute-done.5
  105.3 1.2 add_convert_fusion
  106.5 8.3 %all-to-all-start.3 = ((bf16[32,64,128]{2,1,0:T(8,128)(2,1)}), bf16[32,64,128]{2,1,0:T(8,128)(2,1)S(1)}, u32[]{:S(2)}, u32[]{:S(2)}) async-start(bf16[32,64,128]{2,1,0:T(8,128)(2,1)} %bitcast.8), calls=%async_computation.3 | async-start | bytes 1048576 | tf_op jit(solution)/shard_map/all_to_all | solution.py:341
  114.8 9.4 %shard_map.99 = (bf16[3,64,768]{2,1,0:T(8,128)(2,1)}, bf16[3,64,768]{2,1,0:T(8,128)(2,1)}) custom-call(s32[1]{0:T(128)} %bitcast.core_ref, bf16[3,128,768]{2,1,0:T(8,128)(2,1)} %get-tuple-element.22.tokens_ref, bf16[768,384]{1,0:T(8,128)(2,1)} %bitcast.14, bf16[768,768]{1,0:T(8,128)(2,1)} %wo_ref.1, bf16[768,3072]{1,0:T(8,128)(2,1)} %wu_ref.1, ...), custom_call_target="tpu_custom_call" | custom-call | tf_op jit(solution)/shard_map/pallas_call | solution.py:187
  124.3 1.7 %all-to-all-done.3 = bf16[32,64,128]{2,1,0:T(8,128)(2,1)S(1)} async-done(((bf16[32,64,128]{2,1,0:T(8,128)(2,1)}), bf16[32,64,128]{2,1,0:T(8,128)(2,1)S(1)}, u32[]{:S(2)}, u32[]{:S(2)}) %all-to-all-start.3) | async-done | bytes 524320 | tf_op jit(solution)/shard_map/all_to_all | solution.py:341
  125.9 0.9 collective-permute-start.8
  126.8 5.2 %shard_map.100 = f32[64,128,128]{2,1,0:T(8,128)} custom-call(f32[64,128,128]{2,1,0:T(8,128)} %get-tuple-element.39.normed_ref, f32[64,128]{1,0:T(8,128)} %get-tuple-element.40.scaled_ref, bf16[16,2,64,128]{3,2,1,0:T(8,128)(2,1)} %bitcast.16, bf16[16,128]{1,0:T(8,128)(2,1)} %bitcast.18), custom_call_target="tpu_custom_call" | custom-call | tf_op jit(solution)/shard_map/pallas_call | solution.py:93
  132.1 0.9 pad_maximum_fusion
  (13 shorter events, 0.1 us)
Async XLA Ops:
  0.6 14.1 %collective-permute-start = (bf16[6,64,768]{2,1,0:T(8,128)(2,1)}, bf16[6,64,768]{2,1,0:T(8,128)(2,1)S(1)}, u32[]{:S(2)}, u32[]{:S(2)}) collective-permute-start(bf16[6,64,768]{2,1,0:T(8,128)(2,1)} %single_ref.1), channel_id=1, source_target_pairs={{0,8},{8,0},{16,24},{24,16},{32,40},{40,32},{48,56},{56,48},{64,72... | collective-permute-start | bytes 1769480 | tf_op jit(solution)/shard_map/ppermute | solution.py:338
  2.1 12.6 %collective-permute-start.1 = (bf16[6,64,768]{2,1,0:T(8,128)(2,1)}, bf16[6,64,768]{2,1,0:T(8,128)(2,1)S(1)}, u32[]{:S(2)}, u32[]{:S(2)}) collective-permute-start(bf16[6,64,768]{2,1,0:T(8,128)(2,1)} %cot_ref.1), channel_id=1, source_target_pairs={{0,8},{8,0},{16,24},{24,16},{32,40},{40,32},{48,56},{56,48},{64,72... | collective-permute-start | bytes 1769480 | tf_op jit(solution)/shard_map/ppermute | solution.py:339
  6.3 19.5 %all-to-all-start.1 = ((bf16[32,64,128]{2,1,0:T(8,128)(2,1)}), bf16[32,64,128]{2,1,0:T(8,128)(2,1)S(1)}, u32[]{:S(2)}, u32[]{:S(2)}) async-start(bf16[32,64,128]{2,1,0:T(8,128)(2,1)} %bitcast.15), calls=%async_computation.1 | async-start | bytes 1048576 | tf_op jit(solution)/shard_map/all_to_all | solution.py:341
  14.8 0.8 copy-start.2
  14.8 1.0 copy-start.3
  25.8 37.1 %all-to-all-start = ((bf16[16,192,384]{2,1,0:T(8,128)(2,1)}), bf16[16,192,384]{2,1,0:T(8,128)(2,1)}, u32[]{:S(2)}, u32[]{:S(2)}) async-start(bf16[16,192,384]{2,1,0:T(8,128)(2,1)} %get-tuple-element.23), calls=%async_computation | async-start | bytes 4718592 | tf_op jit(solution)/shard_map/all_to_all | solution.py:350
  31.6 31.4 %collective-permute-start.2 = (bf16[16,2,64,128]{3,2,1,0:T(8,128)(2,1)S(1)}, bf16[16,2,64,128]{3,2,1,0:T(8,128)(2,1)S(1)}, u32[]{:S(2)}, u32[]{:S(2)}) collective-permute-start(bf16[16,2,64,128]{3,2,1,0:T(8,128)(2,1)S(1)} %bitcast.10), channel_id=1, source_target_pairs={{0,1},{1,0},{2,3},{3,2},{4,5},{5,4},{6,7},{7,6},{8,9},{9,8},{10,11... | collective-permute-start | bytes 1572872 | tf_op jit(solution)/shard_map/ppermute | solution.py:346
  32.9 30.1 %collective-permute-start.3 = (bf16[16,2,64,128]{3,2,1,0:T(8,128)(2,1)S(1)}, bf16[16,2,64,128]{3,2,1,0:T(8,128)(2,1)S(1)}, u32[]{:S(2)}, u32[]{:S(2)}) collective-permute-start(bf16[16,2,64,128]{3,2,1,0:T(8,128)(2,1)S(1)} %bitcast.11), channel_id=1, source_target_pairs={{0,2},{1,3},{2,0},{3,1},{4,6},{5,7},{6,4},{7,5},{8,10},{9,11},{10,... | collective-permute-start | bytes 1572872 | tf_op jit(solution)/shard_map/ppermute | solution.py:346
  35.6 27.5 %collective-permute-start.4 = (bf16[16,2,64,128]{3,2,1,0:T(8,128)(2,1)S(1)}, bf16[16,2,64,128]{3,2,1,0:T(8,128)(2,1)S(1)}, u32[]{:S(2)}, u32[]{:S(2)}) collective-permute-start(bf16[16,2,64,128]{3,2,1,0:T(8,128)(2,1)S(1)} %bitcast.12), channel_id=1, source_target_pairs={{0,3},{1,2},{2,1},{3,0},{4,7},{5,6},{6,5},{7,4},{8,11},{9,10},{10,... | collective-permute-start | bytes 1572872 | tf_op jit(solution)/shard_map/ppermute | solution.py:346
  79.6 25.6 %collective-permute-start.7 = (bf16[16,2,64,128]{3,2,1,0:T(8,128)(2,1)}, bf16[16,2,64,128]{3,2,1,0:T(8,128)(2,1)S(1)}, u32[]{:S(2)}, u32[]{:S(2)}) collective-permute-start(bf16[16,2,64,128]{3,2,1,0:T(8,128)(2,1)} %get-tuple-element.32), channel_id=1, source_target_pairs={{0,3},{1,2},{2,1},{3,0},{4,7},{5,6},{6,5},{7,4},{8,11},{9,10},{10,... | collective-permute-start | bytes 1572872 | tf_op jit(solution)/shard_map/ppermute | solution.py:354
  82.4 22.8 %collective-permute-start.6 = (bf16[16,2,64,128]{3,2,1,0:T(8,128)(2,1)}, bf16[16,2,64,128]{3,2,1,0:T(8,128)(2,1)S(1)}, u32[]{:S(2)}, u32[]{:S(2)}) collective-permute-start(bf16[16,2,64,128]{3,2,1,0:T(8,128)(2,1)} %get-tuple-element.31), channel_id=1, source_target_pairs={{0,2},{1,3},{2,0},{3,1},{4,6},{5,7},{6,4},{7,5},{8,10},{9,11},{10,... | collective-permute-start | bytes 1572872 | tf_op jit(solution)/shard_map/ppermute | solution.py:354
  82.7 22.6 %collective-permute-start.5 = (bf16[16,2,64,128]{3,2,1,0:T(8,128)(2,1)S(1)}, bf16[16,2,64,128]{3,2,1,0:T(8,128)(2,1)S(1)}, u32[]{:S(2)}, u32[]{:S(2)}) collective-permute-start(bf16[16,2,64,128]{3,2,1,0:T(8,128)(2,1)S(1)} %get-tuple-element.30), channel_id=1, source_target_pairs={{0,1},{1,0},{2,3},{3,2},{4,5},{5,4},{6,7},{7,6},{8,9},{9,8},{10,11... | collective-permute-start | bytes 1572872 | tf_op jit(solution)/shard_map/ppermute | solution.py:354
  83.0 23.6 %all-to-all-start.2 = ((bf16[16,48,384]{2,1,0:T(8,128)(2,1)}), bf16[16,48,384]{2,1,0:T(8,128)(2,1)S(1)}, u32[]{:S(2)}, u32[]{:S(2)}) async-start(bf16[16,48,384]{2,1,0:T(8,128)(2,1)} %bitcast.6), calls=%async_computation.2 | async-start | bytes 1179648 | tf_op jit(solution)/shard_map/all_to_all | solution.py:356
  106.5 8.3 %copy-start = (bf16[16,48,384]{2,1,0:T(8,128)(2,1)}, bf16[16,48,384]{2,1,0:T(8,128)(2,1)S(1)}, u32[]{:S(2)}) copy-start(bf16[16,48,384]{2,1,0:T(8,128)(2,1)S(1)} %all-to-all-done.2) | copy-start | bytes 1769476
  106.5 19.4 %all-to-all-start.3 = ((bf16[32,64,128]{2,1,0:T(8,128)(2,1)}), bf16[32,64,128]{2,1,0:T(8,128)(2,1)S(1)}, u32[]{:S(2)}, u32[]{:S(2)}) async-start(bf16[32,64,128]{2,1,0:T(8,128)(2,1)} %bitcast.8), calls=%async_computation.3 | async-start | bytes 1048576 | tf_op jit(solution)/shard_map/all_to_all | solution.py:341
  125.9 0.9 copy-start.1
  125.9 6.1 %collective-permute-start.8 = (bf16[3,64,768]{2,1,0:T(8,128)(2,1)}, bf16[3,64,768]{2,1,0:T(8,128)(2,1)S(1)}, u32[]{:S(2)}, u32[]{:S(2)}) collective-permute-start(bf16[3,64,768]{2,1,0:T(8,128)(2,1)} %get-tuple-element.38), channel_id=1, source_target_pairs={{0,8},{8,0},{16,24},{24,16},{32,40},{40,32},{48,56},{56,48},{64,72... | collective-permute-start | bytes 884744 | tf_op jit(solution)/shard_map/ppermute | solution.py:366
  126.8 5.2 %copy-start.4 = (bf16[3,64,768]{2,1,0:T(8,128)(2,1)S(1)}, bf16[3,64,768]{2,1,0:T(8,128)(2,1)}, u32[]{:S(2)}) copy-start(bf16[3,64,768]{2,1,0:T(8,128)(2,1)} %get-tuple-element.37) | copy-start | bytes 884740

commit v8 on v7

--- a/solution.py
+++ b/solution.py
@@ -29,10 +29,15 @@
 def pair_kernel(pair_ref, w_ref, out_ref):
     rows, cols, chans = pair_ref.shape
     heads = w_ref.shape[0]
-    values = pair_ref[...].astype(F32).reshape(rows * cols, chans)
+    raw = pair_ref[...].reshape(rows * cols, chans)
+    values = raw.astype(F32)
     centred = values - jnp.mean(values, axis=-1, keepdims=True)
-    weight = w_ref[...]
-    flat = across(jnp.concatenate([weight, weight], axis=1), jnp.concatenate(halves(centred), axis=1))
+    weight = w_ref[...].astype(F32)
+    weight = weight - jnp.mean(weight, axis=1, keepdims=True)
+    w0 = weight.astype(BF)
+    w1, w2 = halves(weight - w0.astype(F32))
+    flat = across(jnp.concatenate([w0, w1, w2], axis=0), raw)
+    flat = flat[:heads] + flat[heads : 2 * heads] + flat[2 * heads :]
     ones = jnp.full((8, chans), 1.0 / chans, BF)
     variance = across(ones, (centred * centred).astype(BF))[:1]
     flat = (flat * lax.rsqrt(variance + 1e-05)).reshape(heads, rows, cols).astype(BF)
@@ -98,7 +103,7 @@
                   pl.BlockSpec((heads, chans), lambda i: (0, 0))],
         out_specs=pl.BlockSpec((step, cols, chans), lambda i: (i, 0, 0)),
         out_shape=jax.ShapeDtypeStruct((rows, cols, chans), F32),
-        compiler_params=pltpu.CompilerParams(dimension_semantics=("arbitrary",), vmem_limit_bytes=60 << 20),
+        compiler_params=pltpu.CompilerParams(dimension_semantics=("arbitrary",), vmem_limit_bytes=50 << 20),
     )(normed, scaled, grad, bias_weight.T)
 
 def project_kernel(core_ref, single_ref, got_ref, cot_ref, gotc_ref, w_ref, packed_ref, tokens_ref, normed, cotan):
@@ -147,7 +152,7 @@
             scratch_shapes=[pltpu.VMEM((lanes, width), BF), pltpu.VMEM((half, block, width), BF)],
         ),
         out_shape=[jax.ShapeDtypeStruct((heads, 4 * size, lanes), BF), jax.ShapeDtypeStruct((half, block, width), BF)],
-        compiler_params=pltpu.CompilerParams(dimension_semantics=("arbitrary",), vmem_limit_bytes=60 << 20),
+        compiler_params=pltpu.CompilerParams(dimension_semantics=("arbitrary",), vmem_limit_bytes=50 << 20),
     )(core, single, got, cot, gotc, w_qkv)
 
 def transition_kernel(core_ref, tokens_ref, att_ref, wo_ref, wg_ref, wu_ref, wd_ref, mine_ref, theirs_ref, mid, normed, done):
@@ -175,7 +180,8 @@
         mine = pl.ds(pl.multiple_of(core * rows, rows), rows)
         other = pl.ds(pl.multiple_of((1 - core) * rows, rows), rows)
         for u in range(half):
-            mine_ref[u] = done[u, mine, :]
+            mine_ref[core * half + u] = done[u, mine, :]
+            mine_ref[(1 - core) * half + u] = jnp.zeros((rows, width), BF)
             theirs_ref[u] = done[u, other, :]
 
 def transition(core, tokens, attended_t, w_out, w_gate_up, w_down, steps=4):
@@ -183,7 +189,7 @@
     lanes = half * block
     inner = w_down.shape[0]
     part = inner // steps
-    out = pl.BlockSpec((half, block // 2, width), lambda i, c: (0, 0, 0))
+    out = lambda n: pl.BlockSpec((n, block // 2, width), lambda i, c: (0, 0, 0))
     return pl.pallas_call(
         transition_kernel,
         grid_spec=pltpu.PrefetchScalarGridSpec(
@@ -194,11 +200,11 @@
                       pl.BlockSpec((width, part), lambda i, c: (0, i)),
                       pl.BlockSpec((width, part), lambda i, c: (0, i + steps)),
                       pl.BlockSpec((part, width), lambda i, c: (i, 0))],
-            out_specs=[out, out],
+            out_specs=[out(2 * half), out(half)],
             scratch_shapes=[pltpu.VMEM((lanes, width), F32), pltpu.VMEM((lanes, width), BF),
                             pltpu.VMEM((half, block, width), BF)],
         ),
-        out_shape=[jax.ShapeDtypeStruct((half, block // 2, width), BF)] * 2,
+        out_shape=[jax.ShapeDtypeStruct((n * half, block // 2, width), BF) for n in (2, 1)],
         compiler_params=pltpu.CompilerParams(dimension_semantics=("arbitrary",), vmem_limit_bytes=60 << 20),
     )(core, tokens, attended_t, w_out, w_gate_up, w_gate_up, w_down)
 
@@ -364,7 +370,7 @@
     )
     mine, theirs, total = lax.optimization_barrier((mine, theirs, total))
     got = lax.ppermute(theirs, "row", cores)
-    updated = jnp.concatenate([jnp.where(core == 0, mine, got), jnp.where(core == 0, got, mine)], axis=0)
+    updated = lax.dynamic_update_slice_in_dim(mine, got, (1 - core) * half, 0)
     pair_grad = pair_back(stats, total, bias_weight, 32)
     return (updated, pair_grad)
 

time: 134 us -> 132 us (0.985)
  transfers between devices with their start and end apart: 13 -> 13, of which waited for: 5 -> 5; matrix products, arithmetic and copies ran while one was open for 1% -> 1% of each run, Pallas kernels for 25% -> 24%
where the time goes in v8:
time: 132 us
  Pallas kernels  48.3 us (37%)
  waiting for transfers between devices  41.5 us (31%)
  starting transfers between devices  38.2 us (29%)
  local copies, waits for them, and re-layouts  1.67 us (1%)
    all_to_all x1, waiting for transfers between devices, shards(): packed = lax.all_to_all(packed, 'row', 0, 0, tiled=True)  21.9 us
    pallas_call x1, Pallas kernels, attend(): pl.pallas_call(functools.partial(attend_kernel, n_col, n_chip, per, size)...  16.6 us
    all_to_all x2, starting transfers between devices, shards(): lax.all_to_all(v.reshape(2 * n_row, rows, pair.shape[1]), ('row', 'col'),...  16.5 us
    ppermute x3, waiting for transfers between devices, shards(): lax.ppermute(grads[k], 'col', flip(k))  15.4 us
    pallas_call x1, Pallas kernels, transition(): pl.pallas_call(transition_kernel, grid_spec=pltpu.PrefetchScalarGridSpec(...  9.55 us
    pallas_call x1, Pallas kernels, project(): pl.pallas_call(project_kernel, grid_spec=pltpu.PrefetchScalarGridSpec(num...  7.65 us
    all_to_all x1, starting transfers between devices, shards(): attended = lax.all_to_all(attended, 'row', 0, 0, tiled=True)  6.93 us
    pallas_call x1, Pallas kernels, pair_stats(): pl.pallas_call(stats_kernel, grid=(rows // step,), in_specs=[pl.BlockSpec...  5.6 us
  transfers between devices with their start and end apart: 13, of which 5 were waited for; matrix products, arithmetic and copies ran while one was open for 1% of the time, Pallas kernels for 24%

profile of v8, /device:TPU:1, one launch (start us, length us, event | category | flops | bytes accessed | tf_op | source)
XLA Modules:
  0.0 131.6 jit_solution(4421083240710634384)
XLA Ops:
  0.6 1.5 %collective-permute-start = (bf16[6,64,768]{2,1,0:T(8,128)(2,1)}, bf16[6,64,768]{2,1,0:T(8,128)(2,1)S(1)}, u32[]{:S(2)}, u32[]{:S(2)}) collective-permute-start(bf16[6,64,768]{2,1,0:T(8,128)(2,1)} %single_ref.1), channel_id=1, source_target_pairs={{0,8},{8,0},{16,24},{24,16},{32,40},{40,32},{48,56},{56,48},{64,72... | collective-permute-start | bytes 1769480 | tf_op jit(solution)/shard_map/ppermute | solution.py:344
  2.2 0.1 collective-permute-start.1
  2.2 3.7 %shard_map.96 = bf16[16,2,64,128]{3,2,1,0:T(8,128)(2,1)} custom-call(bf16[64,128,128]{2,1,0:T(8,128)(2,1)} %pair_ref.2, bf16[16,128]{1,0:T(8,128)(2,1)} %bitcast.15), custom_call_target="tpu_custom_call" | custom-call | tf_op jit(solution)/shard_map/pallas_call | solution.py:50
  5.9 8.4 %all-to-all-start.1 = ((bf16[32,64,128]{2,1,0:T(8,128)(2,1)}), bf16[32,64,128]{2,1,0:T(8,128)(2,1)S(1)}, u32[]{:S(2)}, u32[]{:S(2)}) async-start(bf16[32,64,128]{2,1,0:T(8,128)(2,1)} %bitcast.18), calls=%async_computation.1 | async-start | bytes 1048576 | tf_op jit(solution)/shard_map/all_to_all | solution.py:347
  14.4 0.0 collective-permute-done.1.gotc_ref
  14.4 7.7 %shard_map.95 = (bf16[16,192,384]{2,1,0:T(8,128)(2,1)}, bf16[3,128,768]{2,1,0:T(8,128)(2,1)S(1)}) custom-call(s32[1]{0:T(128)} %bitcast.core_ref, bf16[6,64,768]{2,1,0:T(8,128)(2,1)S(1)} %copy-done, bf16[6,64,768]{2,1,0:T(8,128)(2,1)S(1)} %collective-permute-done.got_ref, bf16[6,64,768]{2,1,0:T(8,128)(2,1)S(1)} %copy-done.1, ...), custom_call_target="tpu_custom_call" | custom-call | tf_op jit(solution)/shard_map/pallas_call | solution.py:145
  22.1 0.8 copy-done.2
  22.9 2.6 %all-to-all-done.1 = bf16[32,64,128]{2,1,0:T(8,128)(2,1)S(1)} async-done(((bf16[32,64,128]{2,1,0:T(8,128)(2,1)}), bf16[32,64,128]{2,1,0:T(8,128)(2,1)S(1)}, u32[]{:S(2)}, u32[]{:S(2)}) %all-to-all-start.1) | async-done | bytes 524320 | tf_op jit(solution)/shard_map/all_to_all | solution.py:347
  25.5 5.0 %all-to-all-start = ((bf16[16,192,384]{2,1,0:T(8,128)(2,1)}), bf16[16,192,384]{2,1,0:T(8,128)(2,1)}, u32[]{:S(2)}, u32[]{:S(2)}) async-start(bf16[16,192,384]{2,1,0:T(8,128)(2,1)} %get-tuple-element.23), calls=%async_computation | async-start | bytes 4718592 | tf_op jit(solution)/shard_map/all_to_all | solution.py:356
  30.5 1.3 collective-permute-start.2
  31.8 2.6 %collective-permute-start.3 = (bf16[16,2,64,128]{3,2,1,0:T(8,128)(2,1)S(1)}, bf16[16,2,64,128]{3,2,1,0:T(8,128)(2,1)S(1)}, u32[]{:S(2)}, u32[]{:S(2)}) collective-permute-start(bf16[16,2,64,128]{3,2,1,0:T(8,128)(2,1)S(1)} %bitcast.11), channel_id=1, source_target_pairs={{0,2},{1,3},{2,0},{3,1},{4,6},{5,7},{6,4},{7,5},{8,10},{9,11},{10,... | collective-permute-start | bytes 1572872 | tf_op jit(solution)/shard_map/ppermute | solution.py:352
  34.4 5.6 %shard_map.97 = (f32[64,128,128]{2,1,0:T(8,128)}, f32[64,128]{1,0:T(8,128)}) custom-call(bf16[64,128,128]{2,1,0:T(8,128)(2,1)} %pair_ref.2), custom_call_target="tpu_custom_call" | custom-call | tf_op jit(solution)/shard_map/pallas_call | solution.py:69
  40.0 21.9 %all-to-all-done = bf16[16,192,384]{2,1,0:T(8,128)(2,1)} async-done(((bf16[16,192,384]{2,1,0:T(8,128)(2,1)}), bf16[16,192,384]{2,1,0:T(8,128)(2,1)}, u32[]{:S(2)}, u32[]{:S(2)}) %all-to-all-start) | async-done | bytes 2359328 | tf_op jit(solution)/shard_map/all_to_all | solution.py:356
  61.9 0.0 collective-permute-done.3.refs_2_
  62.0 0.0 collective-permute-done.4.refs_3_
  62.0 16.6 %shard_map.98 = (bf16[8,2,48,384]{3,2,1,0:T(8,128)(2,1)}, bf16[16,2,64,128]{3,2,1,0:T(8,128)(2,1)S(1)}, bf16[16,2,64,128]{3,2,1,0:T(8,128)(2,1)S(1)}, bf16[16,2,...) custom-call(s32[1]{0:T(128)} %bitcast.1.c_ref, bf16[8,2,192,384]{3,2,1,0:T(8,128)(2,1)} %bitcast.5.blk_ref, ...), custom_call_target="tpu_custom_call" | custom-call | tf_op jit(solution)/shard_map/pallas_call | solution.py:310
  78.6 2.7 %collective-permute-start.7 = (bf16[16,2,64,128]{3,2,1,0:T(8,128)(2,1)}, bf16[16,2,64,128]{3,2,1,0:T(8,128)(2,1)S(1)}, u32[]{:S(2)}, u32[]{:S(2)}) collective-permute-start(bf16[16,2,64,128]{3,2,1,0:T(8,128)(2,1)} %get-tuple-element.32), channel_id=1, source_target_pairs={{0,3},{1,2},{2,1},{3,0},{4,7},{5,6},{6,5},{7,4},{8,11},{9,10},{10,... | collective-permute-start | bytes 1572872 | tf_op jit(solution)/shard_map/ppermute | solution.py:360
  81.3 0.3 collective-permute-start.6
  81.7 0.2 collective-permute-start.5
  81.9 6.9 %all-to-all-start.2 = ((bf16[16,48,384]{2,1,0:T(8,128)(2,1)}), bf16[16,48,384]{2,1,0:T(8,128)(2,1)S(1)}, u32[]{:S(2)}, u32[]{:S(2)}) async-start(bf16[16,48,384]{2,1,0:T(8,128)(2,1)} %bitcast.6), calls=%async_computation.2 | async-start | bytes 1179648 | tf_op jit(solution)/shard_map/all_to_all | solution.py:362
  88.8 15.3 %collective-permute-done.7 = bf16[16,2,64,128]{3,2,1,0:T(8,128)(2,1)S(1)} collective-permute-done((bf16[16,2,64,128]{3,2,1,0:T(8,128)(2,1)}, bf16[16,2,64,128]{3,2,1,0:T(8,128)(2,1)S(1)}, u32[]{:S(2)}, u32[]{:S(2)}) %collective-permute-start.7) | collective-permute-done | bytes 524320 | tf_op jit(solution)/shard_map/ppermute | solution.py:360
  104.2 0.0 collective-permute-done.6
  104.2 0.1 collective-permute-done.5
  104.3 1.2 add_convert_fusion
  105.5 8.1 %all-to-all-start.3 = ((bf16[32,64,128]{2,1,0:T(8,128)(2,1)}), bf16[32,64,128]{2,1,0:T(8,128)(2,1)S(1)}, u32[]{:S(2)}, u32[]{:S(2)}) async-start(bf16[32,64,128]{2,1,0:T(8,128)(2,1)} %bitcast.8), calls=%async_computation.3 | async-start | bytes 1048576 | tf_op jit(solution)/shard_map/all_to_all | solution.py:347
  113.6 0.0 copy-start.4
  113.6 9.6 %shard_map.99 = (bf16[6,64,768]{2,1,0:T(8,128)(2,1)}, bf16[3,64,768]{2,1,0:T(8,128)(2,1)}) custom-call(s32[1]{0:T(128)} %bitcast.core_ref, bf16[3,128,768]{2,1,0:T(8,128)(2,1)} %copy-done.2, bf16[768,384]{1,0:T(8,128)(2,1)} %bitcast.17, bf16[768,768]{1,0:T(8,128)(2,1)} %wo_ref.1, bf16[768,3072]{1,0:T(8,128)(2,1)} %wu_ref.1, bf16[768,3072]{1,0:T(8,128)(2,1)} %wu_ref.1, ...), custom_call_target="tpu_custom_call" | custom-call | tf_op jit(solution)/shard_map/pallas_call | solution.py:193
  123.1 1.5 %all-to-all-done.3 = bf16[32,64,128]{2,1,0:T(8,128)(2,1)S(1)} async-done(((bf16[32,64,128]{2,1,0:T(8,128)(2,1)}), bf16[32,64,128]{2,1,0:T(8,128)(2,1)S(1)}, u32[]{:S(2)}, u32[]{:S(2)}) %all-to-all-start.3) | async-done | bytes 524320 | tf_op jit(solution)/shard_map/all_to_all | solution.py:347
  124.7 0.9 collective-permute-start.8
  125.5 5.2 %shard_map.100 = f32[64,128,128]{2,1,0:T(8,128)} custom-call(f32[64,128,128]{2,1,0:T(8,128)} %get-tuple-element.39.normed_ref, f32[64,128]{1,0:T(8,128)S(1)} %copy-done.3, bf16[16,2,64,128]{3,2,1,0:T(8,128)(2,1)S(1)} %bitcast.14, bf16[16,128]{1,0:T(8,128)(2,1)S(1)} %bitcast.16), custom_call_target="tpu_custom_call" | custom-call | tf_op jit(solution)/shard_map/pallas_call | solution.py:98
  130.8 0.0 copy-start.7
  130.8 0.8 copy-done.7
  (18 shorter events, 0.1 us)
Async XLA Ops:
  0.6 13.8 %copy-start = (bf16[6,64,768]{2,1,0:T(8,128)(2,1)S(1)}, bf16[6,64,768]{2,1,0:T(8,128)(2,1)}, u32[]{:S(2)}) copy-start(bf16[6,64,768]{2,1,0:T(8,128)(2,1)} %single_ref.1) | copy-start | bytes 1769476
  0.6 13.8 %copy-start.1 = (bf16[6,64,768]{2,1,0:T(8,128)(2,1)S(1)}, bf16[6,64,768]{2,1,0:T(8,128)(2,1)}, u32[]{:S(2)}) copy-start(bf16[6,64,768]{2,1,0:T(8,128)(2,1)} %cot_ref.1) | copy-start | bytes 1769476
  0.6 13.7 %collective-permute-start = (bf16[6,64,768]{2,1,0:T(8,128)(2,1)}, bf16[6,64,768]{2,1,0:T(8,128)(2,1)S(1)}, u32[]{:S(2)}, u32[]{:S(2)}) collective-permute-start(bf16[6,64,768]{2,1,0:T(8,128)(2,1)} %single_ref.1), channel_id=1, source_target_pairs={{0,8},{8,0},{16,24},{24,16},{32,40},{40,32},{48,56},{56,48},{64,72... | collective-permute-start | bytes 1769480 | tf_op jit(solution)/shard_map/ppermute | solution.py:344
  2.2 12.2 %collective-permute-start.1 = (bf16[6,64,768]{2,1,0:T(8,128)(2,1)}, bf16[6,64,768]{2,1,0:T(8,128)(2,1)S(1)}, u32[]{:S(2)}, u32[]{:S(2)}) collective-permute-start(bf16[6,64,768]{2,1,0:T(8,128)(2,1)} %cot_ref.1), channel_id=1, source_target_pairs={{0,8},{8,0},{16,24},{24,16},{32,40},{40,32},{48,56},{56,48},{64,72... | collective-permute-start | bytes 1769480 | tf_op jit(solution)/shard_map/ppermute | solution.py:345
  5.9 19.5 %all-to-all-start.1 = ((bf16[32,64,128]{2,1,0:T(8,128)(2,1)}), bf16[32,64,128]{2,1,0:T(8,128)(2,1)S(1)}, u32[]{:S(2)}, u32[]{:S(2)}) async-start(bf16[32,64,128]{2,1,0:T(8,128)(2,1)} %bitcast.18), calls=%async_computation.1 | async-start | bytes 1048576 | tf_op jit(solution)/shard_map/all_to_all | solution.py:347
  22.1 0.8 copy-start.2
  25.5 36.5 %all-to-all-start = ((bf16[16,192,384]{2,1,0:T(8,128)(2,1)}), bf16[16,192,384]{2,1,0:T(8,128)(2,1)}, u32[]{:S(2)}, u32[]{:S(2)}) async-start(bf16[16,192,384]{2,1,0:T(8,128)(2,1)} %get-tuple-element.23), calls=%async_computation | async-start | bytes 4718592 | tf_op jit(solution)/shard_map/all_to_all | solution.py:356
  30.5 31.4 %collective-permute-start.2 = (bf16[16,2,64,128]{3,2,1,0:T(8,128)(2,1)S(1)}, bf16[16,2,64,128]{3,2,1,0:T(8,128)(2,1)S(1)}, u32[]{:S(2)}, u32[]{:S(2)}) collective-permute-start(bf16[16,2,64,128]{3,2,1,0:T(8,128)(2,1)S(1)} %bitcast.10), channel_id=1, source_target_pairs={{0,1},{1,0},{2,3},{3,2},{4,5},{5,4},{6,7},{7,6},{8,9},{9,8},{10,11... | collective-permute-start | bytes 1572872 | tf_op jit(solution)/shard_map/ppermute | solution.py:352
  31.8 30.2 %collective-permute-start.3 = (bf16[16,2,64,128]{3,2,1,0:T(8,128)(2,1)S(1)}, bf16[16,2,64,128]{3,2,1,0:T(8,128)(2,1)S(1)}, u32[]{:S(2)}, u32[]{:S(2)}) collective-permute-start(bf16[16,2,64,128]{3,2,1,0:T(8,128)(2,1)S(1)} %bitcast.11), channel_id=1, source_target_pairs={{0,2},{1,3},{2,0},{3,1},{4,6},{5,7},{6,4},{7,5},{8,10},{9,11},{10,... | collective-permute-start | bytes 1572872 | tf_op jit(solution)/shard_map/ppermute | solution.py:352
  34.4 27.5 %collective-permute-start.4 = (bf16[16,2,64,128]{3,2,1,0:T(8,128)(2,1)S(1)}, bf16[16,2,64,128]{3,2,1,0:T(8,128)(2,1)S(1)}, u32[]{:S(2)}, u32[]{:S(2)}) collective-permute-start(bf16[16,2,64,128]{3,2,1,0:T(8,128)(2,1)S(1)} %bitcast.12), channel_id=1, source_target_pairs={{0,3},{1,2},{2,1},{3,0},{4,7},{5,6},{6,5},{7,4},{8,11},{9,10},{10,... | collective-permute-start | bytes 1572872 | tf_op jit(solution)/shard_map/ppermute | solution.py:352
  78.6 25.6 %collective-permute-start.7 = (bf16[16,2,64,128]{3,2,1,0:T(8,128)(2,1)}, bf16[16,2,64,128]{3,2,1,0:T(8,128)(2,1)S(1)}, u32[]{:S(2)}, u32[]{:S(2)}) collective-permute-start(bf16[16,2,64,128]{3,2,1,0:T(8,128)(2,1)} %get-tuple-element.32), channel_id=1, source_target_pairs={{0,3},{1,2},{2,1},{3,0},{4,7},{5,6},{6,5},{7,4},{8,11},{9,10},{10,... | collective-permute-start | bytes 1572872 | tf_op jit(solution)/shard_map/ppermute | solution.py:360
  81.3 22.8 %collective-permute-start.6 = (bf16[16,2,64,128]{3,2,1,0:T(8,128)(2,1)}, bf16[16,2,64,128]{3,2,1,0:T(8,128)(2,1)S(1)}, u32[]{:S(2)}, u32[]{:S(2)}) collective-permute-start(bf16[16,2,64,128]{3,2,1,0:T(8,128)(2,1)} %get-tuple-element.31), channel_id=1, source_target_pairs={{0,2},{1,3},{2,0},{3,1},{4,6},{5,7},{6,4},{7,5},{8,10},{9,11},{10,... | collective-permute-start | bytes 1572872 | tf_op jit(solution)/shard_map/ppermute | solution.py:360
  81.7 22.6 %collective-permute-start.5 = (bf16[16,2,64,128]{3,2,1,0:T(8,128)(2,1)S(1)}, bf16[16,2,64,128]{3,2,1,0:T(8,128)(2,1)S(1)}, u32[]{:S(2)}, u32[]{:S(2)}) collective-permute-start(bf16[16,2,64,128]{3,2,1,0:T(8,128)(2,1)S(1)} %get-tuple-element.30), channel_id=1, source_target_pairs={{0,1},{1,0},{2,3},{3,2},{4,5},{5,4},{6,7},{7,6},{8,9},{9,8},{10,11... | collective-permute-start | bytes 1572872 | tf_op jit(solution)/shard_map/ppermute | solution.py:360
  81.9 23.6 %all-to-all-start.2 = ((bf16[16,48,384]{2,1,0:T(8,128)(2,1)}), bf16[16,48,384]{2,1,0:T(8,128)(2,1)S(1)}, u32[]{:S(2)}, u32[]{:S(2)}) async-start(bf16[16,48,384]{2,1,0:T(8,128)(2,1)} %bitcast.6), calls=%async_computation.2 | async-start | bytes 1179648 | tf_op jit(solution)/shard_map/all_to_all | solution.py:362
  105.5 8.1 %copy-start.5 = (bf16[16,48,384]{2,1,0:T(8,128)(2,1)}, bf16[16,48,384]{2,1,0:T(8,128)(2,1)S(1)}, u32[]{:S(2)}) copy-start(bf16[16,48,384]{2,1,0:T(8,128)(2,1)S(1)} %all-to-all-done.2) | copy-start | bytes 1769476
  105.5 19.2 %all-to-all-start.3 = ((bf16[32,64,128]{2,1,0:T(8,128)(2,1)}), bf16[32,64,128]{2,1,0:T(8,128)(2,1)S(1)}, u32[]{:S(2)}, u32[]{:S(2)}) async-start(bf16[32,64,128]{2,1,0:T(8,128)(2,1)} %bitcast.8), calls=%async_computation.3 | async-start | bytes 1048576 | tf_op jit(solution)/shard_map/all_to_all | solution.py:347
  113.6 12.0 %copy-start.3 = (f32[64,128]{1,0:T(8,128)S(1)}, f32[64,128]{1,0:T(8,128)}, u32[]{:S(2)}) copy-start(f32[64,128]{1,0:T(8,128)} %get-tuple-element.40.scaled_ref) | copy-start | bytes 98308
  113.6 11.9 %copy-start.4 = (bf16[128,16]{0,1:T(8,128)(2,1)S(1)}, bf16[128,16]{0,1:T(8,128)(2,1)}, u32[]{:S(2)}) copy-start(bf16[128,16]{0,1:T(8,128)(2,1)} %param.9) | copy-start | bytes 12292
  124.7 6.1 %collective-permute-start.8 = (bf16[3,64,768]{2,1,0:T(8,128)(2,1)}, bf16[3,64,768]{2,1,0:T(8,128)(2,1)S(1)}, u32[]{:S(2)}, u32[]{:S(2)}) collective-permute-start(bf16[3,64,768]{2,1,0:T(8,128)(2,1)} %get-tuple-element.38), channel_id=1, source_target_pairs={{0,8},{8,0},{16,24},{24,16},{32,40},{40,32},{48,56},{56,48},{64,72... | collective-permute-start | bytes 884744 | tf_op jit(solution)/shard_map/ppermute | solution.py:372
  125.5 5.2 %copy-start.6 = (bf16[6,64,768]{2,1,0:T(8,128)(2,1)S(1)}, bf16[6,64,768]{2,1,0:T(8,128)(2,1)}, u32[]{:S(2)}) copy-start(bf16[6,64,768]{2,1,0:T(8,128)(2,1)} %get-tuple-element.37) | copy-start | bytes 1769476
  130.8 0.8 copy-start.7

commit v9 on v8

--- a/solution.py
+++ b/solution.py
@@ -215,8 +215,9 @@
 def attend_kernel(n_col, n_chip, per, size, c_ref, blk_ref, *refs):
     bias_refs = refs[: n_col // 2]
     att_ref = refs[n_col // 2]
-    out_refs = refs[n_col // 2 + 1 : n_col + 1]
-    bias2, acc, kt, vt = refs[n_col + 1 :]
+    out_refs = refs[n_col // 2 + 1 : n_col]
+    pair_refs = refs[n_col : n_col + 2]
+    bias2, acc, kt, vt = refs[n_col + 2 :]
     me = c_ref[0]
     side = me // (n_col // 2)
     block = blk_ref.shape[3] // per
@@ -292,9 +293,13 @@
             term = (acc[...] + term).astype(BF)
             for k in range(n_col):
                 part = term[:, k * block : (k + 1) * block]
-                out_ref = out_refs[k % (n_col // 2)]
-                far = jnp.bitwise_xor(side, k // (n_col // 2))
-                out_ref[:, far] = part.reshape(out_ref.shape[0], out_ref.shape[2], block)
+                part = part.reshape(out_refs[0].shape[0], out_refs[0].shape[2], block)
+                ring = k % (n_col // 2)
+                if ring == 2:
+                    pair_refs[k // (n_col // 2)][...] = part
+                else:
+                    out_ref = out_refs[min(ring, 2)]
+                    out_ref[:, jnp.bitwise_xor(side, k // (n_col // 2))] = part
 
 
 def attend(me, qkvc, biases, n_samp, size, limit=48):
@@ -306,6 +311,9 @@
     wide = n_col * block
     parts = biases[0].shape
     whole = pl.BlockSpec(parts, lambda s, c: (0, 0, 0, 0))
+    single = (parts[0],) + parts[2:]
+    made = [whole] * 3 + [pl.BlockSpec(single, lambda s, c: (0, 0, 0))] * 2
+    shapes = [parts] * 3 + [single] * 2
     spec = lambda feats: pl.BlockSpec((n_chip, 2, feats, lanes), lambda s, c: (0, 0, 0, 0))
     return pl.pallas_call(
         functools.partial(attend_kernel, n_col, n_chip, per, size),
@@ -313,7 +321,7 @@
             num_scalar_prefetch=1,
             grid=(1,),
             in_specs=[spec(4 * size)] + [whole] * len(biases),
-            out_specs=[spec(size)] + [whole] * len(biases),
+            out_specs=[spec(size)] + made,
             scratch_shapes=[
                 pltpu.VMEM((tokens, wide), F32),
                 pltpu.VMEM((tokens, wide), F32),
@@ -322,7 +330,7 @@
             ],
         ),
         out_shape=[jax.ShapeDtypeStruct((n_chip, 2, size, lanes), BF)]
-        + [jax.ShapeDtypeStruct(parts, BF)] * len(biases),
+        + [jax.ShapeDtypeStruct(shape, BF) for shape in shapes],
         compiler_params=pltpu.CompilerParams(
             dimension_semantics=("arbitrary",), vmem_limit_bytes=limit * 1024 * 1024
         ),
@@ -357,12 +365,16 @@
     packed, stats = lax.optimization_barrier((packed, stats))
     packed = packed.reshape(n_chip, 2, 4 * size, half * block)
     attended, *grads = attend(me, packed, biases, samp, size)
-    grads = [grads[0]] + [lax.ppermute(grads[k], "col", flip(k)) for k in range(1, n_col // 2)]
+    mine, one, three, two, far = grads
+    far = lax.ppermute(far, "col", flip(n_col // 2))
+    one = lax.ppermute(one, "col", flip(1))
+    three = lax.ppermute(three, "col", flip(3))
     attended = attended.reshape(n_row, size, half * block)
     attended = lax.all_to_all(attended, "row", 0, 0, tiled=True)
-    total = grads[0].astype(F32)
-    for part in grads[1:]:
-        total = total + part.astype(F32)
+    two = lax.ppermute((two.astype(F32) + far.astype(F32)).astype(BF), "col", flip(2))
+    side = lax.broadcasted_iota(jnp.int32, mine.shape, 1) == me[0] // (n_col // 2)
+    total = mine.astype(F32) + one.astype(F32) + three.astype(F32)
+    total = total + jnp.where(side, two.astype(F32)[:, None], 0.0)
     attended, total = lax.optimization_barrier((attended, total.astype(BF)))
     total = share(total)
     mine, theirs = transition(

time: 132 us -> 128 us (0.970)
  waiting for transfers between devices: 41.5 us -> 35 us
  starting transfers between devices: 38.2 us -> 40 us
    ppermute x3 -> x4, waiting for transfers between devices: 15.4 us -> 8.62 us  [the longest x1 8.61 us: shards(): lax.ppermute((two.astype(F32) + far.astype(F32)).astype(BF), 'col', flip(2))]
    ppermute x3 -> x4, starting transfers between devices: 3.32 us -> 4.18 us  [the longest x1 2.72 us: shards(): three = lax.ppermute(three, 'col', flip(3))]
  transfers between devices with their start and end apart: 13 -> 14, of which waited for: 5 -> 5; matrix products, arithmetic and copies ran while one was open for 1% -> 1% of each run, Pallas kernels for 24% -> 25%
where the time goes in v9:
time: 128 us; the launch traced here: 127 us
  Pallas kernels  48.2 us (38%)
  starting transfers between devices  40 us (31%)
  waiting for transfers between devices  35 us (27%)
  local copies, waits for them, and re-layouts  1.67 us (1%)
  other arithmetic  1.31 us (1%)
    all_to_all x1, waiting for transfers between devices, shards(): packed = lax.all_to_all(packed, 'row', 0, 0, tiled=True)  21.9 us
    all_to_all x2, starting transfers between devices, shards(): lax.all_to_all(v.reshape(2 * n_row, rows, pair.shape[1]), ('row', 'col'),...  16.9 us
    pallas_call x1, Pallas kernels, attend(): pl.pallas_call(functools.partial(attend_kernel, n_col, n_chip, per, size)...  16.5 us
    pallas_call x1, Pallas kernels, transition(): pl.pallas_call(transition_kernel, grid_spec=pltpu.PrefetchScalarGridSpec(...  9.55 us
    ppermute x1, waiting for transfers between devices, shards(): lax.ppermute((two.astype(F32) + far.astype(F32)).astype(BF), 'col', flip(2))  8.61 us
    pallas_call x1, Pallas kernels, project(): pl.pallas_call(project_kernel, grid_spec=pltpu.PrefetchScalarGridSpec(num...  7.65 us
    all_to_all x1, starting transfers between devices, shards(): attended = lax.all_to_all(attended, 'row', 0, 0, tiled=True)  7.43 us
    pallas_call x1, Pallas kernels, pair_stats(): pl.pallas_call(stats_kernel, grid=(rows // step,), in_specs=[pl.BlockSpec...  5.61 us
  transfers between devices with their start and end apart: 14, of which 5 were waited for; matrix products, arithmetic and copies ran while one was open for 1% of the time, Pallas kernels for 25%

profile of v9, /device:TPU:1, one launch (start us, length us, event | category | flops | bytes accessed | tf_op | source)
XLA Modules:
  0.0 127.0 jit_solution(11498768996282966649)
XLA Ops:
  0.6 1.5 %collective-permute-start = (bf16[6,64,768]{2,1,0:T(8,128)(2,1)}, bf16[6,64,768]{2,1,0:T(8,128)(2,1)S(1)}, u32[]{:S(2)}, u32[]{:S(2)}) collective-permute-start(bf16[6,64,768]{2,1,0:T(8,128)(2,1)} %single_ref.1), channel_id=1, source_target_pairs={{0,8},{8,0},{16,24},{24,16},{32,40},{40,32},{48,56},{56,48},{64,72... | collective-permute-start | bytes 1769480 | tf_op jit(solution)/shard_map/ppermute | solution.py:352
  2.2 0.1 collective-permute-start.1
  2.2 3.7 %shard_map.96 = bf16[16,2,64,128]{3,2,1,0:T(8,128)(2,1)} custom-call(bf16[64,128,128]{2,1,0:T(8,128)(2,1)} %pair_ref.2, bf16[16,128]{1,0:T(8,128)(2,1)} %bitcast.15), custom_call_target="tpu_custom_call" | custom-call | tf_op jit(solution)/shard_map/pallas_call | solution.py:50
  5.9 8.4 %all-to-all-start.1 = ((bf16[32,64,128]{2,1,0:T(8,128)(2,1)}), bf16[32,64,128]{2,1,0:T(8,128)(2,1)S(1)}, u32[]{:S(2)}, u32[]{:S(2)}) async-start(bf16[32,64,128]{2,1,0:T(8,128)(2,1)} %bitcast.18), calls=%async_computation.1 | async-start | bytes 1048576 | tf_op jit(solution)/shard_map/all_to_all | solution.py:355
  14.4 0.0 collective-permute-done.got_ref
  14.4 7.7 %shard_map.95 = (bf16[16,192,384]{2,1,0:T(8,128)(2,1)}, bf16[3,128,768]{2,1,0:T(8,128)(2,1)S(1)}) custom-call(s32[1]{0:T(128)} %bitcast.core_ref, bf16[6,64,768]{2,1,0:T(8,128)(2,1)S(1)} %copy-done, bf16[6,64,768]{2,1,0:T(8,128)(2,1)S(1)} %collective-permute-done.got_ref, bf16[6,64,768]{2,1,0:T(8,128)(2,1)S(1)} %copy-done.1, ...), custom_call_target="tpu_custom_call" | custom-call | tf_op jit(solution)/shard_map/pallas_call | solution.py:145
  22.1 0.8 copy-done.2
  22.9 2.6 %all-to-all-done.1 = bf16[32,64,128]{2,1,0:T(8,128)(2,1)S(1)} async-done(((bf16[32,64,128]{2,1,0:T(8,128)(2,1)}), bf16[32,64,128]{2,1,0:T(8,128)(2,1)S(1)}, u32[]{:S(2)}, u32[]{:S(2)}) %all-to-all-start.1) | async-done | bytes 524320 | tf_op jit(solution)/shard_map/all_to_all | solution.py:355
  25.5 5.0 %all-to-all-start = ((bf16[16,192,384]{2,1,0:T(8,128)(2,1)}), bf16[16,192,384]{2,1,0:T(8,128)(2,1)}, u32[]{:S(2)}, u32[]{:S(2)}) async-start(bf16[16,192,384]{2,1,0:T(8,128)(2,1)} %get-tuple-element.24), calls=%async_computation | async-start | bytes 4718592 | tf_op jit(solution)/shard_map/all_to_all | solution.py:364
  30.5 1.3 %collective-permute-start.2 = (bf16[16,2,64,128]{3,2,1,0:T(8,128)(2,1)S(1)}, bf16[16,2,64,128]{3,2,1,0:T(8,128)(2,1)S(1)}, u32[]{:S(2)}, u32[]{:S(2)}) collective-permute-start(bf16[16,2,64,128]{3,2,1,0:T(8,128)(2,1)S(1)} %bitcast.10), channel_id=1, source_target_pairs={{0,1},{1,0},{2,3},{3,2},{4,5},{5,4},{6,7},{7,6},{8,9},{9,8},{10,11... | collective-permute-start | bytes 1572872 | tf_op jit(solution)/shard_map/ppermute | solution.py:360
  31.8 2.6 %collective-permute-start.3 = (bf16[16,2,64,128]{3,2,1,0:T(8,128)(2,1)S(1)}, bf16[16,2,64,128]{3,2,1,0:T(8,128)(2,1)S(1)}, u32[]{:S(2)}, u32[]{:S(2)}) collective-permute-start(bf16[16,2,64,128]{3,2,1,0:T(8,128)(2,1)S(1)} %bitcast.11), channel_id=1, source_target_pairs={{0,2},{1,3},{2,0},{3,1},{4,6},{5,7},{6,4},{7,5},{8,10},{9,11},{10,... | collective-permute-start | bytes 1572872 | tf_op jit(solution)/shard_map/ppermute | solution.py:360
  34.4 0.0 collective-permute-start.4
  34.4 5.6 %shard_map.97 = (f32[64,128,128]{2,1,0:T(8,128)}, f32[64,128]{1,0:T(8,128)}) custom-call(bf16[64,128,128]{2,1,0:T(8,128)(2,1)} %pair_ref.2), custom_call_target="tpu_custom_call" | custom-call | tf_op jit(solution)/shard_map/pallas_call | solution.py:69
  40.0 21.9 %all-to-all-done = bf16[16,192,384]{2,1,0:T(8,128)(2,1)} async-done(((bf16[16,192,384]{2,1,0:T(8,128)(2,1)}), bf16[16,192,384]{2,1,0:T(8,128)(2,1)}, u32[]{:S(2)}, u32[]{:S(2)}) %all-to-all-start) | async-done | bytes 2359328 | tf_op jit(solution)/shard_map/all_to_all | solution.py:364
  62.0 16.5 %shard_map.98 = (bf16[8,2,48,384]{3,2,1,0:T(8,128)(2,1)}, bf16[16,2,64,128]{3,2,1,0:T(8,128)(2,1)S(1)}, bf16[16,2,64,128]{3,2,1,0:T(8,128)(2,1)S(1)}, bf16[16,2,...) custom-call(s32[1]{0:T(128)} %bitcast.1.c_ref, ...), custom_call_target="tpu_custom_call" | custom-call | tf_op jit(solution)/shard_map/pallas_call | solution.py:318
  78.5 0.1 collective-permute-start.7
  78.6 2.7 %collective-permute-start.6 = (bf16[16,2,64,128]{3,2,1,0:T(8,128)(2,1)}, bf16[16,2,64,128]{3,2,1,0:T(8,128)(2,1)S(1)}, u32[]{:S(2)}, u32[]{:S(2)}) collective-permute-start(bf16[16,2,64,128]{3,2,1,0:T(8,128)(2,1)} %get-tuple-element.32), channel_id=1, source_target_pairs={{0,3},{1,2},{2,1},{3,0},{4,7},{5,6},{6,5},{7,4},{8,11},{9,10},{10,... | collective-permute-start | bytes 1572872 | tf_op jit(solution)/shard_map/ppermute | solution.py:371
  81.3 7.4 %all-to-all-start.2 = ((bf16[16,48,384]{2,1,0:T(8,128)(2,1)}), bf16[16,48,384]{2,1,0:T(8,128)(2,1)S(1)}, u32[]{:S(2)}, u32[]{:S(2)}) async-start(bf16[16,48,384]{2,1,0:T(8,128)(2,1)} %bitcast.6), calls=%async_computation.2 | async-start | bytes 1179648 | tf_op jit(solution)/shard_map/all_to_all | solution.py:373
  88.7 0.0 collective-permute-done.7
  88.7 0.1 add_convert_fusion.1
  88.8 1.4 %collective-permute-start.8 = (bf16[16,64,128]{2,1,0:T(8,128)(2,1)S(1)}, bf16[16,64,128]{2,1,0:T(8,128)(2,1)S(1)}, u32[]{:S(2)}, u32[]{:S(2)}) collective-permute-start(bf16[16,64,128]{2,1,0:T(8,128)(2,1)S(1)} %add_convert_fusion.1), channel_id=1, source_target_pairs={{0,2},{1,3},{2,0},{3,1},{4,6},{5,7},{6,4},{7,5},{8,10},{9,11},{10,... | collective-permute-start | bytes 786440 | tf_op jit(solution)/shard_map/ppermute | solution.py:374
  90.2 8.6 %collective-permute-done.8 = bf16[16,64,128]{2,1,0:T(8,128)(2,1)S(1)} collective-permute-done((bf16[16,64,128]{2,1,0:T(8,128)(2,1)S(1)}, bf16[16,64,128]{2,1,0:T(8,128)(2,1)S(1)}, u32[]{:S(2)}, u32[]{:S(2)}) %collective-permute-start.8) | collective-permute-done | bytes 262176 | tf_op jit(solution)/shard_map/ppermute | solution.py:374
  98.9 1.2 add_convert_fusion
  100.1 0.3 all-to-all-done.2
  100.4 8.5 %all-to-all-start.3 = ((bf16[32,64,128]{2,1,0:T(8,128)(2,1)}), bf16[32,64,128]{2,1,0:T(8,128)(2,1)S(1)}, u32[]{:S(2)}, u32[]{:S(2)}) async-start(bf16[32,64,128]{2,1,0:T(8,128)(2,1)} %bitcast.8), calls=%async_computation.3 | async-start | bytes 1048576 | tf_op jit(solution)/shard_map/all_to_all | solution.py:355
  108.9 0.0 copy-start.4
  108.9 9.5 %shard_map.99 = (bf16[6,64,768]{2,1,0:T(8,128)(2,1)}, bf16[3,64,768]{2,1,0:T(8,128)(2,1)}) custom-call(s32[1]{0:T(128)} %bitcast.core_ref, bf16[3,128,768]{2,1,0:T(8,128)(2,1)} %copy-done.2, bf16[768,384]{1,0:T(8,128)(2,1)} %bitcast.17, bf16[768,768]{1,0:T(8,128)(2,1)} %wo_ref.1, bf16[768,3072]{1,0:T(8,128)(2,1)} %wu_ref.1, bf16[768,3072]{1,0:T(8,128)(2,1)} %wu_ref.1, ...), custom_call_target="tpu_custom_call" | custom-call | tf_op jit(solution)/shard_map/pallas_call | solution.py:193
  118.5 1.5 %all-to-all-done.3 = bf16[32,64,128]{2,1,0:T(8,128)(2,1)S(1)} async-done(((bf16[32,64,128]{2,1,0:T(8,128)(2,1)}), bf16[32,64,128]{2,1,0:T(8,128)(2,1)S(1)}, u32[]{:S(2)}, u32[]{:S(2)}) %all-to-all-start.3) | async-done | bytes 524320 | tf_op jit(solution)/shard_map/all_to_all | solution.py:355
  120.0 0.9 collective-permute-start.9
  120.9 5.2 %shard_map.100 = f32[64,128,128]{2,1,0:T(8,128)} custom-call(f32[64,128,128]{2,1,0:T(8,128)} %get-tuple-element.41.normed_ref, f32[64,128]{1,0:T(8,128)S(1)} %copy-done.3, bf16[16,2,64,128]{3,2,1,0:T(8,128)(2,1)S(1)} %bitcast.14, bf16[16,128]{1,0:T(8,128)(2,1)S(1)} %bitcast.16), custom_call_target="tpu_custom_call" | custom-call | tf_op jit(solution)/shard_map/pallas_call | solution.py:98
  126.1 0.0 copy-start.7
  126.1 0.8 copy-done.7
  (23 shorter events, 0.1 us)
Async XLA Ops:
  0.6 13.8 %copy-start = (bf16[6,64,768]{2,1,0:T(8,128)(2,1)S(1)}, bf16[6,64,768]{2,1,0:T(8,128)(2,1)}, u32[]{:S(2)}) copy-start(bf16[6,64,768]{2,1,0:T(8,128)(2,1)} %single_ref.1) | copy-start | bytes 1769476
  0.6 13.8 %copy-start.1 = (bf16[6,64,768]{2,1,0:T(8,128)(2,1)S(1)}, bf16[6,64,768]{2,1,0:T(8,128)(2,1)}, u32[]{:S(2)}) copy-start(bf16[6,64,768]{2,1,0:T(8,128)(2,1)} %cot_ref.1) | copy-start | bytes 1769476
  0.6 13.7 %collective-permute-start = (bf16[6,64,768]{2,1,0:T(8,128)(2,1)}, bf16[6,64,768]{2,1,0:T(8,128)(2,1)S(1)}, u32[]{:S(2)}, u32[]{:S(2)}) collective-permute-start(bf16[6,64,768]{2,1,0:T(8,128)(2,1)} %single_ref.1), channel_id=1, source_target_pairs={{0,8},{8,0},{16,24},{24,16},{32,40},{40,32},{48,56},{56,48},{64,72... | collective-permute-start | bytes 1769480 | tf_op jit(solution)/shard_map/ppermute | solution.py:352
  2.2 12.2 %collective-permute-start.1 = (bf16[6,64,768]{2,1,0:T(8,128)(2,1)}, bf16[6,64,768]{2,1,0:T(8,128)(2,1)S(1)}, u32[]{:S(2)}, u32[]{:S(2)}) collective-permute-start(bf16[6,64,768]{2,1,0:T(8,128)(2,1)} %cot_ref.1), channel_id=1, source_target_pairs={{0,8},{8,0},{16,24},{24,16},{32,40},{40,32},{48,56},{56,48},{64,72... | collective-permute-start | bytes 1769480 | tf_op jit(solution)/shard_map/ppermute | solution.py:353
  5.9 19.5 %all-to-all-start.1 = ((bf16[32,64,128]{2,1,0:T(8,128)(2,1)}), bf16[32,64,128]{2,1,0:T(8,128)(2,1)S(1)}, u32[]{:S(2)}, u32[]{:S(2)}) async-start(bf16[32,64,128]{2,1,0:T(8,128)(2,1)} %bitcast.18), calls=%async_computation.1 | async-start | bytes 1048576 | tf_op jit(solution)/shard_map/all_to_all | solution.py:355
  22.1 0.8 copy-start.2
  25.5 36.5 %all-to-all-start = ((bf16[16,192,384]{2,1,0:T(8,128)(2,1)}), bf16[16,192,384]{2,1,0:T(8,128)(2,1)}, u32[]{:S(2)}, u32[]{:S(2)}) async-start(bf16[16,192,384]{2,1,0:T(8,128)(2,1)} %get-tuple-element.24), calls=%async_computation | async-start | bytes 4718592 | tf_op jit(solution)/shard_map/all_to_all | solution.py:364
  30.5 31.4 %collective-permute-start.2 = (bf16[16,2,64,128]{3,2,1,0:T(8,128)(2,1)S(1)}, bf16[16,2,64,128]{3,2,1,0:T(8,128)(2,1)S(1)}, u32[]{:S(2)}, u32[]{:S(2)}) collective-permute-start(bf16[16,2,64,128]{3,2,1,0:T(8,128)(2,1)S(1)} %bitcast.10), channel_id=1, source_target_pairs={{0,1},{1,0},{2,3},{3,2},{4,5},{5,4},{6,7},{7,6},{8,9},{9,8},{10,11... | collective-permute-start | bytes 1572872 | tf_op jit(solution)/shard_map/ppermute | solution.py:360
  31.8 30.2 %collective-permute-start.3 = (bf16[16,2,64,128]{3,2,1,0:T(8,128)(2,1)S(1)}, bf16[16,2,64,128]{3,2,1,0:T(8,128)(2,1)S(1)}, u32[]{:S(2)}, u32[]{:S(2)}) collective-permute-start(bf16[16,2,64,128]{3,2,1,0:T(8,128)(2,1)S(1)} %bitcast.11), channel_id=1, source_target_pairs={{0,2},{1,3},{2,0},{3,1},{4,6},{5,7},{6,4},{7,5},{8,10},{9,11},{10,... | collective-permute-start | bytes 1572872 | tf_op jit(solution)/shard_map/ppermute | solution.py:360
  34.4 27.5 %collective-permute-start.4 = (bf16[16,2,64,128]{3,2,1,0:T(8,128)(2,1)S(1)}, bf16[16,2,64,128]{3,2,1,0:T(8,128)(2,1)S(1)}, u32[]{:S(2)}, u32[]{:S(2)}) collective-permute-start(bf16[16,2,64,128]{3,2,1,0:T(8,128)(2,1)S(1)} %bitcast.12), channel_id=1, source_target_pairs={{0,3},{1,2},{2,1},{3,0},{4,7},{5,6},{6,5},{7,4},{8,11},{9,10},{10,... | collective-permute-start | bytes 1572872 | tf_op jit(solution)/shard_map/ppermute | solution.py:360
  78.5 10.2 %collective-permute-start.7 = (bf16[16,64,128]{2,1,0:T(8,128)(2,1)}, bf16[16,64,128]{2,1,0:T(8,128)(2,1)S(1)}, u32[]{:S(2)}, u32[]{:S(2)}) collective-permute-start(bf16[16,64,128]{2,1,0:T(8,128)(2,1)} %get-tuple-element.34), channel_id=1, source_target_pairs={{0,4},{1,5},{2,6},{3,7},{4,0},{5,1},{6,2},{7,3},{8,12},{9,13},{10,... | collective-permute-start | bytes 786440 | tf_op jit(solution)/shard_map/ppermute | solution.py:369
  78.6 20.3 %collective-permute-start.6 = (bf16[16,2,64,128]{3,2,1,0:T(8,128)(2,1)}, bf16[16,2,64,128]{3,2,1,0:T(8,128)(2,1)S(1)}, u32[]{:S(2)}, u32[]{:S(2)}) collective-permute-start(bf16[16,2,64,128]{3,2,1,0:T(8,128)(2,1)} %get-tuple-element.32), channel_id=1, source_target_pairs={{0,3},{1,2},{2,1},{3,0},{4,7},{5,6},{6,5},{7,4},{8,11},{9,10},{10,... | collective-permute-start | bytes 1572872 | tf_op jit(solution)/shard_map/ppermute | solution.py:371
  81.3 17.6 %collective-permute-start.5 = (bf16[16,2,64,128]{3,2,1,0:T(8,128)(2,1)S(1)}, bf16[16,2,64,128]{3,2,1,0:T(8,128)(2,1)S(1)}, u32[]{:S(2)}, u32[]{:S(2)}) collective-permute-start(bf16[16,2,64,128]{3,2,1,0:T(8,128)(2,1)S(1)} %get-tuple-element.31), channel_id=1, source_target_pairs={{0,1},{1,0},{2,3},{3,2},{4,5},{5,4},{6,7},{7,6},{8,9},{9,8},{10,11... | collective-permute-start | bytes 1572872 | tf_op jit(solution)/shard_map/ppermute | solution.py:370
  81.3 19.1 %all-to-all-start.2 = ((bf16[16,48,384]{2,1,0:T(8,128)(2,1)}), bf16[16,48,384]{2,1,0:T(8,128)(2,1)S(1)}, u32[]{:S(2)}, u32[]{:S(2)}) async-start(bf16[16,48,384]{2,1,0:T(8,128)(2,1)} %bitcast.6), calls=%async_computation.2 | async-start | bytes 1179648 | tf_op jit(solution)/shard_map/all_to_all | solution.py:373
  88.8 10.0 %collective-permute-start.8 = (bf16[16,64,128]{2,1,0:T(8,128)(2,1)S(1)}, bf16[16,64,128]{2,1,0:T(8,128)(2,1)S(1)}, u32[]{:S(2)}, u32[]{:S(2)}) collective-permute-start(bf16[16,64,128]{2,1,0:T(8,128)(2,1)S(1)} %add_convert_fusion.1), channel_id=1, source_target_pairs={{0,2},{1,3},{2,0},{3,1},{4,6},{5,7},{6,4},{7,5},{8,10},{9,11},{10,... | collective-permute-start | bytes 786440 | tf_op jit(solution)/shard_map/ppermute | solution.py:374
  100.4 8.5 %copy-start.5 = (bf16[16,48,384]{2,1,0:T(8,128)(2,1)}, bf16[16,48,384]{2,1,0:T(8,128)(2,1)S(1)}, u32[]{:S(2)}) copy-start(bf16[16,48,384]{2,1,0:T(8,128)(2,1)S(1)} %all-to-all-done.2) | copy-start | bytes 1769476
  100.4 19.6 %all-to-all-start.3 = ((bf16[32,64,128]{2,1,0:T(8,128)(2,1)}), bf16[32,64,128]{2,1,0:T(8,128)(2,1)S(1)}, u32[]{:S(2)}, u32[]{:S(2)}) async-start(bf16[32,64,128]{2,1,0:T(8,128)(2,1)} %bitcast.8), calls=%async_computation.3 | async-start | bytes 1048576 | tf_op jit(solution)/shard_map/all_to_all | solution.py:355
  108.9 12.0 %copy-start.3 = (f32[64,128]{1,0:T(8,128)S(1)}, f32[64,128]{1,0:T(8,128)}, u32[]{:S(2)}) copy-start(f32[64,128]{1,0:T(8,128)} %get-tuple-element.42.scaled_ref) | copy-start | bytes 98308
  108.9 11.9 %copy-start.4 = (bf16[128,16]{0,1:T(8,128)(2,1)S(1)}, bf16[128,16]{0,1:T(8,128)(2,1)}, u32[]{:S(2)}) copy-start(bf16[128,16]{0,1:T(8,128)(2,1)} %param.9) | copy-start | bytes 12292
  120.0 6.1 %collective-permute-start.9 = (bf16[3,64,768]{2,1,0:T(8,128)(2,1)}, bf16[3,64,768]{2,1,0:T(8,128)(2,1)S(1)}, u32[]{:S(2)}, u32[]{:S(2)}) collective-permute-start(bf16[3,64,768]{2,1,0:T(8,128)(2,1)} %get-tuple-element.40), channel_id=1, source_target_pairs={{0,8},{8,0},{16,24},{24,16},{32,40},{40,32},{48,56},{56,48},{64,72... | collective-permute-start | bytes 884744 | tf_op jit(solution)/shard_map/ppermute | solution.py:384
  120.9 5.2 %copy-start.6 = (bf16[6,64,768]{2,1,0:T(8,128)(2,1)S(1)}, bf16[6,64,768]{2,1,0:T(8,128)(2,1)}, u32[]{:S(2)}) copy-start(bf16[6,64,768]{2,1,0:T(8,128)(2,1)} %get-tuple-element.39) | copy-start | bytes 1769476
  126.1 0.8 copy-start.7

commit v10 on v9

--- a/solution.py
+++ b/solution.py
@@ -59,7 +59,7 @@
 def stats_kernel(pair_ref, normed_ref, scaled_ref):
     rows, cols, chans = pair_ref.shape
     normed, scaled = unit(pair_ref[...].astype(F32).reshape(rows * cols, chans))
-    normed_ref[...] = normed.reshape(rows, cols, chans)
+    normed_ref[...] = normed.reshape(rows, cols, chans).astype(BF)
     lanes = jnp.broadcast_to(scaled, (rows * cols, chans)).reshape(rows, cols, chans)
     for i in range(rows):
         scaled_ref[i : i + 1] = lanes[i].T[:1]
@@ -70,7 +70,7 @@
         stats_kernel, grid=(rows // step,),
         in_specs=[pl.BlockSpec((step, cols, chans), lambda i: (i, 0, 0))],
         out_specs=[pl.BlockSpec((step, cols, chans), lambda i: (i, 0, 0)), pl.BlockSpec((step, cols), lambda i: (i, 0))],
-        out_shape=[jax.ShapeDtypeStruct((rows, cols, chans), F32), jax.ShapeDtypeStruct((rows, cols), F32)],
+        out_shape=[jax.ShapeDtypeStruct((rows, cols, chans), BF), jax.ShapeDtypeStruct((rows, cols), F32)],
         compiler_params=pltpu.CompilerParams(dimension_semantics=("arbitrary",), vmem_limit_bytes=60 << 20),
     )(pair)
 
@@ -87,7 +87,7 @@
     both = jnp.concatenate([high, low, high, low], axis=0)
     weight = jnp.concatenate([w_high, w_high, w_low, w_low], axis=0)
     centred = lax.dot_general(both, weight, (((0,), (0,)), ((), ())), preferred_element_type=F32)
-    normed = normed_ref[...].reshape(rows * cols, chans)
+    normed = normed_ref[...].astype(F32).reshape(rows * cols, chans)
     along = jnp.mean(centred * normed, axis=-1, keepdims=True)
     out_ref[...] = (centred - normed * along).reshape(rows, cols, chans)
 

time: 128 us -> 126 us (0.984)
  Pallas kernels: 48.2 us -> 46.6 us
    pallas_call x1, Pallas kernels: 5.23 us -> 3.65 us  [pair_back(): pl.pallas_call(back_kernel, grid=(rows // step,), in_specs=[pl.BlockSpec(...]
  transfers between devices with their start and end apart: 14 -> 14, of which waited for: 5 -> 5; matrix products, arithmetic and copies ran while one was open for 1% -> 1% of each run, Pallas kernels for 25% -> 24%
where the time goes in v10:
time: 126 us; the launch traced here: 125 us
  Pallas kernels  46.6 us (37%)
  starting transfers between devices  39.9 us (32%)
  waiting for transfers between devices  35.1 us (28%)
  local copies, waits for them, and re-layouts  1.68 us (1%)
  other arithmetic  1.3 us (1%)
    all_to_all x1, waiting for transfers between devices, shards(): packed = lax.all_to_all(packed, 'row', 0, 0, tiled=True)  22.1 us
    all_to_all x2, starting transfers between devices, shards(): lax.all_to_all(v.reshape(2 * n_row, rows, pair.shape[1]), ('row', 'col'),...  16.9 us
    pallas_call x1, Pallas kernels, attend(): pl.pallas_call(functools.partial(attend_kernel, n_col, n_chip, per, size)...  16.6 us
    pallas_call x1, Pallas kernels, transition(): pl.pallas_call(transition_kernel, grid_spec=pltpu.PrefetchScalarGridSpec(...  9.65 us
    ppermute x1, waiting for transfers between devices, shards(): lax.ppermute((two.astype(F32) + far.astype(F32)).astype(BF), 'col', flip(2))  8.62 us
    pallas_call x1, Pallas kernels, project(): pl.pallas_call(project_kernel, grid_spec=pltpu.PrefetchScalarGridSpec(num...  7.65 us
    all_to_all x1, starting transfers between devices, shards(): attended = lax.all_to_all(attended, 'row', 0, 0, tiled=True)  7.43 us
    pallas_call x1, Pallas kernels, pair_stats(): pl.pallas_call(stats_kernel, grid=(rows // step,), in_specs=[pl.BlockSpec...  5.38 us
  transfers between devices with their start and end apart: 14, of which 5 were waited for; matrix products, arithmetic and copies ran while one was open for 1% of the time, Pallas kernels for 24%

profile of v10, /device:TPU:1, one launch (start us, length us, event | category | flops | bytes accessed | tf_op | source)
XLA Modules:
  0.0 125.4 jit_solution(15347642887409045367)
XLA Ops:
  0.6 1.5 %collective-permute-start = (bf16[6,64,768]{2,1,0:T(8,128)(2,1)}, bf16[6,64,768]{2,1,0:T(8,128)(2,1)S(1)}, u32[]{:S(2)}, u32[]{:S(2)}) collective-permute-start(bf16[6,64,768]{2,1,0:T(8,128)(2,1)} %single_ref.1), channel_id=1, source_target_pairs={{0,8},{8,0},{16,24},{24,16},{32,40},{40,32},{48,56},{56,48},{64,72... | collective-permute-start | bytes 1769480 | tf_op jit(solution)/shard_map/ppermute | solution.py:352
  2.2 0.1 collective-permute-start.1
  2.2 3.7 %shard_map.96 = bf16[16,2,64,128]{3,2,1,0:T(8,128)(2,1)} custom-call(bf16[64,128,128]{2,1,0:T(8,128)(2,1)} %pair_ref.2, bf16[16,128]{1,0:T(8,128)(2,1)} %bitcast.15), custom_call_target="tpu_custom_call" | custom-call | tf_op jit(solution)/shard_map/pallas_call | solution.py:50
  5.9 8.4 %all-to-all-start.1 = ((bf16[32,64,128]{2,1,0:T(8,128)(2,1)}), bf16[32,64,128]{2,1,0:T(8,128)(2,1)S(1)}, u32[]{:S(2)}, u32[]{:S(2)}) async-start(bf16[32,64,128]{2,1,0:T(8,128)(2,1)} %bitcast.18), calls=%async_computation.1 | async-start | bytes 1048576 | tf_op jit(solution)/shard_map/all_to_all | solution.py:355
  14.4 0.0 collective-permute-done.1.gotc_ref
  14.4 7.7 %shard_map.95 = (bf16[16,192,384]{2,1,0:T(8,128)(2,1)}, bf16[3,128,768]{2,1,0:T(8,128)(2,1)S(1)}) custom-call(s32[1]{0:T(128)} %bitcast.core_ref, bf16[6,64,768]{2,1,0:T(8,128)(2,1)S(1)} %copy-done.1, bf16[6,64,768]{2,1,0:T(8,128)(2,1)S(1)} %collective-permute-done.got_ref, bf16[6,64,768]{2,1,0:T(8,128)(2,1)S(1)} %copy-done.2, ...), custom_call_target="tpu_custom_call" | custom-call | tf_op jit(solution)/shard_map/pallas_call | solution.py:145
  22.1 0.8 copy-done.3
  22.9 2.6 %all-to-all-done.1 = bf16[32,64,128]{2,1,0:T(8,128)(2,1)S(1)} async-done(((bf16[32,64,128]{2,1,0:T(8,128)(2,1)}), bf16[32,64,128]{2,1,0:T(8,128)(2,1)S(1)}, u32[]{:S(2)}, u32[]{:S(2)}) %all-to-all-start.1) | async-done | bytes 524320 | tf_op jit(solution)/shard_map/all_to_all | solution.py:355
  25.5 5.0 %all-to-all-start = ((bf16[16,192,384]{2,1,0:T(8,128)(2,1)}), bf16[16,192,384]{2,1,0:T(8,128)(2,1)}, u32[]{:S(2)}, u32[]{:S(2)}) async-start(bf16[16,192,384]{2,1,0:T(8,128)(2,1)} %get-tuple-element.24), calls=%async_computation | async-start | bytes 4718592 | tf_op jit(solution)/shard_map/all_to_all | solution.py:364
  30.5 1.3 %collective-permute-start.2 = (bf16[16,2,64,128]{3,2,1,0:T(8,128)(2,1)S(1)}, bf16[16,2,64,128]{3,2,1,0:T(8,128)(2,1)S(1)}, u32[]{:S(2)}, u32[]{:S(2)}) collective-permute-start(bf16[16,2,64,128]{3,2,1,0:T(8,128)(2,1)S(1)} %bitcast.10), channel_id=1, source_target_pairs={{0,1},{1,0},{2,3},{3,2},{4,5},{5,4},{6,7},{7,6},{8,9},{9,8},{10,11... | collective-permute-start | bytes 1572872 | tf_op jit(solution)/shard_map/ppermute | solution.py:360
  31.8 2.6 %collective-permute-start.3 = (bf16[16,2,64,128]{3,2,1,0:T(8,128)(2,1)S(1)}, bf16[16,2,64,128]{3,2,1,0:T(8,128)(2,1)S(1)}, u32[]{:S(2)}, u32[]{:S(2)}) collective-permute-start(bf16[16,2,64,128]{3,2,1,0:T(8,128)(2,1)S(1)} %bitcast.11), channel_id=1, source_target_pairs={{0,2},{1,3},{2,0},{3,1},{4,6},{5,7},{6,4},{7,5},{8,10},{9,11},{10,... | collective-permute-start | bytes 1572872 | tf_op jit(solution)/shard_map/ppermute | solution.py:360
  34.4 5.4 %shard_map.97 = (bf16[64,128,128]{2,1,0:T(8,128)(2,1)}, f32[64,128]{1,0:T(8,128)}) custom-call(bf16[64,128,128]{2,1,0:T(8,128)(2,1)} %pair_ref.2), custom_call_target="tpu_custom_call" | custom-call | tf_op jit(solution)/shard_map/pallas_call | solution.py:69
  39.8 22.1 %all-to-all-done = bf16[16,192,384]{2,1,0:T(8,128)(2,1)} async-done(((bf16[16,192,384]{2,1,0:T(8,128)(2,1)}), bf16[16,192,384]{2,1,0:T(8,128)(2,1)}, u32[]{:S(2)}, u32[]{:S(2)}) %all-to-all-start) | async-done | bytes 2359328 | tf_op jit(solution)/shard_map/all_to_all | solution.py:364
  61.9 0.0 collective-permute-done.2.refs_1_
  61.9 0.0 collective-permute-done.3.refs_2_
  61.9 16.6 %shard_map.98 = (bf16[8,2,48,384]{3,2,1,0:T(8,128)(2,1)}, bf16[16,2,64,128]{3,2,1,0:T(8,128)(2,1)S(1)}, bf16[16,2,64,128]{3,2,1,0:T(8,128)(2,1)S(1)}, bf16[16,2,...) custom-call(s32[1]{0:T(128)} %bitcast.1.c_ref, ...), custom_call_target="tpu_custom_call" | custom-call | tf_op jit(solution)/shard_map/pallas_call | solution.py:318
  78.5 0.1 collective-permute-start.7
  78.6 2.7 %collective-permute-start.6 = (bf16[16,2,64,128]{3,2,1,0:T(8,128)(2,1)}, bf16[16,2,64,128]{3,2,1,0:T(8,128)(2,1)S(1)}, u32[]{:S(2)}, u32[]{:S(2)}) collective-permute-start(bf16[16,2,64,128]{3,2,1,0:T(8,128)(2,1)} %get-tuple-element.32), channel_id=1, source_target_pairs={{0,3},{1,2},{2,1},{3,0},{4,7},{5,6},{6,5},{7,4},{8,11},{9,10},{10,... | collective-permute-start | bytes 1572872 | tf_op jit(solution)/shard_map/ppermute | solution.py:371
  81.3 7.4 %all-to-all-start.2 = ((bf16[16,48,384]{2,1,0:T(8,128)(2,1)}), bf16[16,48,384]{2,1,0:T(8,128)(2,1)S(1)}, u32[]{:S(2)}, u32[]{:S(2)}) async-start(bf16[16,48,384]{2,1,0:T(8,128)(2,1)} %bitcast.6), calls=%async_computation.2 | async-start | bytes 1179648 | tf_op jit(solution)/shard_map/all_to_all | solution.py:373
  88.8 0.1 add_convert_fusion.1
  88.8 1.4 %collective-permute-start.8 = (bf16[16,64,128]{2,1,0:T(8,128)(2,1)S(1)}, bf16[16,64,128]{2,1,0:T(8,128)(2,1)S(1)}, u32[]{:S(2)}, u32[]{:S(2)}) collective-permute-start(bf16[16,64,128]{2,1,0:T(8,128)(2,1)S(1)} %add_convert_fusion.1), channel_id=1, source_target_pairs={{0,2},{1,3},{2,0},{3,1},{4,6},{5,7},{6,4},{7,5},{8,10},{9,11},{10,... | collective-permute-start | bytes 786440 | tf_op jit(solution)/shard_map/ppermute | solution.py:374
  90.2 8.6 %collective-permute-done.8 = bf16[16,64,128]{2,1,0:T(8,128)(2,1)S(1)} collective-permute-done((bf16[16,64,128]{2,1,0:T(8,128)(2,1)S(1)}, bf16[16,64,128]{2,1,0:T(8,128)(2,1)S(1)}, u32[]{:S(2)}, u32[]{:S(2)}) %collective-permute-start.8) | collective-permute-done | bytes 262176 | tf_op jit(solution)/shard_map/ppermute | solution.py:374
  98.9 1.2 add_convert_fusion
  100.1 0.3 all-to-all-done.2
  100.4 8.5 %all-to-all-start.3 = ((bf16[32,64,128]{2,1,0:T(8,128)(2,1)}), bf16[32,64,128]{2,1,0:T(8,128)(2,1)S(1)}, u32[]{:S(2)}, u32[]{:S(2)}) async-start(bf16[32,64,128]{2,1,0:T(8,128)(2,1)} %bitcast.8), calls=%async_computation.3 | async-start | bytes 1048576 | tf_op jit(solution)/shard_map/all_to_all | solution.py:355
  108.9 0.0 copy-start.5
  109.0 9.6 %shard_map.99 = (bf16[6,64,768]{2,1,0:T(8,128)(2,1)}, bf16[3,64,768]{2,1,0:T(8,128)(2,1)}) custom-call(s32[1]{0:T(128)} %bitcast.core_ref, bf16[3,128,768]{2,1,0:T(8,128)(2,1)} %copy-done.3, bf16[768,384]{1,0:T(8,128)(2,1)} %bitcast.17, bf16[768,768]{1,0:T(8,128)(2,1)} %wo_ref.1, bf16[768,3072]{1,0:T(8,128)(2,1)} %wu_ref.1, bf16[768,3072]{1,0:T(8,128)(2,1)} %wu_ref.1, ...), custom_call_target="tpu_custom_call" | custom-call | tf_op jit(solution)/shard_map/pallas_call | solution.py:193
  118.6 1.4 %all-to-all-done.3 = bf16[32,64,128]{2,1,0:T(8,128)(2,1)S(1)} async-done(((bf16[32,64,128]{2,1,0:T(8,128)(2,1)}), bf16[32,64,128]{2,1,0:T(8,128)(2,1)S(1)}, u32[]{:S(2)}, u32[]{:S(2)}) %all-to-all-start.3) | async-done | bytes 524320 | tf_op jit(solution)/shard_map/all_to_all | solution.py:355
  120.0 0.9 collective-permute-start.9
  120.9 3.6 %shard_map.100 = f32[64,128,128]{2,1,0:T(8,128)} custom-call(bf16[64,128,128]{2,1,0:T(8,128)(2,1)S(1)} %copy-done, f32[64,128]{1,0:T(8,128)S(1)} %copy-done.4, bf16[16,2,64,128]{3,2,1,0:T(8,128)(2,1)S(1)} %bitcast.14, bf16[16,128]{1,0:T(8,128)(2,1)S(1)} %bitcast.16), custom_call_target="tpu_custom_call" | custom-call | tf_op jit(solution)/shard_map/pallas_call | solution.py:98
  124.6 0.0 copy-start.8
  124.6 0.8 copy-done.8
  (25 shorter events, 0.1 us)
Async XLA Ops:
  0.6 13.8 %copy-start.1 = (bf16[6,64,768]{2,1,0:T(8,128)(2,1)S(1)}, bf16[6,64,768]{2,1,0:T(8,128)(2,1)}, u32[]{:S(2)}) copy-start(bf16[6,64,768]{2,1,0:T(8,128)(2,1)} %single_ref.1) | copy-start | bytes 1769476
  0.6 13.8 %copy-start.2 = (bf16[6,64,768]{2,1,0:T(8,128)(2,1)S(1)}, bf16[6,64,768]{2,1,0:T(8,128)(2,1)}, u32[]{:S(2)}) copy-start(bf16[6,64,768]{2,1,0:T(8,128)(2,1)} %cot_ref.1) | copy-start | bytes 1769476
  0.6 13.7 %collective-permute-start = (bf16[6,64,768]{2,1,0:T(8,128)(2,1)}, bf16[6,64,768]{2,1,0:T(8,128)(2,1)S(1)}, u32[]{:S(2)}, u32[]{:S(2)}) collective-permute-start(bf16[6,64,768]{2,1,0:T(8,128)(2,1)} %single_ref.1), channel_id=1, source_target_pairs={{0,8},{8,0},{16,24},{24,16},{32,40},{40,32},{48,56},{56,48},{64,72... | collective-permute-start | bytes 1769480 | tf_op jit(solution)/shard_map/ppermute | solution.py:352
  2.2 12.2 %collective-permute-start.1 = (bf16[6,64,768]{2,1,0:T(8,128)(2,1)}, bf16[6,64,768]{2,1,0:T(8,128)(2,1)S(1)}, u32[]{:S(2)}, u32[]{:S(2)}) collective-permute-start(bf16[6,64,768]{2,1,0:T(8,128)(2,1)} %cot_ref.1), channel_id=1, source_target_pairs={{0,8},{8,0},{16,24},{24,16},{32,40},{40,32},{48,56},{56,48},{64,72... | collective-permute-start | bytes 1769480 | tf_op jit(solution)/shard_map/ppermute | solution.py:353
  5.9 19.5 %all-to-all-start.1 = ((bf16[32,64,128]{2,1,0:T(8,128)(2,1)}), bf16[32,64,128]{2,1,0:T(8,128)(2,1)S(1)}, u32[]{:S(2)}, u32[]{:S(2)}) async-start(bf16[32,64,128]{2,1,0:T(8,128)(2,1)} %bitcast.18), calls=%async_computation.1 | async-start | bytes 1048576 | tf_op jit(solution)/shard_map/all_to_all | solution.py:355
  22.1 0.8 copy-start.3
  25.5 36.5 %all-to-all-start = ((bf16[16,192,384]{2,1,0:T(8,128)(2,1)}), bf16[16,192,384]{2,1,0:T(8,128)(2,1)}, u32[]{:S(2)}, u32[]{:S(2)}) async-start(bf16[16,192,384]{2,1,0:T(8,128)(2,1)} %get-tuple-element.24), calls=%async_computation | async-start | bytes 4718592 | tf_op jit(solution)/shard_map/all_to_all | solution.py:364
  30.5 31.4 %collective-permute-start.2 = (bf16[16,2,64,128]{3,2,1,0:T(8,128)(2,1)S(1)}, bf16[16,2,64,128]{3,2,1,0:T(8,128)(2,1)S(1)}, u32[]{:S(2)}, u32[]{:S(2)}) collective-permute-start(bf16[16,2,64,128]{3,2,1,0:T(8,128)(2,1)S(1)} %bitcast.10), channel_id=1, source_target_pairs={{0,1},{1,0},{2,3},{3,2},{4,5},{5,4},{6,7},{7,6},{8,9},{9,8},{10,11... | collective-permute-start | bytes 1572872 | tf_op jit(solution)/shard_map/ppermute | solution.py:360
  31.8 30.2 %collective-permute-start.3 = (bf16[16,2,64,128]{3,2,1,0:T(8,128)(2,1)S(1)}, bf16[16,2,64,128]{3,2,1,0:T(8,128)(2,1)S(1)}, u32[]{:S(2)}, u32[]{:S(2)}) collective-permute-start(bf16[16,2,64,128]{3,2,1,0:T(8,128)(2,1)S(1)} %bitcast.11), channel_id=1, source_target_pairs={{0,2},{1,3},{2,0},{3,1},{4,6},{5,7},{6,4},{7,5},{8,10},{9,11},{10,... | collective-permute-start | bytes 1572872 | tf_op jit(solution)/shard_map/ppermute | solution.py:360
  34.4 27.5 %collective-permute-start.4 = (bf16[16,2,64,128]{3,2,1,0:T(8,128)(2,1)S(1)}, bf16[16,2,64,128]{3,2,1,0:T(8,128)(2,1)S(1)}, u32[]{:S(2)}, u32[]{:S(2)}) collective-permute-start(bf16[16,2,64,128]{3,2,1,0:T(8,128)(2,1)S(1)} %bitcast.12), channel_id=1, source_target_pairs={{0,3},{1,2},{2,1},{3,0},{4,7},{5,6},{6,5},{7,4},{8,11},{9,10},{10,... | collective-permute-start | bytes 1572872 | tf_op jit(solution)/shard_map/ppermute | solution.py:360
  78.5 10.2 %collective-permute-start.7 = (bf16[16,64,128]{2,1,0:T(8,128)(2,1)}, bf16[16,64,128]{2,1,0:T(8,128)(2,1)S(1)}, u32[]{:S(2)}, u32[]{:S(2)}) collective-permute-start(bf16[16,64,128]{2,1,0:T(8,128)(2,1)} %get-tuple-element.34), channel_id=1, source_target_pairs={{0,4},{1,5},{2,6},{3,7},{4,0},{5,1},{6,2},{7,3},{8,12},{9,13},{10,... | collective-permute-start | bytes 786440 | tf_op jit(solution)/shard_map/ppermute | solution.py:369
  78.6 20.3 %collective-permute-start.6 = (bf16[16,2,64,128]{3,2,1,0:T(8,128)(2,1)}, bf16[16,2,64,128]{3,2,1,0:T(8,128)(2,1)S(1)}, u32[]{:S(2)}, u32[]{:S(2)}) collective-permute-start(bf16[16,2,64,128]{3,2,1,0:T(8,128)(2,1)} %get-tuple-element.32), channel_id=1, source_target_pairs={{0,3},{1,2},{2,1},{3,0},{4,7},{5,6},{6,5},{7,4},{8,11},{9,10},{10,... | collective-permute-start | bytes 1572872 | tf_op jit(solution)/shard_map/ppermute | solution.py:371
  81.3 17.6 %collective-permute-start.5 = (bf16[16,2,64,128]{3,2,1,0:T(8,128)(2,1)S(1)}, bf16[16,2,64,128]{3,2,1,0:T(8,128)(2,1)S(1)}, u32[]{:S(2)}, u32[]{:S(2)}) collective-permute-start(bf16[16,2,64,128]{3,2,1,0:T(8,128)(2,1)S(1)} %get-tuple-element.31), channel_id=1, source_target_pairs={{0,1},{1,0},{2,3},{3,2},{4,5},{5,4},{6,7},{7,6},{8,9},{9,8},{10,11... | collective-permute-start | bytes 1572872 | tf_op jit(solution)/shard_map/ppermute | solution.py:370
  81.3 19.1 %all-to-all-start.2 = ((bf16[16,48,384]{2,1,0:T(8,128)(2,1)}), bf16[16,48,384]{2,1,0:T(8,128)(2,1)S(1)}, u32[]{:S(2)}, u32[]{:S(2)}) async-start(bf16[16,48,384]{2,1,0:T(8,128)(2,1)} %bitcast.6), calls=%async_computation.2 | async-start | bytes 1179648 | tf_op jit(solution)/shard_map/all_to_all | solution.py:373
  88.8 10.0 %collective-permute-start.8 = (bf16[16,64,128]{2,1,0:T(8,128)(2,1)S(1)}, bf16[16,64,128]{2,1,0:T(8,128)(2,1)S(1)}, u32[]{:S(2)}, u32[]{:S(2)}) collective-permute-start(bf16[16,64,128]{2,1,0:T(8,128)(2,1)S(1)} %add_convert_fusion.1), channel_id=1, source_target_pairs={{0,2},{1,3},{2,0},{3,1},{4,6},{5,7},{6,4},{7,5},{8,10},{9,11},{10,... | collective-permute-start | bytes 786440 | tf_op jit(solution)/shard_map/ppermute | solution.py:374
  100.4 8.5 %copy-start.6 = (bf16[16,48,384]{2,1,0:T(8,128)(2,1)}, bf16[16,48,384]{2,1,0:T(8,128)(2,1)S(1)}, u32[]{:S(2)}) copy-start(bf16[16,48,384]{2,1,0:T(8,128)(2,1)S(1)} %all-to-all-done.2) | copy-start | bytes 1769476
  100.4 19.6 %all-to-all-start.3 = ((bf16[32,64,128]{2,1,0:T(8,128)(2,1)}), bf16[32,64,128]{2,1,0:T(8,128)(2,1)S(1)}, u32[]{:S(2)}, u32[]{:S(2)}) async-start(bf16[32,64,128]{2,1,0:T(8,128)(2,1)} %bitcast.8), calls=%async_computation.3 | async-start | bytes 1048576 | tf_op jit(solution)/shard_map/all_to_all | solution.py:355
  108.9 12.0 %copy-start = (bf16[64,128,128]{2,1,0:T(8,128)(2,1)S(1)}, bf16[64,128,128]{2,1,0:T(8,128)(2,1)}, u32[]{:S(2)}) copy-start(bf16[64,128,128]{2,1,0:T(8,128)(2,1)} %get-tuple-element.41.normed_ref) | copy-start | bytes 6291460
  108.9 11.9 %copy-start.4 = (f32[64,128]{1,0:T(8,128)S(1)}, f32[64,128]{1,0:T(8,128)}, u32[]{:S(2)}) copy-start(f32[64,128]{1,0:T(8,128)} %get-tuple-element.42.scaled_ref) | copy-start | bytes 98308
  108.9 11.9 %copy-start.5 = (bf16[128,16]{0,1:T(8,128)(2,1)S(1)}, bf16[128,16]{0,1:T(8,128)(2,1)}, u32[]{:S(2)}) copy-start(bf16[128,16]{0,1:T(8,128)(2,1)} %param.9) | copy-start | bytes 12292
  120.0 4.5 %collective-permute-start.9 = (bf16[3,64,768]{2,1,0:T(8,128)(2,1)}, bf16[3,64,768]{2,1,0:T(8,128)(2,1)S(1)}, u32[]{:S(2)}, u32[]{:S(2)}) collective-permute-start(bf16[3,64,768]{2,1,0:T(8,128)(2,1)} %get-tuple-element.40), channel_id=1, source_target_pairs={{0,8},{8,0},{16,24},{24,16},{32,40},{40,32},{48,56},{56,48},{64,72... | collective-permute-start | bytes 884744 | tf_op jit(solution)/shard_map/ppermute | solution.py:384
  120.9 3.7 %copy-start.7 = (bf16[6,64,768]{2,1,0:T(8,128)(2,1)S(1)}, bf16[6,64,768]{2,1,0:T(8,128)(2,1)}, u32[]{:S(2)}) copy-start(bf16[6,64,768]{2,1,0:T(8,128)(2,1)} %get-tuple-element.39) | copy-start | bytes 1769476
  124.6 0.8 copy-start.8

commit v11 on v10

--- a/solution.py
+++ b/solution.py
@@ -383,7 +383,7 @@
     mine, theirs, total = lax.optimization_barrier((mine, theirs, total))
     got = lax.ppermute(theirs, "row", cores)
     updated = lax.dynamic_update_slice_in_dim(mine, got, (1 - core) * half, 0)
-    pair_grad = pair_back(stats, total, bias_weight, 32)
+    pair_grad = pair_back(stats, total, bias_weight, 16)
     return (updated, pair_grad)
 
 

time: 126 us -> 126 us (level)
  no operation moved by 1% of the time
where the time goes in v11:
time: 126 us
  Pallas kernels  46.8 us (37%)
  starting transfers between devices  39.9 us (32%)
  waiting for transfers between devices  35.1 us (28%)
  local copies, waits for them, and re-layouts  1.68 us (1%)
  other arithmetic  1.3 us (1%)
    all_to_all x1, waiting for transfers between devices, shards(): packed = lax.all_to_all(packed, 'row', 0, 0, tiled=True)  22.1 us
    all_to_all x2, starting transfers between devices, shards(): lax.all_to_all(v.reshape(2 * n_row, rows, pair.shape[1]), ('row', 'col'),...  16.9 us
    pallas_call x1, Pallas kernels, attend(): pl.pallas_call(functools.partial(attend_kernel, n_col, n_chip, per, size)...  16.6 us
    pallas_call x1, Pallas kernels, transition(): pl.pallas_call(transition_kernel, grid_spec=pltpu.PrefetchScalarGridSpec(...  9.65 us
    ppermute x1, waiting for transfers between devices, shards(): lax.ppermute((two.astype(F32) + far.astype(F32)).astype(BF), 'col', flip(2))  8.62 us
    pallas_call x1, Pallas kernels, project(): pl.pallas_call(project_kernel, grid_spec=pltpu.PrefetchScalarGridSpec(num...  7.65 us
    all_to_all x1, starting transfers between devices, shards(): attended = lax.all_to_all(attended, 'row', 0, 0, tiled=True)  7.43 us
    pallas_call x1, Pallas kernels, pair_stats(): pl.pallas_call(stats_kernel, grid=(rows // step,), in_specs=[pl.BlockSpec...  5.38 us
  transfers between devices with their start and end apart: 14, of which 5 were waited for; matrix products, arithmetic and copies ran while one was open for 1% of the time, Pallas kernels for 24%

profile of v11, /device:TPU:1, one launch (start us, length us, event | category | flops | bytes accessed | tf_op | source)
XLA Modules:
  0.0 125.7 jit_solution(16151622456398433638)
XLA Ops:
  0.6 1.5 %collective-permute-start = (bf16[6,64,768]{2,1,0:T(8,128)(2,1)}, bf16[6,64,768]{2,1,0:T(8,128)(2,1)S(1)}, u32[]{:S(2)}, u32[]{:S(2)}) collective-permute-start(bf16[6,64,768]{2,1,0:T(8,128)(2,1)} %single_ref.1), channel_id=1, source_target_pairs={{0,8},{8,0},{16,24},{24,16},{32,40},{40,32},{48,56},{56,48},{64,72... | collective-permute-start | bytes 1769480 | tf_op jit(solution)/shard_map/ppermute | solution.py:352
  2.2 0.1 collective-permute-start.1
  2.2 3.7 %shard_map.96 = bf16[16,2,64,128]{3,2,1,0:T(8,128)(2,1)} custom-call(bf16[64,128,128]{2,1,0:T(8,128)(2,1)} %pair_ref.2, bf16[16,128]{1,0:T(8,128)(2,1)} %bitcast.15), custom_call_target="tpu_custom_call" | custom-call | tf_op jit(solution)/shard_map/pallas_call | solution.py:50
  5.9 8.4 %all-to-all-start.1 = ((bf16[32,64,128]{2,1,0:T(8,128)(2,1)}), bf16[32,64,128]{2,1,0:T(8,128)(2,1)S(1)}, u32[]{:S(2)}, u32[]{:S(2)}) async-start(bf16[32,64,128]{2,1,0:T(8,128)(2,1)} %bitcast.18), calls=%async_computation.1 | async-start | bytes 1048576 | tf_op jit(solution)/shard_map/all_to_all | solution.py:355
  14.4 0.0 collective-permute-done.got_ref
  14.4 0.0 collective-permute-done.1.gotc_ref
  14.4 7.7 %shard_map.95 = (bf16[16,192,384]{2,1,0:T(8,128)(2,1)}, bf16[3,128,768]{2,1,0:T(8,128)(2,1)S(1)}) custom-call(s32[1]{0:T(128)} %bitcast.core_ref, bf16[6,64,768]{2,1,0:T(8,128)(2,1)S(1)} %copy-done.1, bf16[6,64,768]{2,1,0:T(8,128)(2,1)S(1)} %collective-permute-done.got_ref, bf16[6,64,768]{2,1,0:T(8,128)(2,1)S(1)} %copy-done.2, ...), custom_call_target="tpu_custom_call" | custom-call | tf_op jit(solution)/shard_map/pallas_call | solution.py:145
  22.1 0.8 copy-done.3
  22.9 2.6 %all-to-all-done.1 = bf16[32,64,128]{2,1,0:T(8,128)(2,1)S(1)} async-done(((bf16[32,64,128]{2,1,0:T(8,128)(2,1)}), bf16[32,64,128]{2,1,0:T(8,128)(2,1)S(1)}, u32[]{:S(2)}, u32[]{:S(2)}) %all-to-all-start.1) | async-done | bytes 524320 | tf_op jit(solution)/shard_map/all_to_all | solution.py:355
  25.5 5.0 %all-to-all-start = ((bf16[16,192,384]{2,1,0:T(8,128)(2,1)}), bf16[16,192,384]{2,1,0:T(8,128)(2,1)}, u32[]{:S(2)}, u32[]{:S(2)}) async-start(bf16[16,192,384]{2,1,0:T(8,128)(2,1)} %get-tuple-element.24), calls=%async_computation | async-start | bytes 4718592 | tf_op jit(solution)/shard_map/all_to_all | solution.py:364
  30.5 1.3 %collective-permute-start.2 = (bf16[16,2,64,128]{3,2,1,0:T(8,128)(2,1)S(1)}, bf16[16,2,64,128]{3,2,1,0:T(8,128)(2,1)S(1)}, u32[]{:S(2)}, u32[]{:S(2)}) collective-permute-start(bf16[16,2,64,128]{3,2,1,0:T(8,128)(2,1)S(1)} %bitcast.10), channel_id=1, source_target_pairs={{0,1},{1,0},{2,3},{3,2},{4,5},{5,4},{6,7},{7,6},{8,9},{9,8},{10,11... | collective-permute-start | bytes 1572872 | tf_op jit(solution)/shard_map/ppermute | solution.py:360
  31.8 2.6 %collective-permute-start.3 = (bf16[16,2,64,128]{3,2,1,0:T(8,128)(2,1)S(1)}, bf16[16,2,64,128]{3,2,1,0:T(8,128)(2,1)S(1)}, u32[]{:S(2)}, u32[]{:S(2)}) collective-permute-start(bf16[16,2,64,128]{3,2,1,0:T(8,128)(2,1)S(1)} %bitcast.11), channel_id=1, source_target_pairs={{0,2},{1,3},{2,0},{3,1},{4,6},{5,7},{6,4},{7,5},{8,10},{9,11},{10,... | collective-permute-start | bytes 1572872 | tf_op jit(solution)/shard_map/ppermute | solution.py:360
  34.4 5.4 %shard_map.97 = (bf16[64,128,128]{2,1,0:T(8,128)(2,1)}, f32[64,128]{1,0:T(8,128)}) custom-call(bf16[64,128,128]{2,1,0:T(8,128)(2,1)} %pair_ref.2), custom_call_target="tpu_custom_call" | custom-call | tf_op jit(solution)/shard_map/pallas_call | solution.py:69
  39.8 22.1 %all-to-all-done = bf16[16,192,384]{2,1,0:T(8,128)(2,1)} async-done(((bf16[16,192,384]{2,1,0:T(8,128)(2,1)}), bf16[16,192,384]{2,1,0:T(8,128)(2,1)}, u32[]{:S(2)}, u32[]{:S(2)}) %all-to-all-start) | async-done | bytes 2359328 | tf_op jit(solution)/shard_map/all_to_all | solution.py:364
  61.9 0.0 collective-permute-done.4.refs_3_
  61.9 16.6 %shard_map.98 = (bf16[8,2,48,384]{3,2,1,0:T(8,128)(2,1)}, bf16[16,2,64,128]{3,2,1,0:T(8,128)(2,1)S(1)}, bf16[16,2,64,128]{3,2,1,0:T(8,128)(2,1)S(1)}, bf16[16,2,...) custom-call(s32[1]{0:T(128)} %bitcast.1.c_ref, ...), custom_call_target="tpu_custom_call" | custom-call | tf_op jit(solution)/shard_map/pallas_call | solution.py:318
  78.5 0.1 collective-permute-start.7
  78.6 2.7 %collective-permute-start.6 = (bf16[16,2,64,128]{3,2,1,0:T(8,128)(2,1)}, bf16[16,2,64,128]{3,2,1,0:T(8,128)(2,1)S(1)}, u32[]{:S(2)}, u32[]{:S(2)}) collective-permute-start(bf16[16,2,64,128]{3,2,1,0:T(8,128)(2,1)} %get-tuple-element.32), channel_id=1, source_target_pairs={{0,3},{1,2},{2,1},{3,0},{4,7},{5,6},{6,5},{7,4},{8,11},{9,10},{10,... | collective-permute-start | bytes 1572872 | tf_op jit(solution)/shard_map/ppermute | solution.py:371
  81.3 7.4 %all-to-all-start.2 = ((bf16[16,48,384]{2,1,0:T(8,128)(2,1)}), bf16[16,48,384]{2,1,0:T(8,128)(2,1)S(1)}, u32[]{:S(2)}, u32[]{:S(2)}) async-start(bf16[16,48,384]{2,1,0:T(8,128)(2,1)} %bitcast.6), calls=%async_computation.2 | async-start | bytes 1179648 | tf_op jit(solution)/shard_map/all_to_all | solution.py:373
  88.7 0.1 add_convert_fusion.1
  88.8 1.4 %collective-permute-start.8 = (bf16[16,64,128]{2,1,0:T(8,128)(2,1)S(1)}, bf16[16,64,128]{2,1,0:T(8,128)(2,1)S(1)}, u32[]{:S(2)}, u32[]{:S(2)}) collective-permute-start(bf16[16,64,128]{2,1,0:T(8,128)(2,1)S(1)} %add_convert_fusion.1), channel_id=1, source_target_pairs={{0,2},{1,3},{2,0},{3,1},{4,6},{5,7},{6,4},{7,5},{8,10},{9,11},{10,... | collective-permute-start | bytes 786440 | tf_op jit(solution)/shard_map/ppermute | solution.py:374
  90.2 8.6 %collective-permute-done.8 = bf16[16,64,128]{2,1,0:T(8,128)(2,1)S(1)} collective-permute-done((bf16[16,64,128]{2,1,0:T(8,128)(2,1)S(1)}, bf16[16,64,128]{2,1,0:T(8,128)(2,1)S(1)}, u32[]{:S(2)}, u32[]{:S(2)}) %collective-permute-start.8) | collective-permute-done | bytes 262176 | tf_op jit(solution)/shard_map/ppermute | solution.py:374
  98.9 1.2 add_convert_fusion
  100.1 0.3 all-to-all-done.2
  100.4 8.5 %all-to-all-start.3 = ((bf16[32,64,128]{2,1,0:T(8,128)(2,1)}), bf16[32,64,128]{2,1,0:T(8,128)(2,1)S(1)}, u32[]{:S(2)}, u32[]{:S(2)}) async-start(bf16[32,64,128]{2,1,0:T(8,128)(2,1)} %bitcast.8), calls=%async_computation.3 | async-start | bytes 1048576 | tf_op jit(solution)/shard_map/all_to_all | solution.py:355
  108.9 0.0 copy-start.5
  109.0 9.6 %shard_map.99 = (bf16[6,64,768]{2,1,0:T(8,128)(2,1)}, bf16[3,64,768]{2,1,0:T(8,128)(2,1)}) custom-call(s32[1]{0:T(128)} %bitcast.core_ref, bf16[3,128,768]{2,1,0:T(8,128)(2,1)} %copy-done.3, bf16[768,384]{1,0:T(8,128)(2,1)} %bitcast.17, bf16[768,768]{1,0:T(8,128)(2,1)} %wo_ref.1, bf16[768,3072]{1,0:T(8,128)(2,1)} %wu_ref.1, bf16[768,3072]{1,0:T(8,128)(2,1)} %wu_ref.1, ...), custom_call_target="tpu_custom_call" | custom-call | tf_op jit(solution)/shard_map/pallas_call | solution.py:193
  118.6 1.4 %all-to-all-done.3 = bf16[32,64,128]{2,1,0:T(8,128)(2,1)S(1)} async-done(((bf16[32,64,128]{2,1,0:T(8,128)(2,1)}), bf16[32,64,128]{2,1,0:T(8,128)(2,1)S(1)}, u32[]{:S(2)}, u32[]{:S(2)}) %all-to-all-start.3) | async-done | bytes 524320 | tf_op jit(solution)/shard_map/all_to_all | solution.py:355
  120.0 0.9 collective-permute-start.9
  120.9 3.9 %shard_map.100 = f32[64,128,128]{2,1,0:T(8,128)} custom-call(bf16[64,128,128]{2,1,0:T(8,128)(2,1)S(1)} %copy-done, f32[64,128]{1,0:T(8,128)S(1)} %copy-done.4, bf16[16,2,64,128]{3,2,1,0:T(8,128)(2,1)S(1)} %bitcast.14, bf16[16,128]{1,0:T(8,128)(2,1)S(1)} %bitcast.16), custom_call_target="tpu_custom_call" | custom-call | tf_op jit(solution)/shard_map/pallas_call | solution.py:98
  124.8 0.0 copy-start.8
  124.9 0.8 copy-done.8
  (25 shorter events, 0.1 us)
Async XLA Ops:
  0.6 13.8 %copy-start.1 = (bf16[6,64,768]{2,1,0:T(8,128)(2,1)S(1)}, bf16[6,64,768]{2,1,0:T(8,128)(2,1)}, u32[]{:S(2)}) copy-start(bf16[6,64,768]{2,1,0:T(8,128)(2,1)} %single_ref.1) | copy-start | bytes 1769476
  0.6 13.8 %copy-start.2 = (bf16[6,64,768]{2,1,0:T(8,128)(2,1)S(1)}, bf16[6,64,768]{2,1,0:T(8,128)(2,1)}, u32[]{:S(2)}) copy-start(bf16[6,64,768]{2,1,0:T(8,128)(2,1)} %cot_ref.1) | copy-start | bytes 1769476
  0.6 13.7 %collective-permute-start = (bf16[6,64,768]{2,1,0:T(8,128)(2,1)}, bf16[6,64,768]{2,1,0:T(8,128)(2,1)S(1)}, u32[]{:S(2)}, u32[]{:S(2)}) collective-permute-start(bf16[6,64,768]{2,1,0:T(8,128)(2,1)} %single_ref.1), channel_id=1, source_target_pairs={{0,8},{8,0},{16,24},{24,16},{32,40},{40,32},{48,56},{56,48},{64,72... | collective-permute-start | bytes 1769480 | tf_op jit(solution)/shard_map/ppermute | solution.py:352
  2.2 12.2 %collective-permute-start.1 = (bf16[6,64,768]{2,1,0:T(8,128)(2,1)}, bf16[6,64,768]{2,1,0:T(8,128)(2,1)S(1)}, u32[]{:S(2)}, u32[]{:S(2)}) collective-permute-start(bf16[6,64,768]{2,1,0:T(8,128)(2,1)} %cot_ref.1), channel_id=1, source_target_pairs={{0,8},{8,0},{16,24},{24,16},{32,40},{40,32},{48,56},{56,48},{64,72... | collective-permute-start | bytes 1769480 | tf_op jit(solution)/shard_map/ppermute | solution.py:353
  5.9 19.5 %all-to-all-start.1 = ((bf16[32,64,128]{2,1,0:T(8,128)(2,1)}), bf16[32,64,128]{2,1,0:T(8,128)(2,1)S(1)}, u32[]{:S(2)}, u32[]{:S(2)}) async-start(bf16[32,64,128]{2,1,0:T(8,128)(2,1)} %bitcast.18), calls=%async_computation.1 | async-start | bytes 1048576 | tf_op jit(solution)/shard_map/all_to_all | solution.py:355
  22.1 0.8 copy-start.3
  25.5 36.5 %all-to-all-start = ((bf16[16,192,384]{2,1,0:T(8,128)(2,1)}), bf16[16,192,384]{2,1,0:T(8,128)(2,1)}, u32[]{:S(2)}, u32[]{:S(2)}) async-start(bf16[16,192,384]{2,1,0:T(8,128)(2,1)} %get-tuple-element.24), calls=%async_computation | async-start | bytes 4718592 | tf_op jit(solution)/shard_map/all_to_all | solution.py:364
  30.5 31.4 %collective-permute-start.2 = (bf16[16,2,64,128]{3,2,1,0:T(8,128)(2,1)S(1)}, bf16[16,2,64,128]{3,2,1,0:T(8,128)(2,1)S(1)}, u32[]{:S(2)}, u32[]{:S(2)}) collective-permute-start(bf16[16,2,64,128]{3,2,1,0:T(8,128)(2,1)S(1)} %bitcast.10), channel_id=1, source_target_pairs={{0,1},{1,0},{2,3},{3,2},{4,5},{5,4},{6,7},{7,6},{8,9},{9,8},{10,11... | collective-permute-start | bytes 1572872 | tf_op jit(solution)/shard_map/ppermute | solution.py:360
  31.8 30.2 %collective-permute-start.3 = (bf16[16,2,64,128]{3,2,1,0:T(8,128)(2,1)S(1)}, bf16[16,2,64,128]{3,2,1,0:T(8,128)(2,1)S(1)}, u32[]{:S(2)}, u32[]{:S(2)}) collective-permute-start(bf16[16,2,64,128]{3,2,1,0:T(8,128)(2,1)S(1)} %bitcast.11), channel_id=1, source_target_pairs={{0,2},{1,3},{2,0},{3,1},{4,6},{5,7},{6,4},{7,5},{8,10},{9,11},{10,... | collective-permute-start | bytes 1572872 | tf_op jit(solution)/shard_map/ppermute | solution.py:360
  34.4 27.5 %collective-permute-start.4 = (bf16[16,2,64,128]{3,2,1,0:T(8,128)(2,1)S(1)}, bf16[16,2,64,128]{3,2,1,0:T(8,128)(2,1)S(1)}, u32[]{:S(2)}, u32[]{:S(2)}) collective-permute-start(bf16[16,2,64,128]{3,2,1,0:T(8,128)(2,1)S(1)} %bitcast.12), channel_id=1, source_target_pairs={{0,3},{1,2},{2,1},{3,0},{4,7},{5,6},{6,5},{7,4},{8,11},{9,10},{10,... | collective-permute-start | bytes 1572872 | tf_op jit(solution)/shard_map/ppermute | solution.py:360
  78.5 10.2 %collective-permute-start.7 = (bf16[16,64,128]{2,1,0:T(8,128)(2,1)}, bf16[16,64,128]{2,1,0:T(8,128)(2,1)S(1)}, u32[]{:S(2)}, u32[]{:S(2)}) collective-permute-start(bf16[16,64,128]{2,1,0:T(8,128)(2,1)} %get-tuple-element.34), channel_id=1, source_target_pairs={{0,4},{1,5},{2,6},{3,7},{4,0},{5,1},{6,2},{7,3},{8,12},{9,13},{10,... | collective-permute-start | bytes 786440 | tf_op jit(solution)/shard_map/ppermute | solution.py:369
  78.6 20.3 %collective-permute-start.6 = (bf16[16,2,64,128]{3,2,1,0:T(8,128)(2,1)}, bf16[16,2,64,128]{3,2,1,0:T(8,128)(2,1)S(1)}, u32[]{:S(2)}, u32[]{:S(2)}) collective-permute-start(bf16[16,2,64,128]{3,2,1,0:T(8,128)(2,1)} %get-tuple-element.32), channel_id=1, source_target_pairs={{0,3},{1,2},{2,1},{3,0},{4,7},{5,6},{6,5},{7,4},{8,11},{9,10},{10,... | collective-permute-start | bytes 1572872 | tf_op jit(solution)/shard_map/ppermute | solution.py:371
  81.3 17.6 %collective-permute-start.5 = (bf16[16,2,64,128]{3,2,1,0:T(8,128)(2,1)S(1)}, bf16[16,2,64,128]{3,2,1,0:T(8,128)(2,1)S(1)}, u32[]{:S(2)}, u32[]{:S(2)}) collective-permute-start(bf16[16,2,64,128]{3,2,1,0:T(8,128)(2,1)S(1)} %get-tuple-element.31), channel_id=1, source_target_pairs={{0,1},{1,0},{2,3},{3,2},{4,5},{5,4},{6,7},{7,6},{8,9},{9,8},{10,11... | collective-permute-start | bytes 1572872 | tf_op jit(solution)/shard_map/ppermute | solution.py:370
  81.3 19.1 %all-to-all-start.2 = ((bf16[16,48,384]{2,1,0:T(8,128)(2,1)}), bf16[16,48,384]{2,1,0:T(8,128)(2,1)S(1)}, u32[]{:S(2)}, u32[]{:S(2)}) async-start(bf16[16,48,384]{2,1,0:T(8,128)(2,1)} %bitcast.6), calls=%async_computation.2 | async-start | bytes 1179648 | tf_op jit(solution)/shard_map/all_to_all | solution.py:373
  88.8 10.0 %collective-permute-start.8 = (bf16[16,64,128]{2,1,0:T(8,128)(2,1)S(1)}, bf16[16,64,128]{2,1,0:T(8,128)(2,1)S(1)}, u32[]{:S(2)}, u32[]{:S(2)}) collective-permute-start(bf16[16,64,128]{2,1,0:T(8,128)(2,1)S(1)} %add_convert_fusion.1), channel_id=1, source_target_pairs={{0,2},{1,3},{2,0},{3,1},{4,6},{5,7},{6,4},{7,5},{8,10},{9,11},{10,... | collective-permute-start | bytes 786440 | tf_op jit(solution)/shard_map/ppermute | solution.py:374
  100.4 8.5 %copy-start.6 = (bf16[16,48,384]{2,1,0:T(8,128)(2,1)}, bf16[16,48,384]{2,1,0:T(8,128)(2,1)S(1)}, u32[]{:S(2)}) copy-start(bf16[16,48,384]{2,1,0:T(8,128)(2,1)S(1)} %all-to-all-done.2) | copy-start | bytes 1769476
  100.4 19.6 %all-to-all-start.3 = ((bf16[32,64,128]{2,1,0:T(8,128)(2,1)}), bf16[32,64,128]{2,1,0:T(8,128)(2,1)S(1)}, u32[]{:S(2)}, u32[]{:S(2)}) async-start(bf16[32,64,128]{2,1,0:T(8,128)(2,1)} %bitcast.8), calls=%async_computation.3 | async-start | bytes 1048576 | tf_op jit(solution)/shard_map/all_to_all | solution.py:355
  108.9 12.0 %copy-start = (bf16[64,128,128]{2,1,0:T(8,128)(2,1)S(1)}, bf16[64,128,128]{2,1,0:T(8,128)(2,1)}, u32[]{:S(2)}) copy-start(bf16[64,128,128]{2,1,0:T(8,128)(2,1)} %get-tuple-element.41.normed_ref) | copy-start | bytes 6291460
  108.9 11.9 %copy-start.4 = (f32[64,128]{1,0:T(8,128)S(1)}, f32[64,128]{1,0:T(8,128)}, u32[]{:S(2)}) copy-start(f32[64,128]{1,0:T(8,128)} %get-tuple-element.42.scaled_ref) | copy-start | bytes 98308
  108.9 11.9 %copy-start.5 = (bf16[128,16]{0,1:T(8,128)(2,1)S(1)}, bf16[128,16]{0,1:T(8,128)(2,1)}, u32[]{:S(2)}) copy-start(bf16[128,16]{0,1:T(8,128)(2,1)} %param.9) | copy-start | bytes 12292
  120.0 4.8 %collective-permute-start.9 = (bf16[3,64,768]{2,1,0:T(8,128)(2,1)}, bf16[3,64,768]{2,1,0:T(8,128)(2,1)S(1)}, u32[]{:S(2)}, u32[]{:S(2)}) collective-permute-start(bf16[3,64,768]{2,1,0:T(8,128)(2,1)} %get-tuple-element.40), channel_id=1, source_target_pairs={{0,8},{8,0},{16,24},{24,16},{32,40},{40,32},{48,56},{56,48},{64,72... | collective-permute-start | bytes 884744 | tf_op jit(solution)/shard_map/ppermute | solution.py:384
  120.9 3.9 %copy-start.7 = (bf16[6,64,768]{2,1,0:T(8,128)(2,1)S(1)}, bf16[6,64,768]{2,1,0:T(8,128)(2,1)}, u32[]{:S(2)}) copy-start(bf16[6,64,768]{2,1,0:T(8,128)(2,1)} %get-tuple-element.39) | copy-start | bytes 1769476
  124.8 0.8 copy-start.8
